TPU v7x, 32 devices: a whole 2x2x4 slice. The times are simulated.
32 devices in a mesh: groups: 2 (over x), tensor: 8 (over z, y), dp: 2 (over core).
Axes of the slice: x: 2, y: 2, z: 4, core: 2. Of those that a mesh axis runs over, the one named last changes fastest.
Arguments:
- inputs: bfloat16 [4, 256, 16384], P(('groups', 'dp'), None, 'tensor'), parts along dimension 0, may hold values from -6 to 6
- cross_w: bfloat16 [16384, 16384], P('dp', 'tensor'), may hold values from -0.046875 to 0.046875
- cross_b: float32 [16384], P('tensor'), may hold values from -3 to 3
- mix_weight: bfloat16 [128, 512], replicated, may hold values from -0.5 to 0.5
- mix_bias: float32 [512], replicated, may hold values from -3 to 3
- out_weight: bfloat16 [512, 128], replicated, may hold values from -0.25 to 0.25
- cotangent: bfloat16 [4, 256, 16384], P(('groups', 'dp'), 'tensor'), parts along dimension 0, may hold values from -12 to 12
Outputs:
- compressed: bfloat16 [4, 256, 16384], P(('groups', 'dp'), 'tensor'), parts along dimension 0
- grad_inputs: bfloat16 [4, 256, 16384], P(('groups', 'dp'), None, 'tensor'), parts along dimension 0
- grad_mix: float32 [256, 512], P('groups'), parts along dimension 0
- grad_mix_bias: float32 [1024], P('groups'), parts along dimension 0
- grad_out: float32 [1024, 128], P('groups'), parts along dimension 0
There are 2 independent parts, one for each index of `groups`. A program takes and returns all parts, laid end to end along the dimension named above; an argument that names none is the same for every part. Nothing has to cross between parts.
All inputs are finite; a program needn't handle non-finite values.
Results may differ from a plain program's by a relative error of at most 0.019.
Values may be sent and summed in bfloat16 or wider, within the bound.
No kernel may reach another device: no remote copies, remote signals or barrier semaphores. Data moves between devices by JAX's collectives and lax.ppermute only.
A program may use at most 256 MiB of HBM per device.

v0:
```python
import functools

import jax
import jax.numpy as jnp
from jax import lax
from jax.experimental import pallas as pl
from jax.experimental.pallas import tpu as pltpu
from jax.sharding import PartitionSpec as P

F = 128
E = 128
K = 128

PAIR = [(2 * a + y, 2 * b + y) for a, b in ((0, 1), (1, 0), (2, 3), (3, 2)) for y in range(2)]
MID = [(2 * a + y, 2 * b + y) for a, b in ((1, 2), (2, 1)) for y in range(2)]
OUT = [(2 * a + y, 2 * b + y) for a, b in ((1, 0), (2, 3)) for y in range(2)]
INN = [(b, a) for a, b in OUT]
ACROSS = [(2 * z + y, 2 * z + 1 - y) for z in range(4) for y in range(2)]
CROSS = [(2 * z + y, 2 * (z ^ 2) + y) for z in range(4) for y in range(2)]
F32 = jnp.float32
BF16 = jnp.bfloat16


def forward_kernel(count, plan_ref, *refs):
    sources, (w_ref, own_ref, other_ref, x_ref, acc_ref, sems) = refs[: 4 * count], refs[4 * count :]
    at = pl.program_id(0)
    per = pl.num_programs(0) // count
    rows, width = x_ref.shape[1] // 2, x_ref.shape[2]
    depth = width // per
    near = plan_ref[count] == 1
    piece, part = at // per, at % per

    @pl.when(at == 0)
    def _():
        for q in range(count):
            close, distant, close_other, distant_other = sources[4 * q : 4 * q + 4]
            for half, a, b in ((0, close, distant), (1, close_other, distant_other)):
                place = x_ref.at[q, pl.ds(half * rows, rows)]
                pl.when(near)(pltpu.make_async_copy(a, place, sems.at[q, half]).start)
                pl.when(jnp.logical_not(near))(pltpu.make_async_copy(b, place, sems.at[q, half]).start)

    for q in range(count):

        @pl.when((part == 0) & (piece == q))
        def _(q=q):
            for half in range(2):
                place = x_ref.at[q, pl.ds(half * rows, rows)]
                pltpu.make_async_copy(sources[4 * q + 2 * half], place, sems.at[q, half]).wait()

    columns = pl.ds(pl.multiple_of(part * depth, depth), depth)
    term = jnp.dot(x_ref[piece, :, columns], w_ref[...], preferred_element_type=F32)

    @pl.when(at == 0)
    def _():
        acc_ref[...] = term

    @pl.when(at > 0)
    def _():
        acc_ref[...] += term

    @pl.when(at == pl.num_programs(0) - 1)
    def _():
        own_ref[...] = acc_ref[:rows]
        other_ref[...] = acc_ref[rows:].astype(BF16)


def forward_rows(pieces, order, near, cross_w, per=2):
    count = len(pieces)
    rows, width = pieces[0][0].shape
    columns = cross_w.shape[1]
    plan = jnp.stack([*order, near.astype(jnp.int32)])
    half = pl.BlockSpec((rows, columns), lambda s, plan: (0, 0), pipeline_mode=pl.Buffered(1))
    return pl.pallas_call(
        functools.partial(forward_kernel, count),
        grid_spec=pltpu.PrefetchScalarGridSpec(
            num_scalar_prefetch=1,
            grid=(count * per,),
            in_specs=[pl.BlockSpec(memory_space=pl.ANY)] * (4 * count)
            + [pl.BlockSpec((width // per, columns), lambda s, plan: (plan[s // per] * per + s % per, 0))],
            out_specs=[half, half],
            scratch_shapes=[
                pltpu.VMEM((count, 2 * rows, width), BF16),
                pltpu.VMEM((2 * rows, columns), F32),
                pltpu.SemaphoreType.DMA((count, 2)),
            ],
        ),
        out_shape=[jax.ShapeDtypeStruct((rows, columns), F32), jax.ShapeDtypeStruct((rows, columns), BF16)],
        cost_estimate=pl.CostEstimate(
            flops=4 * rows * width * count * columns,
            transcendentals=0,
            bytes_accessed=2 * width * count * columns,
        ),
        name="forward_rows",
    )(plan, *[ref for piece in pieces for ref in piece], cross_w)


def back_kernel(count, plan_ref, own_ref, other_ref, w_ref, *refs):
    outs, x_ref = refs[:-1], refs[-1]
    rows = own_ref.shape[0]
    p = pl.program_id(0)

    @pl.when(p + pl.program_id(1) == 0)
    def _():
        x_ref[:rows] = own_ref[...]
        x_ref[rows:] = other_ref[...]

    contract = (((1,), (1,)), ((), ()))
    term = lax.dot_general(x_ref[...], w_ref[...], contract, preferred_element_type=F32).astype(BF16)
    for q in range(count):

        @pl.when(p == q)
        def _(q=q):
            outs[2 * q][...] = term[:rows]
            outs[2 * q + 1][...] = term[rows:]


def back_part(own, other, order, cross_w, per=2):
    count = len(order)
    rows, width = own.shape
    plan = jnp.stack(list(order))
    tile = width // per
    whole = pl.BlockSpec((rows, width), lambda p, i, plan: (0, 0), pipeline_mode=pl.Buffered(1))

    def out(q):
        return pl.BlockSpec((rows, tile), lambda p, i, plan: (0, jnp.where(p == q, i, jnp.where(p < q, 0, per - 1))))

    return pl.pallas_call(
        functools.partial(back_kernel, count),
        grid_spec=pltpu.PrefetchScalarGridSpec(
            num_scalar_prefetch=1,
            grid=(count, per),
            in_specs=[whole, whole, pl.BlockSpec((tile, width), lambda p, i, plan: (plan[p] * per + i, 0))],
            out_specs=[out(q) for q in range(count) for _ in range(2)],
            scratch_shapes=[pltpu.VMEM((2 * rows, width), BF16)],
        ),
        out_shape=[jax.ShapeDtypeStruct((rows, width), BF16)] * (2 * count),
        cost_estimate=pl.CostEstimate(
            flops=4 * rows * width * count * width,
            transcendentals=0,
            bytes_accessed=2 * width * count * width,
        ),
        name="back_part",
    )(plan, own, other, cross_w)


def interact_kernel(x_ref, up_ref, mix_ref, bias_ref, out_ref, comp_ref, dx_ref, mix_term, bias_term, out_term):
    group = x_ref.shape[1]
    size = x_ref.shape[0] * x_ref.shape[2]

    @pl.when(pl.program_id(0) == 0)
    def _():
        mix_term[...] = jnp.zeros_like(mix_term)
        bias_term[...] = jnp.zeros_like(bias_term)
        out_term[...] = jnp.zeros_like(out_term)

    across = (((1,), (1,)), ((), ()))
    down = (((0,), (0,)), ((), ()))
    grams = []
    xs = [x_ref[:, b].reshape(size, x_ref.shape[3]) for b in range(group)]
    for x in xs:
        gram = lax.dot_general(x, x, across, preferred_element_type=F32) * (1.0 / x.shape[1])
        grams.append(gram.astype(BF16))
    gram = jnp.concatenate(grams, axis=0)
    up = up_ref[...].reshape(group * size, up_ref.shape[2])
    pre = jnp.dot(gram, mix_ref[...], preferred_element_type=F32) + bias_ref[...]
    d_hidden = lax.dot_general(up, out_ref[...], across, preferred_element_type=F32)
    sig = jax.nn.sigmoid(pre)
    hidden = (pre * sig).astype(BF16)
    d_pre = (d_hidden * sig * (1.0 + pre * (1.0 - sig))).astype(BF16)
    comp = jnp.dot(hidden, out_ref[...], preferred_element_type=F32).astype(BF16)
    comp_ref[...] = comp.reshape(comp_ref.shape)
    out_term[...] += lax.dot_general(hidden, up, down, preferred_element_type=F32)
    mix_term[...] += lax.dot_general(gram, d_pre, down, preferred_element_type=F32)
    wide = d_pre.astype(F32)
    bias_term[...] += jnp.sum(wide.reshape(-1, 8, wide.shape[1]), axis=0)
    d_gram = lax.dot_general(d_pre, mix_ref[...], across, preferred_element_type=F32)
    for b in range(group):
        part = d_gram[b * size : (b + 1) * size]
        both = (part + part.T).astype(BF16)
        dx = jnp.dot(both, xs[b], preferred_element_type=F32) * (1.0 / x_ref.shape[3])
        dx_ref[:, b] = dx.astype(BF16).reshape(x_ref.shape[0], x_ref.shape[2], x_ref.shape[3])


def interact_rows(owned, upstream, mix_weight, mix_bias, out_weight, group=8):
    sources, count, parts, e = owned.shape
    f = sources * parts
    hidden, k = out_weight.shape
    rows = pl.BlockSpec((sources, group, parts, e), lambda i: (0, i, 0, 0))
    rows_k = pl.BlockSpec((group, f, k), lambda i: (i, 0, 0))

    def fixed(*shape):
        return pl.BlockSpec(shape, lambda i: (0,) * len(shape))

    return pl.pallas_call(
        interact_kernel,
        grid=(count // group,),
        in_specs=[rows, rows_k, fixed(f, hidden), fixed(1, hidden), fixed(hidden, k)],
        out_specs=[rows_k, rows, fixed(f, hidden), fixed(8, hidden), fixed(hidden, k)],
        out_shape=[
            jax.ShapeDtypeStruct((count, f, k), BF16),
            jax.ShapeDtypeStruct(owned.shape, BF16),
            jax.ShapeDtypeStruct((f, hidden), F32),
            jax.ShapeDtypeStruct((8, hidden), F32),
            jax.ShapeDtypeStruct((hidden, k), F32),
        ],
        cost_estimate=pl.CostEstimate(
            flops=2 * count * f * (2 * f * e + 6 * f * hidden),
            transcendentals=2 * count * f * hidden,
            bytes_accessed=8 * count * f * e,
        ),
        name="interact_rows",
    )(owned, upstream, mix_weight, mix_bias.reshape(1, -1), out_weight)


def step(value, pairs):
    return lax.ppermute(value, "tensor", pairs)


def swap(value):
    return lax.ppermute(value, "dp", [(0, 1), (1, 0)])


def place():
    index = lax.axis_index("tensor")
    z, y = index // 2, index % 2
    outer = (z == 0) | (z == 3)
    near = lax.axis_index("dp") == z // 2
    here, beside = z % 2, 1 - z % 2
    far_first = jnp.where(z < 2, 0, 1)
    first = jnp.where(near, here, far_first)
    second = jnp.where(near, beside, 1 - far_first)
    order = (2 * first + y, 2 * first + 1 - y, 2 * second + y, 2 * second + 1 - y)
    return outer, near, order


def after(value, *others):
    return lax.optimization_barrier((value, *others))[0]


def hold(values, *others):
    return lax.optimization_barrier((*values, *others))[: len(values)]


def add(a, b):
    return (a.astype(F32) + b.astype(F32)).astype(BF16)


def roles(pieces, q, near):
    own, other = pieces[q]
    other = swap(other)
    return jnp.where(near, own, other), jnp.where(near, other, own)


def interact(owned, cotangent, mix_weight, mix_bias, out_weight):
    count = owned.shape[1]
    comp, d_rows, mix_term, bias_term, out_term = interact_rows(
        owned, cotangent.reshape(count, F, K), mix_weight, mix_bias, out_weight
    )
    return comp.reshape(count, F * K), d_rows, mix_term, jnp.sum(bias_term, axis=0), out_term


def exchange_rows(value, owners):
    if value.ndim == 2:
        value = value.reshape(owners, value.shape[0] // owners, value.shape[1] // E, E)
        return lax.all_to_all(value, "tensor", split_axis=0, concat_axis=0, tiled=True)
    value = lax.all_to_all(value, "tensor", split_axis=0, concat_axis=0, tiled=True)
    return value.reshape(value.shape[0] * value.shape[1], value.shape[2] * value.shape[3])


def grid_sum_start(terms):
    mix_term, bias_term, out_term = (x + y for x, y in zip(*terms))
    mixed = jnp.concatenate([mix_term, jnp.broadcast_to(bias_term[None], (8, bias_term.shape[0]))], axis=0)
    wide = out_term.reshape(-1, mixed.shape[1])
    wide = jnp.concatenate([wide, jnp.zeros((mixed.shape[0] - wide.shape[0], wide.shape[1]), F32)], axis=0)
    first = lax.axis_index("dp") == 0
    return jnp.where(first, mixed, wide) + swap(jnp.where(first, wide, mixed).astype(BF16)).astype(F32)


def grid_sum_step(kept, pairs):
    sent = kept.astype(BF16)
    return sent.astype(F32) + step(sent, pairs).astype(F32)


def grid_sum_end(kept, out_shape):
    kept = kept.astype(BF16)
    other = swap(kept)
    first = lax.axis_index("dp") == 0
    mixed, wide = jnp.where(first, kept, other), jnp.where(first, other, kept)
    rows = out_shape[0] * out_shape[1] // kept.shape[1]
    return mixed[:-8].astype(F32), mixed[-8].astype(F32), wide[:rows].astype(F32).reshape(out_shape)


def grid_path(own, cross_w, cross_b, cotangent, small):
    outer, near, order = place()

    def four(close, distant):
        return close, distant, swap(close), swap(distant)

    def linear(pieces, *beside):
        total, other = hold(forward_rows(pieces, order, near, cross_w), *beside)
        return total + swap(other).astype(F32) + cross_b

    def back(d_linear, other, pair, *beside):
        outs = hold(back_part(d_linear, other, [order[q] for q in pair], cross_w), *beside)
        return {pair[0]: outs[:2], pair[1]: outs[2:]}

    def to_owner(c, line):
        base = own[c].astype(F32)
        return exchange_rows((base * line + base).astype(BF16), 8)

    def exchange(pieces, q):
        close, distant = roles(pieces, q, near)
        return distant, close

    def product(c, d_crossed):
        d_linear = (d_crossed.astype(F32) * own[c].astype(F32)).astype(BF16)
        return d_linear, swap(d_linear)

    def finish(c, d_crossed, line, back):
        return (d_crossed.astype(F32) * (line + 1.0) + back).astype(BF16)

    a, b = own
    y0, e1, m1 = step(a, ACROSS), step(a, PAIR), step(a, MID)
    y1, m2 = step(after(e1, y0, m1), ACROSS), step(after(e1, y0, m1), MID)
    e2 = step(after(m1, y0, e1), OUT)
    b2 = jnp.where(outer, e2, m1)
    y2, e3 = step(after(b2, y1, m2), ACROSS), step(after(m2, y1, e2), OUT)
    b3 = jnp.where(outer, e3, m2)
    y3 = step(after(b3, y2), ACROSS)
    first = after(b, y2, e3)
    f1, n1 = step(first, PAIR), step(first, MID)
    pieces = [four(a, b2), four(y0, y2), four(e1, b3), four(y1, y3)]
    x0 = step(after(b, y3, f1), ACROSS)
    x1, n2, f2 = step(after(f1, y3, n1), ACROSS), step(after(f1, y3, n1), MID), step(after(n1, y3, f1), OUT)
    line_a = linear(pieces, x0, x1, n2, f2)
    b2 = jnp.where(outer, f2, n1)
    x2, f3 = step(after(b2, x0, x1, n2), ACROSS), step(after(n2, x1, f2), OUT)
    owned_a = to_owner(0, after(line_a, b2))
    b3 = jnp.where(outer, f3, n2)
    x3 = step(after(b3, x2), ACROSS)
    out_a, d_rows_a, *terms_a = interact(after(owned_a, x2, f3), cotangent[0], *small)
    back_a = exchange_rows(d_rows_a, 8)
    pieces = [four(after(b, d_rows_a), b2), four(x0, x2), four(f1, b3), four(x1, x3)]
    line_b = linear(pieces, back_a)
    owned_b = to_owner(1, line_b)
    d_linear, other = product(0, back_a)
    part = back(after(d_linear, line_b), other, (3, 2), owned_b)
    distant3, close3 = exchange(part, 3)
    g3, h3 = step(distant3, ACROSS), step(close3, ACROSS)
    out_b, d_rows_b, *terms_b = interact(after(owned_b, distant3, close3), cotangent[1], *small)
    back_b = exchange_rows(d_rows_b, 8)
    second = back(after(d_linear, d_rows_b), other, (1, 0), g3, h3)
    h3_a = h3
    distant2, close2 = exchange(part, 2)
    distant1, close1 = exchange(second, 1)
    b3 = add(distant2, after(g3, distant1))
    k3 = step(b3, INN)
    g1, h1 = step(after(distant1, h3), ACROSS), step(after(close1, h3), ACROSS)
    kept = grid_sum_step(grid_sum_start((terms_a, terms_b)), ACROSS)
    d_next, other = product(1, back_b)
    part = back(after(d_next, second[1][0]), other, (3, 2), g1, k3, kept)
    kept, k3, g1_a = hold((kept, k3, g1), part[3][0])
    close_a, distant0 = roles(second, 0, near)
    distant3, close3 = exchange(part, 3)
    g3, h3 = step(distant3, ACROSS), step(close3, ACROSS)
    h1_a = h1
    b3, b2, e1 = add(b3, k3), add(distant0, g1_a), add(close2, h3_a)
    k2, r2 = step(b3, MID), step(b2, INN)
    kept = grid_sum_step(kept, PAIR)
    second = back(after(d_next, part[3][0], distant3), other, (1, 0), h1, k2, r2, kept)
    kept, k2, r2 = hold((kept, k2, r2), second[1][0])
    distant1, close1 = exchange(second, 1)
    g1, h1 = step(after(distant1, g3), ACROSS), step(after(close1, g3), ACROSS)
    distant2, close2 = exchange(part, 2)
    b3 = add(distant2, g3)
    k3 = step(b3, INN)
    r0, r1 = step(add(b2, r2), MID), step(add(e1, k2), PAIR)
    kept = grid_sum_step(after(kept, k3), CROSS)
    k2 = step(after(add(b3, k3), r0), MID)
    close0, distant0 = roles(second, 0, near)
    sum_a = close_a.astype(F32) + h1_a.astype(F32) + r0.astype(F32) + r1.astype(F32)
    b2 = add(distant0, g1)
    r2 = step(b2, INN)
    e1 = add(add(close2, h3), k2)
    r1 = step(e1, PAIR)
    r0 = step(add(b2, r2), MID)
    sums = grid_sum_end(after(kept, r2), terms_a[2].shape)
    grad_a = finish(0, back_a, line_a, after(sum_a, r2))
    sum_b = close0.astype(F32) + h1.astype(F32) + r0.astype(F32) + r1.astype(F32)
    grad_b = finish(1, back_b, line_b, sum_b)
    return (out_a, out_b), sums, (grad_a, grad_b)


def linear_any(own, cross_w, cross_b):
    rows = own.shape[0]
    full = lax.all_gather(own, "tensor", axis=1, tiled=True)
    half = full.shape[1] // 2
    core = lax.axis_index("dp")
    kept = lax.dynamic_slice_in_dim(full, core * half, half, 1)
    other = swap(lax.dynamic_slice_in_dim(full, (1 - core) * half, half, 1))
    total = jnp.dot(jnp.concatenate([kept, other], axis=0), cross_w, preferred_element_type=F32)
    return total[:rows] + swap(total[rows:].astype(BF16)).astype(F32) + cross_b


def back_any(d_linear, cross_w):
    rows = d_linear.shape[0]
    both = jnp.concatenate([d_linear, swap(d_linear)], axis=0)
    contract = (((1,), (1,)), ((), ()))
    terms = lax.dot_general(both, cross_w, contract, preferred_element_type=F32).astype(BF16)
    own, other = terms[:rows], swap(terms[rows:])
    first = lax.axis_index("dp") == 0
    full = jnp.concatenate([jnp.where(first, own, other), jnp.where(first, other, own)], axis=1)
    return lax.psum_scatter(full, "tensor", scatter_dimension=1, tiled=True).astype(F32)


def shards(inputs, cross_w, cross_b, mix_weight, mix_bias, out_weight, cotangent):
    own = inputs[0]
    rows, width = own.shape
    tensor_count, dp_count = lax.axis_size("tensor"), lax.axis_size("dp")
    small = mix_weight, mix_bias, out_weight
    if tensor_count == 8:
        half = rows // tensor_count // 2
        by_owner = own.reshape(tensor_count, 2 * half, width)
        halves = [by_owner[:, c * half : (c + 1) * half].reshape(rows // 2, width) for c in range(2)]
        up = [cotangent[0, c * half : (c + 1) * half] for c in range(2)]
        compressed, sums, grads = grid_path(halves, cross_w, cross_b, up, small)
        compressed = jnp.concatenate(compressed, axis=0)
        grads = [grad.reshape(tensor_count, half, width) for grad in grads]
        grad = jnp.concatenate(grads, axis=1).reshape(rows, width)
    else:
        base = own.astype(F32)
        linear = linear_any(own, cross_w, cross_b)
        owned = exchange_rows((base * linear + base).astype(BF16), tensor_count)
        compressed, d_rows, *terms = interact(owned, cotangent[0], *small)
        d_crossed = exchange_rows(d_rows, tensor_count).astype(F32)
        back = back_any((d_crossed * base).astype(BF16), cross_w)
        grad = (d_crossed * (linear + 1.0) + back).astype(BF16)
        sums = [value.astype(F32) for value in lax.psum([t.astype(BF16) for t in terms], ("tensor", "dp"))]
    row_total = rows * dp_count
    return compressed[None], grad[None], *(value / row_total for value in sums)


def solution(mesh):
    return jax.shard_map(
        shards,
        mesh=mesh,
        in_specs=(
            P(("groups", "dp"), None, "tensor"),
            P("dp", "tensor"),
            P("tensor"),
            P(),
            P(),
            P(),
            P(("groups", "dp"), "tensor", None),
        ),
        out_specs=(
            P(("groups", "dp"), "tensor", None),
            P(("groups", "dp"), None, "tensor"),
            P("groups", None),
            P("groups"),
            P("groups", None),
        ),
        check_vma=False,
    )
```

profile of v0, /device:TPU:0, one launch (start us, length us, event | category | flops | bytes accessed | tf_op | source)
XLA Modules:
  0.0 345.5 jit_solution(322927810196982171)
XLA Ops:
  0.6 2.1 fusion.11
  3.4 3.0 collective-permute-start.1
  6.5 4.4 %collective-permute-start.2 = (bf16[128,2048]{1,0:T(8,128)(2,1)S(1)}, bf16[128,2048]{1,0:T(8,128)(2,1)S(1)}, u32[]{:S(2)}, u32[]{:S(2)}) collective-permute-start(bf16[128,2048]{1,0:T(8,128)(2,1)S(1)} %bitcast.61), channel_id=1, source_target_pairs={{0,4},{2,6},{4,0},{6,2},{8,12},{10,14},{12,8},{14,10},{1,5},{3,7},... | collective-permute-start | bytes 1572872 | tf_op jit(solution)/shard_map/ppermute | solution.py:216
  10.8 7.6 %collective-permute-done.1.refs_4_ = bf16[128,2048]{1,0:T(8,128)(2,1)S(1)} collective-permute-done((bf16[128,2048]{1,0:T(8,128)(2,1)S(1)}, bf16[128,2048]{1,0:T(8,128)(2,1)S(1)}, u32[]{:S(2)}, u32[]{:S(2)}) %collective-permute-start.1) | collective-permute-done | bytes 524320 | tf_op jit(solution)/shard_map/ppermute | solution.py:216
  18.4 3.8 %collective-permute-done.2.refs_8_ = bf16[128,2048]{1,0:T(8,128)(2,1)S(1)} collective-permute-done((bf16[128,2048]{1,0:T(8,128)(2,1)S(1)}, bf16[128,2048]{1,0:T(8,128)(2,1)S(1)}, u32[]{:S(2)}, u32[]{:S(2)}) %collective-permute-start.2) | collective-permute-done | bytes 524320 | tf_op jit(solution)/shard_map/ppermute | solution.py:216
  22.2 1.3 collective-permute-start.3
  24.1 1.5 collective-permute-start.7
  25.5 11.0 %collective-permute-done.3 = bf16[128,2048]{1,0:T(8,128)(2,1)S(1)} collective-permute-done((bf16[128,2048]{1,0:T(8,128)(2,1)S(1)}, bf16[128,2048]{1,0:T(8,128)(2,1)S(1)}, u32[]{:S(2)}, u32[]{:S(2)}) %collective-permute-start.3) | collective-permute-done | bytes 524320 | tf_op jit(solution)/shard_map/ppermute | solution.py:216
  37.3 1.3 collective-permute-start.11
  40.8 10.5 %collective-permute-done.11 = bf16[128,2048]{1,0:T(8,128)(2,1)S(1)} collective-permute-done((bf16[128,2048]{1,0:T(8,128)(2,1)}, bf16[128,2048]{1,0:T(8,128)(2,1)S(1)}, u32[]{:S(2)}, u32[]{:S(2)}) %collective-permute-start.11) | collective-permute-done | bytes 524320 | tf_op jit(solution)/shard_map/ppermute | solution.py:216
  53.0 2.7 collective-permute-start.17
  57.0 5.7 %collective-permute-done.14.refs_13_ = bf16[128,2048]{1,0:T(8,128)(2,1)} collective-permute-done((bf16[128,2048]{1,0:T(8,128)(2,1)S(1)}, bf16[128,2048]{1,0:T(8,128)(2,1)}, u32[]{:S(2)}, u32[]{:S(2)}) %collective-permute-start.14) | collective-permute-done | bytes 524320 | tf_op jit(solution)/shard_map/ppermute | solution.py:216
  66.2 1.5 collective-permute-start.21
  67.7 1.3 collective-permute-start.18
  69.0 1.3 collective-permute-start.22
  70.4 20.2 %forward_rows.2 = (f32[128,2048]{1,0:T(8,128)}, bf16[128,2048]{1,0:T(8,128)(2,1)}) custom-call(s32[5]{0:T(128)} %stack.49.plan_ref, bf16[128,2048]{1,0:T(8,128)(2,1)} %bitcast.63, bf16[128,2048]{1,0:T(8,128)(2,1)} %copy-done.6, bf16[128,2048]{1,0:T(8,128)(2,1)} %copy-done.21, bf16[128,2048]{1,0:T(8,128)(2,1)} %collective-permute-done.5.refs_3_, ...), custom_call_target="tpu_custom_call" | custom-call | flops 8589934592 | bytes 33554432 | tf_op jit(solution)/shard_map/forward_rows/pallas_call | solution.py:73
  91.0 1.4 collective-permute-start.25
  94.8 7.7 %all-to-all-start = ((bf16[8,16,16,128]{3,2,1,0:T(8,128)(2,1)}), bf16[8,16,16,128]{3,2,1,0:T(8,128)(2,1)}, u32[]{:S(2)}, u32[]{:S(2)}) async-start(bf16[8,16,16,128]{3,2,1,0:T(8,128)(2,1)} %bitcast.16), calls=%async_computation | async-start | bytes 1048576 | tf_op jit(solution)/shard_map/all_to_all | solution.py:265
  102.5 2.0 collective-permute-start.24
  105.1 8.0 %collective-permute-done.25 = bf16[128,2048]{1,0:T(8,128)(2,1)} collective-permute-done((bf16[128,2048]{1,0:T(8,128)(2,1)}, bf16[128,2048]{1,0:T(8,128)(2,1)}, u32[]{:S(2)}, u32[]{:S(2)}) %collective-permute-start.25) | collective-permute-done | bytes 524320 | tf_op jit(solution)/shard_map/ppermute | solution.py:216
  114.2 8.1 %collective-permute-done.24.refs_5_ = bf16[128,2048]{1,0:T(8,128)(2,1)S(1)} collective-permute-done((bf16[128,2048]{1,0:T(8,128)(2,1)S(1)}, bf16[128,2048]{1,0:T(8,128)(2,1)S(1)}, u32[]{:S(2)}, u32[]{:S(2)}) %collective-permute-start.24) | collective-permute-done | bytes 524320 | tf_op jit(solution)/shard_map/ppermute | solution.py:216
  123.1 1.3 slice_bitcast_fusion
  125.7 6.7 %interact_rows.2 = (bf16[16,128,128]{2,1,0:T(8,128)(2,1)}, bf16[8,16,16,128]{3,2,1,0:T(8,128)(2,1)}, f32[128,512]{1,0:T(8,128)}, f32[8,512]{1,0:T(8,128)}, f32[512,128]{1,0:T(8,128)}) custom-call(bf16[8,16,16,128]{3,2,1,0:T(8,128)(2,1)} %all-to-all-done.x_ref, bf16[16,128,128]{2,1,0:T(8,128)(2,1)} %bitcast.72, bf16[128,512]{1,0:T(8,128)(2,1)} %mix_ref.3, ...), custom_call_target="tpu_custom_call" | custom-call | flops 1744830464 | bytes 2097152 | tf_op jit(solution)/shard_map/interact_rows/pallas_call | solution.py:194
  133.1 2.4 collective-permute-done.32.refs_13_
  135.9 5.2 %all-to-all-start.1 = ((bf16[8,16,16,128]{3,2,1,0:T(8,128)(2,1)}), bf16[8,16,16,128]{3,2,1,0:T(8,128)(2,1)S(1)}, u32[]{:S(2)}, u32[]{:S(2)}) async-start(bf16[8,16,16,128]{3,2,1,0:T(8,128)(2,1)} %get-tuple-element.108), calls=%async_computation.1 | async-start | bytes 1048576 | tf_op jit(solution)/shard_map/all_to_all | solution.py:266
  141.1 20.3 %forward_rows.3 = (f32[128,2048]{1,0:T(8,128)}, bf16[128,2048]{1,0:T(8,128)(2,1)}) custom-call(s32[5]{0:T(128)} %stack.49.plan_ref, bf16[128,2048]{1,0:T(8,128)(2,1)} %bitcast.7.refs_0_, bf16[128,2048]{1,0:T(8,128)(2,1)} %copy-done.8, bf16[128,2048]{1,0:T(8,128)(2,1)} %collective-permute-done.26.refs_2_, bf16[128,2048]{1,0:T(8,128)(2,1)} %collective-permute-done.27.refs_3_, ...), custom_call_target="tpu_custom_call" | custom-call | flops 8589934592 | bytes 33554432 | tf_op jit(solution)/shard_map/forward_rows/pallas_call | solution.py:73
  162.3 1.5 collective-permute-done.35
  163.8 2.5 fusion.8
  167.1 6.0 %all-to-all-start.2 = ((bf16[8,16,16,128]{3,2,1,0:T(8,128)(2,1)}), bf16[8,16,16,128]{3,2,1,0:T(8,128)(2,1)}, u32[]{:S(2)}, u32[]{:S(2)}) async-start(bf16[8,16,16,128]{3,2,1,0:T(8,128)(2,1)} %bitcast.27), calls=%async_computation.2 | async-start | bytes 1048576 | tf_op jit(solution)/shard_map/all_to_all | solution.py:265
  174.5 10.8 %back_part.4 = (bf16[128,2048]{1,0:T(8,128)(2,1)}, bf16[128,2048]{1,0:T(8,128)(2,1)}, bf16[128,2048]{1,0:T(8,128)(2,1)}, bf16[128,2048]{1,0:T(8,128)(2,1)}) custom-call(s32[2]{0:T(128)} %pad_add_fusion.plan_ref, bf16[128,2048]{1,0:T(8,128)(2,1)} %copy-done.2, bf16[128,2048]{1,0:T(8,128)(2,1)} %copy-done.4, bf16[8192,2048]{1,0:T(8,128)(2,1)} %w_ref.7), custom_call_target="tpu_custom_call" | custom-call | flops 4294967296 | bytes 16777216 | tf_op jit(solution)/shard_map/back_part/pallas_call | solution.py:127
  185.3 2.6 all-to-all-done.2.x_ref
  190.1 2.2 broadcast_select_fusion.6
  192.3 1.5 collective-permute-start.38
  194.3 6.8 %interact_rows.3 = (bf16[16,128,128]{2,1,0:T(8,128)(2,1)}, bf16[8,16,16,128]{3,2,1,0:T(8,128)(2,1)}, f32[128,512]{1,0:T(8,128)}, f32[8,512]{1,0:T(8,128)}, f32[512,128]{1,0:T(8,128)}) custom-call(bf16[8,16,16,128]{3,2,1,0:T(8,128)(2,1)} %all-to-all-done.2.x_ref, bf16[16,128,128]{2,1,0:T(8,128)(2,1)} %bitcast.71, bf16[128,512]{1,0:T(8,128)(2,1)} %mix_ref.3, ...), custom_call_target="tpu_custom_call" | custom-call | flops 1744830464 | bytes 2097152 | tf_op jit(solution)/shard_map/interact_rows/pallas_call | solution.py:194
  201.1 3.8 %all-to-all-start.3 = ((bf16[8,16,16,128]{3,2,1,0:T(8,128)(2,1)}), bf16[8,16,16,128]{3,2,1,0:T(8,128)(2,1)S(1)}, u32[]{:S(2)}, u32[]{:S(2)}) async-start(bf16[8,16,16,128]{3,2,1,0:T(8,128)(2,1)} %get-tuple-element.124), calls=%async_computation.3 | async-start | bytes 1048576 | tf_op jit(solution)/shard_map/all_to_all | solution.py:266
  206.2 1.8 copy_bitcast_fusion
  209.1 10.8 %back_part.5 = (bf16[128,2048]{1,0:T(8,128)(2,1)}, bf16[128,2048]{1,0:T(8,128)(2,1)}, bf16[128,2048]{1,0:T(8,128)(2,1)}, bf16[128,2048]{1,0:T(8,128)(2,1)}) custom-call(s32[2]{0:T(128)} %pad_add_fusion.1.plan_ref, bf16[128,2048]{1,0:T(8,128)(2,1)} %copy-done.2, bf16[128,2048]{1,0:T(8,128)(2,1)} %copy-done.4, bf16[8192,2048]{1,0:T(8,128)(2,1)} %w_ref.7), custom_call_target="tpu_custom_call" | custom-call | flops 4294967296 | bytes 16777216 | tf_op jit(solution)/shard_map/back_part/pallas_call | solution.py:127
  219.9 2.9 collective-permute-done.39
  222.8 1.5 collective-permute-start.44
  224.5 1.4 fusion.own_ref
  226.2 2.3 broadcast_select_fusion.5
  229.0 2.3 add_convert_fusion.11
  231.3 3.5 %collective-permute-start.46 = (bf16[128,2048]{1,0:T(8,128)(2,1)}, bf16[128,2048]{1,0:T(8,128)(2,1)}, u32[]{:S(2)}, u32[]{:S(2)}) collective-permute-start(bf16[128,2048]{1,0:T(8,128)(2,1)} %add_convert_fusion.11), channel_id=1, source_target_pairs={{0,4},{2,6},{12,8},{14,10},{1,5},{3,7},{13,9},{15,11},{16,20},{18,... | collective-permute-start | bytes 1572872 | tf_op jit(solution)/shard_map/ppermute | solution.py:216
  237.1 10.8 %back_part.6 = (bf16[128,2048]{1,0:T(8,128)(2,1)}, bf16[128,2048]{1,0:T(8,128)(2,1)}, bf16[128,2048]{1,0:T(8,128)(2,1)}, bf16[128,2048]{1,0:T(8,128)(2,1)}) custom-call(s32[2]{0:T(128)} %pad_add_fusion.plan_ref, bf16[128,2048]{1,0:T(8,128)(2,1)} %copy-done.3, bf16[128,2048]{1,0:T(8,128)(2,1)} %copy-done.5, bf16[8192,2048]{1,0:T(8,128)(2,1)} %w_ref.7), custom_call_target="tpu_custom_call" | custom-call | flops 4294967296 | bytes 16777216 | tf_op jit(solution)/shard_map/back_part/pallas_call | solution.py:127
  248.5 2.2 add_convert_fusion.9
  250.7 1.5 collective-permute-start.50
  252.2 1.4 add_convert_fusion.10
  254.3 5.8 %collective-permute-start.51 = (bf16[128,2048]{1,0:T(8,128)(2,1)S(1)}, bf16[128,2048]{1,0:T(8,128)(2,1)}, u32[]{:S(2)}, u32[]{:S(2)}) collective-permute-start(bf16[128,2048]{1,0:T(8,128)(2,1)S(1)} %add_convert_fusion.10), channel_id=1, source_target_pairs={{0,4},{2,6},{12,8},{14,10},{1,5},{3,7},{13,9},{15,11},{16,20},{18,... | collective-permute-start | bytes 1572872 | tf_op jit(solution)/shard_map/ppermute | solution.py:216
  261.8 10.8 %back_part.7 = (bf16[128,2048]{1,0:T(8,128)(2,1)}, bf16[128,2048]{1,0:T(8,128)(2,1)}, bf16[128,2048]{1,0:T(8,128)(2,1)}, bf16[128,2048]{1,0:T(8,128)(2,1)}) custom-call(s32[2]{0:T(128)} %pad_add_fusion.1.plan_ref, bf16[128,2048]{1,0:T(8,128)(2,1)} %copy-done.3, bf16[128,2048]{1,0:T(8,128)(2,1)} %copy-done.5, bf16[8192,2048]{1,0:T(8,128)(2,1)} %w_ref.7), custom_call_target="tpu_custom_call" | custom-call | flops 4294967296 | bytes 16777216 | tf_op jit(solution)/shard_map/back_part/pallas_call | solution.py:127
  272.6 1.3 add_convert_fusion.8
  274.6 1.5 collective-permute-start.63
  276.2 1.7 add_convert_fusion.6
  278.5 2.3 collective-permute-start.54
  280.8 1.4 add_convert_fusion.2
  282.3 1.9 collective-permute-start.64
  285.5 7.6 %collective-permute-done.54 = bf16[128,2048]{1,0:T(8,128)(2,1)S(1)} collective-permute-done((bf16[128,2048]{1,0:T(8,128)(2,1)S(1)}, bf16[128,2048]{1,0:T(8,128)(2,1)S(1)}, u32[]{:S(2)}, u32[]{:S(2)}) %collective-permute-start.54) | collective-permute-done | bytes 524320 | tf_op jit(solution)/shard_map/ppermute | solution.py:216
  293.5 1.5 convert_add_fusion
  294.9 8.5 %collective-permute-done.64 = bf16[128,2048]{1,0:T(8,128)(2,1)S(1)} collective-permute-done((bf16[128,2048]{1,0:T(8,128)(2,1)S(1)}, bf16[128,2048]{1,0:T(8,128)(2,1)S(1)}, u32[]{:S(2)}, u32[]{:S(2)}) %collective-permute-start.64) | collective-permute-done | bytes 524320 | tf_op jit(solution)/shard_map/ppermute | solution.py:216
  304.3 5.2 %collective-permute-start.67 = (bf16[136,512]{1,0:T(8,128)(2,1)S(1)}, bf16[136,512]{1,0:T(8,128)(2,1)S(1)}, u32[]{:S(2)}, u32[]{:S(2)}) collective-permute-start(bf16[136,512]{1,0:T(8,128)(2,1)S(1)} %convert_add_fusion.2), channel_id=1, source_target_pairs={{0,8},{2,10},{4,12},{6,14},{8,0},{10,2},{12,4},{14,6},{1,9},{3,11}... | collective-permute-start | bytes 417800 | tf_op jit(solution)/shard_map/ppermute | solution.py:216
  309.8 1.3 collective-permute-start.59
  311.1 15.4 %collective-permute-done.67 = bf16[136,512]{1,0:T(8,128)(2,1)S(1)} collective-permute-done((bf16[136,512]{1,0:T(8,128)(2,1)S(1)}, bf16[136,512]{1,0:T(8,128)(2,1)S(1)}, u32[]{:S(2)}, u32[]{:S(2)}) %collective-permute-start.67) | collective-permute-done | bytes 139296 | tf_op jit(solution)/shard_map/ppermute | solution.py:216
  328.7 1.4 collective-permute-start.61
  333.6 8.3 %collective-permute-done.66 = bf16[128,2048]{1,0:T(8,128)(2,1)} collective-permute-done((bf16[128,2048]{1,0:T(8,128)(2,1)}, bf16[128,2048]{1,0:T(8,128)(2,1)}, u32[]{:S(2)}, u32[]{:S(2)}) %collective-permute-start.66) | collective-permute-done | bytes 524320 | tf_op jit(solution)/shard_map/ppermute | solution.py:216
  341.9 2.5 fusion.7
  (218 shorter events, 43.3 us)
Async XLA Ops:
  2.7 8.1 %collective-permute-start = (bf16[128,2048]{1,0:T(8,128)(2,1)S(1)}, bf16[128,2048]{1,0:T(8,128)(2,1)S(1)}, u32[]{:S(2)}, u32[]{:S(2)}) collective-permute-start(bf16[128,2048]{1,0:T(8,128)(2,1)S(1)} %bitcast.59), channel_id=1, source_target_pairs={{4,8},{6,10},{8,4},{10,6},{5,9},{7,11},{9,5},{11,7},{20,24},{22,26... | collective-permute-start | bytes 1572872 | tf_op jit(solution)/shard_map/ppermute | solution.py:216
  3.4 15.0 %collective-permute-start.1 = (bf16[128,2048]{1,0:T(8,128)(2,1)S(1)}, bf16[128,2048]{1,0:T(8,128)(2,1)S(1)}, u32[]{:S(2)}, u32[]{:S(2)}) collective-permute-start(bf16[128,2048]{1,0:T(8,128)(2,1)S(1)} %bitcast.60), channel_id=1, source_target_pairs={{0,2},{2,0},{4,6},{6,4},{8,10},{10,8},{12,14},{14,12},{1,3},{3,1},... | collective-permute-start | bytes 1572872 | tf_op jit(solution)/shard_map/ppermute | solution.py:216
  6.5 15.7 %collective-permute-start.2 = (bf16[128,2048]{1,0:T(8,128)(2,1)S(1)}, bf16[128,2048]{1,0:T(8,128)(2,1)S(1)}, u32[]{:S(2)}, u32[]{:S(2)}) collective-permute-start(bf16[128,2048]{1,0:T(8,128)(2,1)S(1)} %bitcast.61), channel_id=1, source_target_pairs={{0,4},{2,6},{4,0},{6,2},{8,12},{10,14},{12,8},{14,10},{1,5},{3,7},... | collective-permute-start | bytes 1572872 | tf_op jit(solution)/shard_map/ppermute | solution.py:216
  22.2 14.4 %collective-permute-start.3 = (bf16[128,2048]{1,0:T(8,128)(2,1)S(1)}, bf16[128,2048]{1,0:T(8,128)(2,1)S(1)}, u32[]{:S(2)}, u32[]{:S(2)}) collective-permute-start(bf16[128,2048]{1,0:T(8,128)(2,1)S(1)} %collective-permute-done), channel_id=1, source_target_pairs={{4,0},{6,2},{8,12},{10,14},{5,1},{7,3},{9,13},{11,15},{20,16},{22,... | collective-permute-start | bytes 1572872 | tf_op jit(solution)/shard_map/ppermute | solution.py:216
  23.5 13.1 %collective-permute-start.6 = (bf16[128,2048]{1,0:T(8,128)(2,1)S(1)}, bf16[128,2048]{1,0:T(8,128)(2,1)S(1)}, u32[]{:S(2)}, u32[]{:S(2)}) collective-permute-start(bf16[128,2048]{1,0:T(8,128)(2,1)S(1)} %collective-permute-done.2.refs_8_), channel_id=1, source_target_pairs={{0,2},{2,0},{4,6},{6,4},{8,10},{10,8},{12,14},{14,12},{1,3},{3,1},... | collective-permute-start | bytes 1572872 | tf_op jit(solution)/shard_map/ppermute | solution.py:216
  24.1 12.5 %collective-permute-start.7 = (bf16[128,2048]{1,0:T(8,128)(2,1)S(1)}, bf16[128,2048]{1,0:T(8,128)(2,1)}, u32[]{:S(2)}, u32[]{:S(2)}) collective-permute-start(bf16[128,2048]{1,0:T(8,128)(2,1)S(1)} %collective-permute-done.2.refs_8_), channel_id=1, source_target_pairs={{4,8},{6,10},{8,4},{10,6},{5,9},{7,11},{9,5},{11,7},{20,24},{22,26... | collective-permute-start | bytes 1572872 | tf_op jit(solution)/shard_map/ppermute | solution.py:216
  37.3 14.0 %collective-permute-start.11 = (bf16[128,2048]{1,0:T(8,128)(2,1)}, bf16[128,2048]{1,0:T(8,128)(2,1)S(1)}, u32[]{:S(2)}, u32[]{:S(2)}) collective-permute-start(bf16[128,2048]{1,0:T(8,128)(2,1)} %collective-permute-done.7), channel_id=1, source_target_pairs={{4,0},{6,2},{8,12},{10,14},{5,1},{7,3},{9,13},{11,15},{20,16},{22,... | collective-permute-start | bytes 1572872 | tf_op jit(solution)/shard_map/ppermute | solution.py:216
  39.7 12.2 %collective-permute-start.8 = (bf16[128,2048]{1,0:T(8,128)(2,1)S(1)}, bf16[128,2048]{1,0:T(8,128)(2,1)}, u32[]{:S(2)}, u32[]{:S(2)}) collective-permute-start(bf16[128,2048]{1,0:T(8,128)(2,1)S(1)} %broadcast_select_fusion.11.refs_1_), channel_id=1, source_target_pairs={{0,2},{2,0},{4,6},{6,4},{8,10},{10,8},{12,14},{14,12},{1,3},{3,1},... | collective-permute-start | bytes 1572872 | tf_op jit(solution)/shard_map/ppermute | solution.py:216
  40.3 15.4 %collective-permute-start.4 = (bf16[128,2048]{1,0:T(8,128)(2,1)S(1)}, bf16[128,2048]{1,0:T(8,128)(2,1)S(1)}, u32[]{:S(2)}, u32[]{:S(2)}) collective-permute-start(bf16[128,2048]{1,0:T(8,128)(2,1)S(1)} %bitcast.62), channel_id=1, source_target_pairs={{0,1},{1,0},{2,3},{3,2},{4,5},{5,4},{6,7},{7,6},{8,9},{9,8},{10,11... | collective-permute-start | bytes 1572872 | tf_op jit(solution)/shard_map/ppermute | solution.py:220
  40.3 16.1 %collective-permute-start.9 = (bf16[128,2048]{1,0:T(8,128)(2,1)S(1)}, bf16[128,2048]{1,0:T(8,128)(2,1)S(1)}, u32[]{:S(2)}, u32[]{:S(2)}) collective-permute-start(bf16[128,2048]{1,0:T(8,128)(2,1)S(1)} %collective-permute-done.1.refs_4_), channel_id=1, source_target_pairs={{0,1},{1,0},{2,3},{3,2},{4,5},{5,4},{6,7},{7,6},{8,9},{9,8},{10,11... | collective-permute-start | bytes 1572872 | tf_op jit(solution)/shard_map/ppermute | solution.py:220
  40.8 15.7 %collective-permute-start.12 = (bf16[128,2048]{1,0:T(8,128)(2,1)S(1)}, bf16[128,2048]{1,0:T(8,128)(2,1)S(1)}, u32[]{:S(2)}, u32[]{:S(2)}) collective-permute-start(bf16[128,2048]{1,0:T(8,128)(2,1)S(1)} %collective-permute-done.2.refs_8_), channel_id=1, source_target_pairs={{0,1},{1,0},{2,3},{3,2},{4,5},{5,4},{6,7},{7,6},{8,9},{9,8},{10,11... | collective-permute-start | bytes 1572872 | tf_op jit(solution)/shard_map/ppermute | solution.py:220
  51.9 10.8 %collective-permute-start.14 = (bf16[128,2048]{1,0:T(8,128)(2,1)S(1)}, bf16[128,2048]{1,0:T(8,128)(2,1)}, u32[]{:S(2)}, u32[]{:S(2)}) collective-permute-start(bf16[128,2048]{1,0:T(8,128)(2,1)S(1)} %broadcast_select_fusion.10.refs_9_), channel_id=1, source_target_pairs={{0,2},{2,0},{4,6},{6,4},{8,10},{10,8},{12,14},{14,12},{1,3},{3,1},... | collective-permute-start | bytes 1572872 | tf_op jit(solution)/shard_map/ppermute | solution.py:216
  53.0 10.5 %collective-permute-start.17 = (bf16[128,2048]{1,0:T(8,128)(2,1)}, bf16[128,2048]{1,0:T(8,128)(2,1)}, u32[]{:S(2)}, u32[]{:S(2)}) collective-permute-start(bf16[128,2048]{1,0:T(8,128)(2,1)} %bitcast.7.refs_0_), channel_id=1, source_target_pairs={{0,4},{2,6},{4,0},{6,2},{8,12},{10,14},{12,8},{14,10},{1,5},{3,7},... | collective-permute-start | bytes 1572872 | tf_op jit(solution)/shard_map/ppermute | solution.py:216
  55.7 7.8 %collective-permute-start.19 = (bf16[128,2048]{1,0:T(8,128)(2,1)}, bf16[128,2048]{1,0:T(8,128)(2,1)S(1)}, u32[]{:S(2)}, u32[]{:S(2)}) collective-permute-start(bf16[128,2048]{1,0:T(8,128)(2,1)} %bitcast.7.refs_0_), channel_id=1, source_target_pairs={{4,8},{6,10},{8,4},{10,6},{5,9},{7,11},{9,5},{11,7},{20,24},{22,26... | collective-permute-start | bytes 1572872 | tf_op jit(solution)/shard_map/ppermute | solution.py:216
  56.4 9.1 %collective-permute-start.5 = (bf16[128,2048]{1,0:T(8,128)(2,1)S(1)}, bf16[128,2048]{1,0:T(8,128)(2,1)}, u32[]{:S(2)}, u32[]{:S(2)}) collective-permute-start(bf16[128,2048]{1,0:T(8,128)(2,1)S(1)} %broadcast_select_fusion.11.refs_1_), channel_id=1, source_target_pairs={{0,1},{1,0},{2,3},{3,2},{4,5},{5,4},{6,7},{7,6},{8,9},{9,8},{10,11... | collective-permute-start | bytes 1572872 | tf_op jit(solution)/shard_map/ppermute | solution.py:220
  56.5 9.7 %collective-permute-start.15 = (bf16[128,2048]{1,0:T(8,128)(2,1)S(1)}, bf16[128,2048]{1,0:T(8,128)(2,1)}, u32[]{:S(2)}, u32[]{:S(2)}) collective-permute-start(bf16[128,2048]{1,0:T(8,128)(2,1)S(1)} %collective-permute-done.6.refs_12_), channel_id=1, source_target_pairs={{0,1},{1,0},{2,3},{3,2},{4,5},{5,4},{6,7},{7,6},{8,9},{9,8},{10,11... | collective-permute-start | bytes 1572872 | tf_op jit(solution)/shard_map/ppermute | solution.py:220
  64.3 6.0 %collective-permute-start.16 = (bf16[128,2048]{1,0:T(8,128)(2,1)}, bf16[128,2048]{1,0:T(8,128)(2,1)}, u32[]{:S(2)}, u32[]{:S(2)}) collective-permute-start(bf16[128,2048]{1,0:T(8,128)(2,1)} %collective-permute-done.14.refs_13_), channel_id=1, source_target_pairs={{0,1},{1,0},{2,3},{3,2},{4,5},{5,4},{6,7},{7,6},{8,9},{9,8},{10,11... | collective-permute-start | bytes 1572872 | tf_op jit(solution)/shard_map/ppermute | solution.py:220
  65.5 25.4 %collective-permute-start.20 = (bf16[128,2048]{1,0:T(8,128)(2,1)}, bf16[128,2048]{1,0:T(8,128)(2,1)}, u32[]{:S(2)}, u32[]{:S(2)}) collective-permute-start(bf16[128,2048]{1,0:T(8,128)(2,1)} %collective-permute-done.17.refs_8_), channel_id=1, source_target_pairs={{0,2},{2,0},{4,6},{6,4},{8,10},{10,8},{12,14},{14,12},{1,3},{3,1},... | collective-permute-start | bytes 1572872 | tf_op jit(solution)/shard_map/ppermute | solution.py:216
  66.2 24.7 %collective-permute-start.21 = (bf16[128,2048]{1,0:T(8,128)(2,1)}, bf16[128,2048]{1,0:T(8,128)(2,1)}, u32[]{:S(2)}, u32[]{:S(2)}) collective-permute-start(bf16[128,2048]{1,0:T(8,128)(2,1)} %collective-permute-done.17.refs_8_), channel_id=1, source_target_pairs={{4,8},{6,10},{8,4},{10,6},{5,9},{7,11},{9,5},{11,7},{20,24},{22,26... | collective-permute-start | bytes 1572872 | tf_op jit(solution)/shard_map/ppermute | solution.py:216
  67.7 23.2 %collective-permute-start.18 = (bf16[128,2048]{1,0:T(8,128)(2,1)}, bf16[128,2048]{1,0:T(8,128)(2,1)}, u32[]{:S(2)}, u32[]{:S(2)}) collective-permute-start(bf16[128,2048]{1,0:T(8,128)(2,1)} %bitcast.7.refs_0_), channel_id=1, source_target_pairs={{0,2},{2,0},{4,6},{6,4},{8,10},{10,8},{12,14},{14,12},{1,3},{3,1},... | collective-permute-start | bytes 1572872 | tf_op jit(solution)/shard_map/ppermute | solution.py:216
  69.0 21.9 %collective-permute-start.22 = (bf16[128,2048]{1,0:T(8,128)(2,1)}, bf16[128,2048]{1,0:T(8,128)(2,1)}, u32[]{:S(2)}, u32[]{:S(2)}) collective-permute-start(bf16[128,2048]{1,0:T(8,128)(2,1)} %copy-done.27), channel_id=1, source_target_pairs={{4,0},{6,2},{8,12},{10,14},{5,1},{7,3},{9,13},{11,15},{20,16},{22,... | collective-permute-start | bytes 1572872 | tf_op jit(solution)/shard_map/ppermute | solution.py:216
  91.0 22.1 %collective-permute-start.25 = (bf16[128,2048]{1,0:T(8,128)(2,1)}, bf16[128,2048]{1,0:T(8,128)(2,1)}, u32[]{:S(2)}, u32[]{:S(2)}) collective-permute-start(bf16[128,2048]{1,0:T(8,128)(2,1)} %collective-permute-done.21), channel_id=1, source_target_pairs={{4,0},{6,2},{8,12},{10,14},{5,1},{7,3},{9,13},{11,15},{20,16},{22,... | collective-permute-start | bytes 1572872 | tf_op jit(solution)/shard_map/ppermute | solution.py:216
  94.8 30.9 %all-to-all-start = ((bf16[8,16,16,128]{3,2,1,0:T(8,128)(2,1)}), bf16[8,16,16,128]{3,2,1,0:T(8,128)(2,1)}, u32[]{:S(2)}, u32[]{:S(2)}) async-start(bf16[8,16,16,128]{3,2,1,0:T(8,128)(2,1)} %bitcast.16), calls=%async_computation | async-start | bytes 1048576 | tf_op jit(solution)/shard_map/all_to_all | solution.py:265
  102.5 19.7 %collective-permute-start.24 = (bf16[128,2048]{1,0:T(8,128)(2,1)S(1)}, bf16[128,2048]{1,0:T(8,128)(2,1)S(1)}, u32[]{:S(2)}, u32[]{:S(2)}) collective-permute-start(bf16[128,2048]{1,0:T(8,128)(2,1)S(1)} %broadcast_select_fusion.9.refs_1_), channel_id=1, source_target_pairs={{0,2},{2,0},{4,6},{6,4},{8,10},{10,8},{12,14},{14,12},{1,3},{3,1},... | collective-permute-start | bytes 1572872 | tf_op jit(solution)/shard_map/ppermute | solution.py:216
  104.5 27.9 %collective-permute-start.30 = (bf16[128,2048]{1,0:T(8,128)(2,1)}, bf16[128,2048]{1,0:T(8,128)(2,1)}, u32[]{:S(2)}, u32[]{:S(2)}) collective-permute-start(bf16[128,2048]{1,0:T(8,128)(2,1)} %collective-permute-done.17.refs_8_), channel_id=1, source_target_pairs={{0,1},{1,0},{2,3},{3,2},{4,5},{5,4},{6,7},{7,6},{8,9},{9,8},{10,11... | collective-permute-start | bytes 1572872 | tf_op jit(solution)/shard_map/ppermute | solution.py:220
  104.6 28.0 %collective-permute-start.27 = (bf16[128,2048]{1,0:T(8,128)(2,1)S(1)}, bf16[128,2048]{1,0:T(8,128)(2,1)}, u32[]{:S(2)}, u32[]{:S(2)}) collective-permute-start(bf16[128,2048]{1,0:T(8,128)(2,1)S(1)} %broadcast_select_fusion.9.refs_1_), channel_id=1, source_target_pairs={{0,1},{1,0},{2,3},{3,2},{4,5},{5,4},{6,7},{7,6},{8,9},{9,8},{10,11... | collective-permute-start | bytes 1572872 | tf_op jit(solution)/shard_map/ppermute | solution.py:220
  122.3 13.2 %collective-permute-start.32 = (bf16[128,2048]{1,0:T(8,128)(2,1)S(1)}, bf16[128,2048]{1,0:T(8,128)(2,1)}, u32[]{:S(2)}, u32[]{:S(2)}) collective-permute-start(bf16[128,2048]{1,0:T(8,128)(2,1)S(1)} %broadcast_select_fusion.8.refs_9_), channel_id=1, source_target_pairs={{0,2},{2,0},{4,6},{6,4},{8,10},{10,8},{12,14},{14,12},{1,3},{3,1},... | collective-permute-start | bytes 1572872 | tf_op jit(solution)/shard_map/ppermute | solution.py:216
  123.0 12.4 %collective-permute-start.28 = (bf16[128,2048]{1,0:T(8,128)(2,1)}, bf16[128,2048]{1,0:T(8,128)(2,1)}, u32[]{:S(2)}, u32[]{:S(2)}) collective-permute-start(bf16[128,2048]{1,0:T(8,128)(2,1)} %collective-permute-done.18.refs_4_), channel_id=1, source_target_pairs={{0,1},{1,0},{2,3},{3,2},{4,5},{5,4},{6,7},{7,6},{8,9},{9,8},{10,11... | collective-permute-start | bytes 1572872 | tf_op jit(solution)/shard_map/ppermute | solution.py:220
  125.2 15.9 %collective-permute-start.33 = (bf16[128,2048]{1,0:T(8,128)(2,1)}, bf16[128,2048]{1,0:T(8,128)(2,1)}, u32[]{:S(2)}, u32[]{:S(2)}) collective-permute-start(bf16[128,2048]{1,0:T(8,128)(2,1)} %collective-permute-done.20.refs_12_), channel_id=1, source_target_pairs={{0,1},{1,0},{2,3},{3,2},{4,5},{5,4},{6,7},{7,6},{8,9},{9,8},{10,11... | collective-permute-start | bytes 1572872 | tf_op jit(solution)/shard_map/ppermute | solution.py:220
  132.5 8.6 %collective-permute-start.31 = (bf16[128,2048]{1,0:T(8,128)(2,1)S(1)}, bf16[128,2048]{1,0:T(8,128)(2,1)}, u32[]{:S(2)}, u32[]{:S(2)}) collective-permute-start(bf16[128,2048]{1,0:T(8,128)(2,1)S(1)} %broadcast_select_fusion.8.refs_9_), channel_id=1, source_target_pairs={{0,1},{1,0},{2,3},{3,2},{4,5},{5,4},{6,7},{7,6},{8,9},{9,8},{10,11... | collective-permute-start | bytes 1572872 | tf_op jit(solution)/shard_map/ppermute | solution.py:220
  132.6 8.5 %collective-permute-start.29 = (bf16[128,2048]{1,0:T(8,128)(2,1)}, bf16[128,2048]{1,0:T(8,128)(2,1)}, u32[]{:S(2)}, u32[]{:S(2)}) collective-permute-start(bf16[128,2048]{1,0:T(8,128)(2,1)} %copy-done.24), channel_id=1, source_target_pairs={{0,1},{1,0},{2,3},{3,2},{4,5},{5,4},{6,7},{7,6},{8,9},{9,8},{10,11... | collective-permute-start | bytes 1572872 | tf_op jit(solution)/shard_map/ppermute | solution.py:220
  135.9 25.6 %all-to-all-start.1 = ((bf16[8,16,16,128]{3,2,1,0:T(8,128)(2,1)}), bf16[8,16,16,128]{3,2,1,0:T(8,128)(2,1)S(1)}, u32[]{:S(2)}, u32[]{:S(2)}) async-start(bf16[8,16,16,128]{3,2,1,0:T(8,128)(2,1)} %get-tuple-element.108), calls=%async_computation.1 | async-start | bytes 1048576 | tf_op jit(solution)/shard_map/all_to_all | solution.py:266
  161.8 12.0 %collective-permute-start.36 = (bf16[128,2048]{1,0:T(8,128)(2,1)S(1)}, bf16[128,2048]{1,0:T(8,128)(2,1)S(1)}, u32[]{:S(2)}, u32[]{:S(2)}) collective-permute-start(bf16[128,2048]{1,0:T(8,128)(2,1)S(1)} %fusion.1.own_ref), channel_id=1, source_target_pairs={{0,1},{1,0},{2,3},{3,2},{4,5},{5,4},{6,7},{7,6},{8,9},{9,8},{10,11... | collective-permute-start | bytes 1572872 | tf_op jit(solution)/shard_map/ppermute | solution.py:220
  167.1 20.9 %all-to-all-start.2 = ((bf16[8,16,16,128]{3,2,1,0:T(8,128)(2,1)}), bf16[8,16,16,128]{3,2,1,0:T(8,128)(2,1)}, u32[]{:S(2)}, u32[]{:S(2)}) async-start(bf16[8,16,16,128]{3,2,1,0:T(8,128)(2,1)} %bitcast.27), calls=%async_computation.2 | async-start | bytes 1048576 | tf_op jit(solution)/shard_map/all_to_all | solution.py:265
  189.5 39.6 %collective-permute-start.45 = (bf16[128,2048]{1,0:T(8,128)(2,1)}, bf16[128,2048]{1,0:T(8,128)(2,1)}, u32[]{:S(2)}, u32[]{:S(2)}) collective-permute-start(bf16[128,2048]{1,0:T(8,128)(2,1)} %get-tuple-element.141), channel_id=1, source_target_pairs={{0,1},{1,0},{2,3},{3,2},{4,5},{5,4},{6,7},{7,6},{8,9},{9,8},{10,11... | collective-permute-start | bytes 1572872 | tf_op jit(solution)/shard_map/ppermute | solution.py:220
  192.3 27.6 %collective-permute-start.38 = (bf16[128,2048]{1,0:T(8,128)(2,1)}, bf16[128,2048]{1,0:T(8,128)(2,1)}, u32[]{:S(2)}, u32[]{:S(2)}) collective-permute-start(bf16[128,2048]{1,0:T(8,128)(2,1)} %get-tuple-element.186), channel_id=1, source_target_pairs={{0,2},{2,0},{4,6},{6,4},{8,10},{10,8},{12,14},{14,12},{1,3},{3,1},... | collective-permute-start | bytes 1572872 | tf_op jit(solution)/shard_map/ppermute | solution.py:216
  193.8 29.0 %collective-permute-start.39 = (bf16[128,2048]{1,0:T(8,128)(2,1)}, bf16[128,2048]{1,0:T(8,128)(2,1)}, u32[]{:S(2)}, u32[]{:S(2)}) collective-permute-start(bf16[128,2048]{1,0:T(8,128)(2,1)} %get-tuple-element.185), channel_id=1, source_target_pairs={{0,2},{2,0},{4,6},{6,4},{8,10},{10,8},{12,14},{14,12},{1,3},{3,1},... | collective-permute-start | bytes 1572872 | tf_op jit(solution)/shard_map/ppermute | solution.py:216
  201.1 23.2 %all-to-all-start.3 = ((bf16[8,16,16,128]{3,2,1,0:T(8,128)(2,1)}), bf16[8,16,16,128]{3,2,1,0:T(8,128)(2,1)S(1)}, u32[]{:S(2)}, u32[]{:S(2)}) async-start(bf16[8,16,16,128]{3,2,1,0:T(8,128)(2,1)} %get-tuple-element.124), calls=%async_computation.3 | async-start | bytes 1048576 | tf_op jit(solution)/shard_map/all_to_all | solution.py:266
  206.1 16.6 %collective-permute-start.43 = (bf16[136,512]{1,0:T(8,128)(2,1)S(1)}, bf16[136,512]{1,0:T(8,128)(2,1)S(1)}, u32[]{:S(2)}, u32[]{:S(2)}) collective-permute-start(bf16[136,512]{1,0:T(8,128)(2,1)S(1)} %select_convert_fusion), channel_id=1, source_target_pairs={{0,1},{1,0},{2,3},{3,2},{4,5},{5,4},{6,7},{7,6},{8,9},{9,8},{10,11... | collective-permute-start | bytes 417800 | tf_op jit(solution)/shard_map/ppermute | solution.py:220
  222.8 12.0 %collective-permute-start.44 = (bf16[136,512]{1,0:T(8,128)(2,1)S(1)}, bf16[136,512]{1,0:T(8,128)(2,1)}, u32[]{:S(2)}, u32[]{:S(2)}) collective-permute-start(bf16[136,512]{1,0:T(8,128)(2,1)S(1)} %add_convert_fusion.12), channel_id=1, source_target_pairs={{0,2},{2,0},{4,6},{6,4},{8,10},{10,8},{12,14},{14,12},{1,3},{3,1},... | collective-permute-start | bytes 417800 | tf_op jit(solution)/shard_map/ppermute | solution.py:216
  225.9 10.4 %collective-permute-start.48 = (bf16[128,2048]{1,0:T(8,128)(2,1)S(1)}, bf16[128,2048]{1,0:T(8,128)(2,1)S(1)}, u32[]{:S(2)}, u32[]{:S(2)}) collective-permute-start(bf16[128,2048]{1,0:T(8,128)(2,1)S(1)} %fusion.own_ref), channel_id=1, source_target_pairs={{0,1},{1,0},{2,3},{3,2},{4,5},{5,4},{6,7},{7,6},{8,9},{9,8},{10,11... | collective-permute-start | bytes 1572872 | tf_op jit(solution)/shard_map/ppermute | solution.py:220
  228.5 19.5 %collective-permute-start.47 = (bf16[128,2048]{1,0:T(8,128)(2,1)}, bf16[128,2048]{1,0:T(8,128)(2,1)}, u32[]{:S(2)}, u32[]{:S(2)}) collective-permute-start(bf16[128,2048]{1,0:T(8,128)(2,1)} %get-tuple-element.144), channel_id=1, source_target_pairs={{0,2},{2,0},{4,6},{6,4},{8,10},{10,8},{12,14},{14,12},{1,3},{3,1},... | collective-permute-start | bytes 1572872 | tf_op jit(solution)/shard_map/ppermute | solution.py:216
  231.3 16.6 %collective-permute-start.46 = (bf16[128,2048]{1,0:T(8,128)(2,1)}, bf16[128,2048]{1,0:T(8,128)(2,1)}, u32[]{:S(2)}, u32[]{:S(2)}) collective-permute-start(bf16[128,2048]{1,0:T(8,128)(2,1)} %add_convert_fusion.11), channel_id=1, source_target_pairs={{0,4},{2,6},{12,8},{14,10},{1,5},{3,7},{13,9},{15,11},{16,20},{18,... | collective-permute-start | bytes 1572872 | tf_op jit(solution)/shard_map/ppermute | solution.py:216
  235.8 14.9 %collective-permute-start.40 = (bf16[128,2048]{1,0:T(8,128)(2,1)}, bf16[128,2048]{1,0:T(8,128)(2,1)}, u32[]{:S(2)}, u32[]{:S(2)}) collective-permute-start(bf16[128,2048]{1,0:T(8,128)(2,1)} %get-tuple-element.131), channel_id=1, source_target_pairs={{0,1},{1,0},{2,3},{3,2},{4,5},{5,4},{6,7},{7,6},{8,9},{9,8},{10,11... | collective-permute-start | bytes 1572872 | tf_op jit(solution)/shard_map/ppermute | solution.py:220
  235.8 36.8 %collective-permute-start.42 = (bf16[128,2048]{1,0:T(8,128)(2,1)}, bf16[128,2048]{1,0:T(8,128)(2,1)}, u32[]{:S(2)}, u32[]{:S(2)}) collective-permute-start(bf16[128,2048]{1,0:T(8,128)(2,1)} %get-tuple-element.134), channel_id=1, source_target_pairs={{0,2},{2,0},{4,6},{6,4},{8,10},{10,8},{12,14},{14,12},{1,3},{3,1},... | collective-permute-start | bytes 1572872 | tf_op jit(solution)/shard_map/ppermute | solution.py:216
  247.9 12.2 %collective-permute-start.52 = (bf16[128,2048]{1,0:T(8,128)(2,1)}, bf16[128,2048]{1,0:T(8,128)(2,1)S(1)}, u32[]{:S(2)}, u32[]{:S(2)}) collective-permute-start(bf16[128,2048]{1,0:T(8,128)(2,1)} %get-tuple-element.154), channel_id=1, source_target_pairs={{0,1},{1,0},{2,3},{3,2},{4,5},{5,4},{6,7},{7,6},{8,9},{9,8},{10,11... | collective-permute-start | bytes 1572872 | tf_op jit(solution)/shard_map/ppermute | solution.py:220
  248.2 29.7 %collective-permute-start.62 = (bf16[128,2048]{1,0:T(8,128)(2,1)}, bf16[128,2048]{1,0:T(8,128)(2,1)}, u32[]{:S(2)}, u32[]{:S(2)}) collective-permute-start(bf16[128,2048]{1,0:T(8,128)(2,1)} %get-tuple-element.170), channel_id=1, source_target_pairs={{0,1},{1,0},{2,3},{3,2},{4,5},{5,4},{6,7},{7,6},{8,9},{9,8},{10,11... | collective-permute-start | bytes 1572872 | tf_op jit(solution)/shard_map/ppermute | solution.py:220
  248.5 5.7 %collective-permute-start.49 = (bf16[136,512]{1,0:T(8,128)(2,1)S(1)}, bf16[136,512]{1,0:T(8,128)(2,1)S(1)}, u32[]{:S(2)}, u32[]{:S(2)}) collective-permute-start(bf16[136,512]{1,0:T(8,128)(2,1)S(1)} %convert_add_fusion.3), channel_id=1, source_target_pairs={{0,4},{2,6},{4,0},{6,2},{8,12},{10,14},{12,8},{14,10},{1,5},{3,7},... | collective-permute-start | bytes 417800 | tf_op jit(solution)/shard_map/ppermute | solution.py:216
  250.7 21.9 %collective-permute-start.50 = (bf16[128,2048]{1,0:T(8,128)(2,1)}, bf16[128,2048]{1,0:T(8,128)(2,1)}, u32[]{:S(2)}, u32[]{:S(2)}) collective-permute-start(bf16[128,2048]{1,0:T(8,128)(2,1)} %add_convert_fusion.9), channel_id=1, source_target_pairs={{4,8},{6,10},{8,4},{10,6},{5,9},{7,11},{9,5},{11,7},{20,24},{22,26... | collective-permute-start | bytes 1572872 | tf_op jit(solution)/shard_map/ppermute | solution.py:216
  254.3 18.4 %collective-permute-start.51 = (bf16[128,2048]{1,0:T(8,128)(2,1)S(1)}, bf16[128,2048]{1,0:T(8,128)(2,1)}, u32[]{:S(2)}, u32[]{:S(2)}) collective-permute-start(bf16[128,2048]{1,0:T(8,128)(2,1)S(1)} %add_convert_fusion.10), channel_id=1, source_target_pairs={{0,4},{2,6},{12,8},{14,10},{1,5},{3,7},{13,9},{15,11},{16,20},{18,... | collective-permute-start | bytes 1572872 | tf_op jit(solution)/shard_map/ppermute | solution.py:216
  261.2 17.2 %collective-permute-start.57 = (bf16[128,2048]{1,0:T(8,128)(2,1)}, bf16[128,2048]{1,0:T(8,128)(2,1)}, u32[]{:S(2)}, u32[]{:S(2)}) collective-permute-start(bf16[128,2048]{1,0:T(8,128)(2,1)} %get-tuple-element.180), channel_id=1, source_target_pairs={{0,2},{2,0},{4,6},{6,4},{8,10},{10,8},{12,14},{14,12},{1,3},{3,1},... | collective-permute-start | bytes 1572872 | tf_op jit(solution)/shard_map/ppermute | solution.py:216
  273.9 11.2 %collective-permute-start.53 = (bf16[128,2048]{1,0:T(8,128)(2,1)S(1)}, bf16[128,2048]{1,0:T(8,128)(2,1)S(1)}, u32[]{:S(2)}, u32[]{:S(2)}) collective-permute-start(bf16[128,2048]{1,0:T(8,128)(2,1)S(1)} %add_convert_fusion.8), channel_id=1, source_target_pairs={{4,8},{6,10},{8,4},{10,6},{5,9},{7,11},{9,5},{11,7},{20,24},{22,26... | collective-permute-start | bytes 1572872 | tf_op jit(solution)/shard_map/ppermute | solution.py:216
  274.6 52.0 %collective-permute-start.63 = (bf16[128,2048]{1,0:T(8,128)(2,1)}, bf16[128,2048]{1,0:T(8,128)(2,1)S(1)}, u32[]{:S(2)}, u32[]{:S(2)}) collective-permute-start(bf16[128,2048]{1,0:T(8,128)(2,1)} %get-tuple-element.179), channel_id=1, source_target_pairs={{0,2},{2,0},{4,6},{6,4},{8,10},{10,8},{12,14},{14,12},{1,3},{3,1},... | collective-permute-start | bytes 1572872 | tf_op jit(solution)/shard_map/ppermute | solution.py:216
  276.1 6.1 %collective-permute-start.56 = (bf16[128,2048]{1,0:T(8,128)(2,1)}, bf16[128,2048]{1,0:T(8,128)(2,1)S(1)}, u32[]{:S(2)}, u32[]{:S(2)}) collective-permute-start(bf16[128,2048]{1,0:T(8,128)(2,1)} %get-tuple-element.165), channel_id=1, source_target_pairs={{0,1},{1,0},{2,3},{3,2},{4,5},{5,4},{6,7},{7,6},{8,9},{9,8},{10,11... | collective-permute-start | bytes 1572872 | tf_op jit(solution)/shard_map/ppermute | solution.py:220
  277.9 26.4 %collective-permute-start.55 = (bf16[128,2048]{1,0:T(8,128)(2,1)S(1)}, bf16[128,2048]{1,0:T(8,128)(2,1)S(1)}, u32[]{:S(2)}, u32[]{:S(2)}) collective-permute-start(bf16[128,2048]{1,0:T(8,128)(2,1)S(1)} %copy-done.35), channel_id=1, source_target_pairs={{0,1},{1,0},{2,3},{3,2},{4,5},{5,4},{6,7},{7,6},{8,9},{9,8},{10,11... | collective-permute-start | bytes 1572872 | tf_op jit(solution)/shard_map/ppermute | solution.py:220
  278.5 14.6 %collective-permute-start.54 = (bf16[128,2048]{1,0:T(8,128)(2,1)S(1)}, bf16[128,2048]{1,0:T(8,128)(2,1)S(1)}, u32[]{:S(2)}, u32[]{:S(2)}) collective-permute-start(bf16[128,2048]{1,0:T(8,128)(2,1)S(1)} %add_convert_fusion.6), channel_id=1, source_target_pairs={{0,4},{2,6},{4,0},{6,2},{8,12},{10,14},{12,8},{14,10},{1,5},{3,7},... | collective-permute-start | bytes 1572872 | tf_op jit(solution)/shard_map/ppermute | solution.py:216
  282.3 21.2 %collective-permute-start.64 = (bf16[128,2048]{1,0:T(8,128)(2,1)S(1)}, bf16[128,2048]{1,0:T(8,128)(2,1)S(1)}, u32[]{:S(2)}, u32[]{:S(2)}) collective-permute-start(bf16[128,2048]{1,0:T(8,128)(2,1)S(1)} %add_convert_fusion.2), channel_id=1, source_target_pairs={{0,4},{2,6},{12,8},{14,10},{1,5},{3,7},{13,9},{15,11},{16,20},{18,... | collective-permute-start | bytes 1572872 | tf_op jit(solution)/shard_map/ppermute | solution.py:216
  285.1 24.4 %collective-permute-start.58 = (bf16[128,2048]{1,0:T(8,128)(2,1)S(1)}, bf16[128,2048]{1,0:T(8,128)(2,1)S(1)}, u32[]{:S(2)}, u32[]{:S(2)}) collective-permute-start(bf16[128,2048]{1,0:T(8,128)(2,1)S(1)} %get-tuple-element.166), channel_id=1, source_target_pairs={{0,2},{2,0},{4,6},{6,4},{8,10},{10,8},{12,14},{14,12},{1,3},{3,1},... | collective-permute-start | bytes 1572872 | tf_op jit(solution)/shard_map/ppermute | solution.py:216
  293.1 40.5 %collective-permute-start.60 = (bf16[128,2048]{1,0:T(8,128)(2,1)}, bf16[128,2048]{1,0:T(8,128)(2,1)}, u32[]{:S(2)}, u32[]{:S(2)}) collective-permute-start(bf16[128,2048]{1,0:T(8,128)(2,1)} %get-tuple-element.168), channel_id=1, source_target_pairs={{0,2},{2,0},{4,6},{6,4},{8,10},{10,8},{12,14},{14,12},{1,3},{3,1},... | collective-permute-start | bytes 1572872 | tf_op jit(solution)/shard_map/ppermute | solution.py:216
  303.6 23.0 %collective-permute-start.65 = (bf16[128,2048]{1,0:T(8,128)(2,1)S(1)}, bf16[128,2048]{1,0:T(8,128)(2,1)S(1)}, u32[]{:S(2)}, u32[]{:S(2)}) collective-permute-start(bf16[128,2048]{1,0:T(8,128)(2,1)S(1)} %add_convert_fusion.1), channel_id=1, source_target_pairs={{4,8},{6,10},{8,4},{10,6},{5,9},{7,11},{9,5},{11,7},{20,24},{22,26... | collective-permute-start | bytes 1572872 | tf_op jit(solution)/shard_map/ppermute | solution.py:216
  304.3 22.2 %collective-permute-start.67 = (bf16[136,512]{1,0:T(8,128)(2,1)S(1)}, bf16[136,512]{1,0:T(8,128)(2,1)S(1)}, u32[]{:S(2)}, u32[]{:S(2)}) collective-permute-start(bf16[136,512]{1,0:T(8,128)(2,1)S(1)} %convert_add_fusion.2), channel_id=1, source_target_pairs={{0,8},{2,10},{4,12},{6,14},{8,0},{10,2},{12,4},{14,6},{1,9},{3,11}... | collective-permute-start | bytes 417800 | tf_op jit(solution)/shard_map/ppermute | solution.py:216
  309.8 18.0 %collective-permute-start.59 = (bf16[128,2048]{1,0:T(8,128)(2,1)S(1)}, bf16[128,2048]{1,0:T(8,128)(2,1)S(1)}, u32[]{:S(2)}, u32[]{:S(2)}) collective-permute-start(bf16[128,2048]{1,0:T(8,128)(2,1)S(1)} %add_convert_fusion.5), channel_id=1, source_target_pairs={{0,4},{2,6},{12,8},{14,10},{1,5},{3,7},{13,9},{15,11},{16,20},{18,... | collective-permute-start | bytes 1572872 | tf_op jit(solution)/shard_map/ppermute | solution.py:216
  327.8 14.1 %collective-permute-start.66 = (bf16[128,2048]{1,0:T(8,128)(2,1)}, bf16[128,2048]{1,0:T(8,128)(2,1)}, u32[]{:S(2)}, u32[]{:S(2)}) collective-permute-start(bf16[128,2048]{1,0:T(8,128)(2,1)} %add_convert_fusion), channel_id=1, source_target_pairs={{0,4},{2,6},{4,0},{6,2},{8,12},{10,14},{12,8},{14,10},{1,5},{3,7},... | collective-permute-start | bytes 1572872 | tf_op jit(solution)/shard_map/ppermute | solution.py:216
  328.7 13.2 %collective-permute-start.61 = (bf16[128,2048]{1,0:T(8,128)(2,1)}, bf16[128,2048]{1,0:T(8,128)(2,1)}, u32[]{:S(2)}, u32[]{:S(2)}) collective-permute-start(bf16[128,2048]{1,0:T(8,128)(2,1)} %add_convert_fusion.4), channel_id=1, source_target_pairs={{4,8},{6,10},{8,4},{10,6},{5,9},{7,11},{9,5},{11,7},{20,24},{22,26... | collective-permute-start | bytes 1572872 | tf_op jit(solution)/shard_map/ppermute | solution.py:216
  (45 other events, 541.1 us)
where the time goes:
time: 349 us; the launch traced here: 345 us
  waiting for transfers between devices  106 us (30%)
  Pallas kernels  97.2 us (28%)
  starting transfers between devices  87.1 us (25%)
  other arithmetic  39 us (11%)
  local copies, waits for them, and re-layouts  14.1 us (4%)
    ppermute x39, waiting for transfers between devices, step(): return lax.ppermute(value, 'tensor', pairs)  102 us
    ppermute x39, starting transfers between devices, step(): return lax.ppermute(value, 'tensor', pairs)  58 us
    pallas_call x4, Pallas kernels, back_part(): pl.pallas_call(functools.partial(back_kernel, count), grid_spec=pltpu.Pre...  43.2 us
    pallas_call x2, Pallas kernels, forward_rows(): pl.pallas_call(functools.partial(forward_kernel, count), grid_spec=pltpu....  40.5 us
    all_to_all x4, starting transfers between devices, exchange_rows(): lax.all_to_all(value, 'tensor', split_axis=0, concat_axis=0, tiled=True)  22.6 us
    pallas_call x2, Pallas kernels, interact_rows(): pl.pallas_call(interact_kernel, grid=(count // group,), in_specs=[rows, r...  13.5 us
    convert_element_type x10, other arithmetic, add(): return (a.astype(F32) + b.astype(F32)).astype(BF16)  12.8 us
    unnamed x77, local copies, waits for them, and re-layouts  8.73 us
  transfers between devices with their start and end apart: 73, of which 21 were waited for; matrix products, arithmetic and copies ran while one was open for 13% of the time, Pallas kernels for 28%

commit v1 on v0

--- a/solution.py
+++ b/solution.py
@@ -64,7 +64,7 @@
         other_ref[...] = acc_ref[rows:].astype(BF16)
 
 
-def forward_rows(pieces, order, near, cross_w, per=2):
+def forward_rows(pieces, order, near, cross_w, per=1):
     count = len(pieces)
     rows, width = pieces[0][0].shape
     columns = cross_w.shape[1]
@@ -344,49 +344,57 @@
     line_b = linear(pieces, back_a)
     owned_b = to_owner(1, line_b)
     d_linear, other = product(0, back_a)
-    part = back(after(d_linear, line_b), other, (3, 2), owned_b)
+    part = back(after(d_linear, line_b), other, (3, 1), owned_b)
     distant3, close3 = exchange(part, 3)
-    g3, h3 = step(distant3, ACROSS), step(close3, ACROSS)
-    out_b, d_rows_b, *terms_b = interact(after(owned_b, distant3, close3), cotangent[1], *small)
+    distant1, close1 = exchange(part, 1)
+    g3, g1 = step(distant3, ACROSS), step(after(distant1, distant3), ACROSS)
+    out_b, d_rows_b, *terms_b = hold(interact(after(owned_b, distant3, distant1), cotangent[1], *small), g3)
     back_b = exchange_rows(d_rows_b, 8)
-    second = back(after(d_linear, d_rows_b), other, (1, 0), g3, h3)
-    h3_a = h3
-    distant2, close2 = exchange(part, 2)
-    distant1, close1 = exchange(second, 1)
-    b3 = add(distant2, after(g3, distant1))
-    k3 = step(b3, INN)
-    g1, h1 = step(after(distant1, h3), ACROSS), step(after(close1, h3), ACROSS)
-    kept = grid_sum_step(grid_sum_start((terms_a, terms_b)), ACROSS)
+    kept = grid_sum_start((terms_a, terms_b))
+    second = back(after(d_linear, d_rows_b), other, (2, 0), g3, back_b)
+    h3, h1 = step(after(close3, g3), ACROSS), step(after(close1, g3), ACROSS)
+    distant2, close2 = exchange(second, 2)
+    close0, distant0 = roles(second, 0, near)
+    b3 = add(distant2, g3)
+    b2 = add(after(distant0, b3), g1)
+    k3, r2 = step(b3, INN), step(b2, INN)
+    kept = grid_sum_step(after(kept, second[2][0]), PAIR)
     d_next, other = product(1, back_b)
-    part = back(after(d_next, second[1][0]), other, (3, 2), g1, k3, kept)
-    kept, k3, g1_a = hold((kept, k3, g1), part[3][0])
-    close_a, distant0 = roles(second, 0, near)
+    part = back(after(d_next, b3), other, (3, 1), k3, h3, kept)
     distant3, close3 = exchange(part, 3)
-    g3, h3 = step(distant3, ACROSS), step(close3, ACROSS)
-    h1_a = h1
-    b3, b2, e1 = add(b3, k3), add(distant0, g1_a), add(close2, h3_a)
-    k2, r2 = step(b3, MID), step(b2, INN)
-    kept = grid_sum_step(kept, PAIR)
-    second = back(after(d_next, part[3][0], distant3), other, (1, 0), h1, k2, r2, kept)
-    kept, k2, r2 = hold((kept, k2, r2), second[1][0])
-    distant1, close1 = exchange(second, 1)
-    g1, h1 = step(after(distant1, g3), ACROSS), step(after(close1, g3), ACROSS)
-    distant2, close2 = exchange(part, 2)
+    distant1, close1 = exchange(part, 1)
+    g3, g1 = step(after(distant3, h3), ACROSS), step(after(distant1, distant3), ACROSS)
+    k3, kept = hold((k3, kept), distant3, distant1)
+    b3, e1 = add(b3, k3), add(close2, h3)
+    k2 = step(b3, MID)
+    sent = kept.astype(BF16)
+    got = step(sent, CROSS)
+    sum_a = close0.astype(F32) + h1.astype(F32)
+    second = back(after(d_next, distant3, distant1), other, (2, 0), g3, g1, h1, r2, k2)
+    h3, h1 = step(after(close3, g3), ACROSS), step(after(close1, g3), ACROSS)
+    distant2, close2 = exchange(second, 2)
+    close0, distant0 = roles(second, 0, near)
     b3 = add(distant2, g3)
     k3 = step(b3, INN)
-    r0, r1 = step(add(b2, r2), MID), step(add(e1, k2), PAIR)
-    kept = grid_sum_step(after(kept, k3), CROSS)
-    k2 = step(after(add(b3, k3), r0), MID)
-    close0, distant0 = roles(second, 0, near)
-    sum_a = close_a.astype(F32) + h1_a.astype(F32) + r0.astype(F32) + r1.astype(F32)
-    b2 = add(distant0, g1)
+    k2, r2, got = hold((k2, r2, got), b3)
+    sent = (sent.astype(F32) + got.astype(F32)).astype(BF16)
+    got = step(sent, ACROSS)
+    r0_a = step(add(b2, r2), MID)
+    e1 = add(e1, k2)
+    b2 = add(after(distant0, b3), g1)
     r2 = step(b2, INN)
+    b3 = add(b3, k3)
+    k2 = step(b3, MID)
+    r1_a = step(after(e1, b2), PAIR)
     e1 = add(add(close2, h3), k2)
     r1 = step(e1, PAIR)
     r0 = step(add(b2, r2), MID)
-    sums = grid_sum_end(after(kept, r2), terms_a[2].shape)
-    grad_a = finish(0, back_a, line_a, after(sum_a, r2))
+    r0_a, r1_a, got = hold((r0_a, r1_a, got), r2, k2)
+    kept = sent.astype(F32) + got.astype(F32)
+    sum_a = sum_a + r0_a.astype(F32) + r1_a.astype(F32)
+    sums = grid_sum_end(kept, terms_a[2].shape)
     sum_b = close0.astype(F32) + h1.astype(F32) + r0.astype(F32) + r1.astype(F32)
+    grad_a = finish(0, back_a, line_a, sum_a)
     grad_b = finish(1, back_b, line_b, sum_b)
     return (out_a, out_b), sums, (grad_a, grad_b)
 

time: 349 us -> 342 us (0.980)
  waiting for transfers between devices: 106 us -> 99.7 us
    ppermute x39, waiting for transfers between devices: 102 us -> 94.7 us  [step(): return lax.ppermute(value, 'tensor', pairs)]
    unnamed x77 -> x91, local copies, waits for them, and re-layouts: 8.73 us -> 12.8 us
  transfers between devices with their start and end apart: 73 -> 73, of which waited for: 21 -> 22; matrix products, arithmetic and copies ran while one was open for 13% -> 13% of each run, Pallas kernels for 28% -> 28%
where the time goes in v1:
time: 342 us; the launch traced here: 340 us
  waiting for transfers between devices  99.7 us (29%)
  Pallas kernels  95.5 us (28%)
  starting transfers between devices  88.4 us (26%)
  other arithmetic  38.3 us (11%)
  local copies, waits for them, and re-layouts  16.3 us (5%)
    ppermute x39, waiting for transfers between devices, step(): return lax.ppermute(value, 'tensor', pairs)  94.7 us
    ppermute x39, starting transfers between devices, step(): return lax.ppermute(value, 'tensor', pairs)  59.9 us
    pallas_call x4, Pallas kernels, back_part(): pl.pallas_call(functools.partial(back_kernel, count), grid_spec=pltpu.Pre...  43.2 us
    pallas_call x2, Pallas kernels, forward_rows(): pl.pallas_call(functools.partial(forward_kernel, count), grid_spec=pltpu....  38.8 us
    all_to_all x4, starting transfers between devices, exchange_rows(): lax.all_to_all(value, 'tensor', split_axis=0, concat_axis=0, tiled=True)  21.6 us
    pallas_call x2, Pallas kernels, interact_rows(): pl.pallas_call(interact_kernel, grid=(count // group,), in_specs=[rows, r...  13.4 us
    unnamed x91, local copies, waits for them, and re-layouts  12.8 us
    convert_element_type x10, other arithmetic, add(): return (a.astype(F32) + b.astype(F32)).astype(BF16)  12 us
  transfers between devices with their start and end apart: 73, of which 22 were waited for; matrix products, arithmetic and copies ran while one was open for 13% of the time, Pallas kernels for 28%

profile of v1, /device:TPU:0, one launch (start us, length us, event | category | flops | bytes accessed | tf_op | source)
XLA Modules:
  0.0 339.8 jit_solution(3193087243621144939)
XLA Ops:
  0.6 2.1 fusion.11
  3.4 3.0 collective-permute-start.1
  6.5 4.4 %collective-permute-start.2 = (bf16[128,2048]{1,0:T(8,128)(2,1)S(1)}, bf16[128,2048]{1,0:T(8,128)(2,1)S(1)}, u32[]{:S(2)}, u32[]{:S(2)}) collective-permute-start(bf16[128,2048]{1,0:T(8,128)(2,1)S(1)} %bitcast.61), channel_id=1, source_target_pairs={{0,4},{2,6},{4,0},{6,2},{8,12},{10,14},{12,8},{14,10},{1,5},{3,7},... | collective-permute-start | bytes 1572872 | tf_op jit(solution)/shard_map/ppermute | solution.py:216
  10.8 7.6 %collective-permute-done.1.refs_4_ = bf16[128,2048]{1,0:T(8,128)(2,1)S(1)} collective-permute-done((bf16[128,2048]{1,0:T(8,128)(2,1)S(1)}, bf16[128,2048]{1,0:T(8,128)(2,1)S(1)}, u32[]{:S(2)}, u32[]{:S(2)}) %collective-permute-start.1) | collective-permute-done | bytes 524320 | tf_op jit(solution)/shard_map/ppermute | solution.py:216
  18.4 3.8 %collective-permute-done.2.refs_8_ = bf16[128,2048]{1,0:T(8,128)(2,1)S(1)} collective-permute-done((bf16[128,2048]{1,0:T(8,128)(2,1)S(1)}, bf16[128,2048]{1,0:T(8,128)(2,1)S(1)}, u32[]{:S(2)}, u32[]{:S(2)}) %collective-permute-start.2) | collective-permute-done | bytes 524320 | tf_op jit(solution)/shard_map/ppermute | solution.py:216
  24.1 1.5 collective-permute-start.7
  25.5 11.0 %collective-permute-done.3 = bf16[128,2048]{1,0:T(8,128)(2,1)S(1)} collective-permute-done((bf16[128,2048]{1,0:T(8,128)(2,1)S(1)}, bf16[128,2048]{1,0:T(8,128)(2,1)S(1)}, u32[]{:S(2)}, u32[]{:S(2)}) %collective-permute-start.3) | collective-permute-done | bytes 524320 | tf_op jit(solution)/shard_map/ppermute | solution.py:216
  40.8 10.5 %collective-permute-done.11 = bf16[128,2048]{1,0:T(8,128)(2,1)S(1)} collective-permute-done((bf16[128,2048]{1,0:T(8,128)(2,1)}, bf16[128,2048]{1,0:T(8,128)(2,1)S(1)}, u32[]{:S(2)}, u32[]{:S(2)}) %collective-permute-start.11) | collective-permute-done | bytes 524320 | tf_op jit(solution)/shard_map/ppermute | solution.py:216
  53.0 2.7 collective-permute-start.17
  57.0 5.7 %collective-permute-done.14.refs_13_ = bf16[128,2048]{1,0:T(8,128)(2,1)} collective-permute-done((bf16[128,2048]{1,0:T(8,128)(2,1)S(1)}, bf16[128,2048]{1,0:T(8,128)(2,1)}, u32[]{:S(2)}, u32[]{:S(2)}) %collective-permute-start.14) | collective-permute-done | bytes 524320 | tf_op jit(solution)/shard_map/ppermute | solution.py:216
  66.1 1.5 collective-permute-start.21
  67.6 1.3 collective-permute-start.18
  69.0 1.3 collective-permute-start.22
  70.3 19.4 %forward_rows.2 = (f32[128,2048]{1,0:T(8,128)}, bf16[128,2048]{1,0:T(8,128)(2,1)}) custom-call(s32[5]{0:T(128)} %stack.49.plan_ref, bf16[128,2048]{1,0:T(8,128)(2,1)} %bitcast.63, bf16[128,2048]{1,0:T(8,128)(2,1)} %copy-done.7, bf16[128,2048]{1,0:T(8,128)(2,1)} %copy-done.22, bf16[128,2048]{1,0:T(8,128)(2,1)} %collective-permute-done.5.refs_3_, ...), custom_call_target="tpu_custom_call" | custom-call | flops 8589934592 | bytes 33554432 | tf_op jit(solution)/shard_map/forward_rows/pallas_call | solution.py:73
  90.9 1.4 collective-permute-start.25
  94.8 6.8 %all-to-all-start = ((bf16[8,16,16,128]{3,2,1,0:T(8,128)(2,1)}), bf16[8,16,16,128]{3,2,1,0:T(8,128)(2,1)}, u32[]{:S(2)}, u32[]{:S(2)}) async-start(bf16[8,16,16,128]{3,2,1,0:T(8,128)(2,1)} %bitcast.16), calls=%async_computation | async-start | bytes 1048576 | tf_op jit(solution)/shard_map/all_to_all | solution.py:265
  101.6 2.0 collective-permute-start.24
  104.1 8.0 %collective-permute-done.25 = bf16[128,2048]{1,0:T(8,128)(2,1)} collective-permute-done((bf16[128,2048]{1,0:T(8,128)(2,1)}, bf16[128,2048]{1,0:T(8,128)(2,1)}, u32[]{:S(2)}, u32[]{:S(2)}) %collective-permute-start.25) | collective-permute-done | bytes 524320 | tf_op jit(solution)/shard_map/ppermute | solution.py:216
  113.2 8.1 %collective-permute-done.24.refs_5_ = bf16[128,2048]{1,0:T(8,128)(2,1)S(1)} collective-permute-done((bf16[128,2048]{1,0:T(8,128)(2,1)S(1)}, bf16[128,2048]{1,0:T(8,128)(2,1)S(1)}, u32[]{:S(2)}, u32[]{:S(2)}) %collective-permute-start.24) | collective-permute-done | bytes 524320 | tf_op jit(solution)/shard_map/ppermute | solution.py:216
  124.8 6.7 %interact_rows.2 = (bf16[16,128,128]{2,1,0:T(8,128)(2,1)}, bf16[8,16,16,128]{3,2,1,0:T(8,128)(2,1)}, f32[128,512]{1,0:T(8,128)}, f32[8,512]{1,0:T(8,128)}, f32[512,128]{1,0:T(8,128)}) custom-call(bf16[8,16,16,128]{3,2,1,0:T(8,128)(2,1)} %all-to-all-done.x_ref, bf16[16,128,128]{2,1,0:T(8,128)(2,1)} %bitcast.76, bf16[128,512]{1,0:T(8,128)(2,1)} %mix_ref.3, ...), custom_call_target="tpu_custom_call" | custom-call | flops 1744830464 | bytes 2097152 | tf_op jit(solution)/shard_map/interact_rows/pallas_call | solution.py:194
  132.1 2.3 collective-permute-done.32.refs_13_
  135.0 5.2 %all-to-all-start.1 = ((bf16[8,16,16,128]{3,2,1,0:T(8,128)(2,1)}), bf16[8,16,16,128]{3,2,1,0:T(8,128)(2,1)S(1)}, u32[]{:S(2)}, u32[]{:S(2)}) async-start(bf16[8,16,16,128]{3,2,1,0:T(8,128)(2,1)} %get-tuple-element.117), calls=%async_computation.1 | async-start | bytes 1048576 | tf_op jit(solution)/shard_map/all_to_all | solution.py:266
  140.2 19.4 %forward_rows.3 = (f32[128,2048]{1,0:T(8,128)}, bf16[128,2048]{1,0:T(8,128)(2,1)}) custom-call(s32[5]{0:T(128)} %stack.49.plan_ref, bf16[128,2048]{1,0:T(8,128)(2,1)} %bitcast.7.refs_0_, bf16[128,2048]{1,0:T(8,128)(2,1)} %copy-done.9, bf16[128,2048]{1,0:T(8,128)(2,1)} %collective-permute-done.26.refs_2_, bf16[128,2048]{1,0:T(8,128)(2,1)} %collective-permute-done.27.refs_3_, ...), custom_call_target="tpu_custom_call" | custom-call | flops 8589934592 | bytes 33554432 | tf_op jit(solution)/shard_map/forward_rows/pallas_call | solution.py:73
  160.5 1.5 collective-permute-done.35
  162.0 2.5 fusion.8
  165.3 6.0 %all-to-all-start.2 = ((bf16[8,16,16,128]{3,2,1,0:T(8,128)(2,1)}), bf16[8,16,16,128]{3,2,1,0:T(8,128)(2,1)}, u32[]{:S(2)}, u32[]{:S(2)}) async-start(bf16[8,16,16,128]{3,2,1,0:T(8,128)(2,1)} %bitcast.27), calls=%async_computation.2 | async-start | bytes 1048576 | tf_op jit(solution)/shard_map/all_to_all | solution.py:265
  172.7 10.8 %back_part.4 = (bf16[128,2048]{1,0:T(8,128)(2,1)}, bf16[128,2048]{1,0:T(8,128)(2,1)}, bf16[128,2048]{1,0:T(8,128)(2,1)}, bf16[128,2048]{1,0:T(8,128)(2,1)}) custom-call(s32[2]{0:T(128)} %pad_add_fusion.plan_ref, bf16[128,2048]{1,0:T(8,128)(2,1)} %copy-done.2, bf16[128,2048]{1,0:T(8,128)(2,1)} %copy-done.5, bf16[8192,2048]{1,0:T(8,128)(2,1)} %w_ref.7), custom_call_target="tpu_custom_call" | custom-call | flops 4294967296 | bytes 16777216 | tf_op jit(solution)/shard_map/back_part/pallas_call | solution.py:127
  183.5 2.7 all-to-all-done.2.x_ref
  188.3 1.9 broadcast_select_fusion.5
  190.3 1.5 collective-permute-start.39
  192.8 6.7 %interact_rows.3 = (bf16[16,128,128]{2,1,0:T(8,128)(2,1)}, bf16[8,16,16,128]{3,2,1,0:T(8,128)(2,1)}, f32[128,512]{1,0:T(8,128)}, f32[8,512]{1,0:T(8,128)}, f32[512,128]{1,0:T(8,128)}) custom-call(bf16[8,16,16,128]{3,2,1,0:T(8,128)(2,1)} %all-to-all-done.2.x_ref, bf16[16,128,128]{2,1,0:T(8,128)(2,1)} %bitcast.75, bf16[128,512]{1,0:T(8,128)(2,1)} %mix_ref.3, ...), custom_call_target="tpu_custom_call" | custom-call | flops 1744830464 | bytes 2097152 | tf_op jit(solution)/shard_map/interact_rows/pallas_call | solution.py:194
  199.5 2.2 copy.32
  202.5 1.7 collective-permute-done.39
  205.1 3.6 %all-to-all-start.3 = ((bf16[8,16,16,128]{3,2,1,0:T(8,128)(2,1)}), bf16[8,16,16,128]{3,2,1,0:T(8,128)(2,1)S(1)}, u32[]{:S(2)}, u32[]{:S(2)}) async-start(bf16[8,16,16,128]{3,2,1,0:T(8,128)(2,1)} %get-tuple-element.140), calls=%async_computation.3 | async-start | bytes 1048576 | tf_op jit(solution)/shard_map/all_to_all | solution.py:266
  209.3 2.1 collective-permute-start.43
  212.6 10.8 %back_part.5 = (bf16[128,2048]{1,0:T(8,128)(2,1)}, bf16[128,2048]{1,0:T(8,128)(2,1)}, bf16[128,2048]{1,0:T(8,128)(2,1)}, bf16[128,2048]{1,0:T(8,128)(2,1)}) custom-call(s32[2]{0:T(128)} %pad_add_fusion.1.plan_ref, bf16[128,2048]{1,0:T(8,128)(2,1)} %copy-done.2, bf16[128,2048]{1,0:T(8,128)(2,1)} %copy-done.5, bf16[8192,2048]{1,0:T(8,128)(2,1)} %w_ref.7), custom_call_target="tpu_custom_call" | custom-call | flops 4294967296 | bytes 16777216 | tf_op jit(solution)/shard_map/back_part/pallas_call | solution.py:127
  224.1 2.0 collective-permute-start.46
  227.6 2.2 add_convert_fusion.11
  231.1 4.5 %collective-permute-start.44 = (bf16[128,2048]{1,0:T(8,128)(2,1)}, bf16[128,2048]{1,0:T(8,128)(2,1)}, u32[]{:S(2)}, u32[]{:S(2)}) collective-permute-start(bf16[128,2048]{1,0:T(8,128)(2,1)} %add_convert_fusion.11), channel_id=1, source_target_pairs={{0,4},{2,6},{12,8},{14,10},{1,5},{3,7},{13,9},{15,11},{16,20},{18,... | collective-permute-start | bytes 1572872 | tf_op jit(solution)/shard_map/ppermute | solution.py:216
  236.5 1.5 collective-permute-start.41
  238.0 10.8 %back_part.6 = (bf16[128,2048]{1,0:T(8,128)(2,1)}, bf16[128,2048]{1,0:T(8,128)(2,1)}, bf16[128,2048]{1,0:T(8,128)(2,1)}, bf16[128,2048]{1,0:T(8,128)(2,1)}) custom-call(s32[2]{0:T(128)} %pad_add_fusion.plan_ref, bf16[128,2048]{1,0:T(8,128)(2,1)} %copy-done.3, bf16[128,2048]{1,0:T(8,128)(2,1)} %copy-done.6, bf16[8192,2048]{1,0:T(8,128)(2,1)} %w_ref.7), custom_call_target="tpu_custom_call" | custom-call | flops 4294967296 | bytes 16777216 | tf_op jit(solution)/shard_map/back_part/pallas_call | solution.py:127
  251.8 1.6 collective-permute-start.52
  254.6 1.5 collective-permute-start.54
  257.7 2.1 add_convert_fusion.9
  259.8 1.5 collective-permute-start.51
  262.4 10.8 %back_part.7 = (bf16[128,2048]{1,0:T(8,128)(2,1)}, bf16[128,2048]{1,0:T(8,128)(2,1)}, bf16[128,2048]{1,0:T(8,128)(2,1)}, bf16[128,2048]{1,0:T(8,128)(2,1)}) custom-call(s32[2]{0:T(128)} %pad_add_fusion.1.plan_ref, bf16[128,2048]{1,0:T(8,128)(2,1)} %copy-done.3, bf16[128,2048]{1,0:T(8,128)(2,1)} %copy-done.6, bf16[8192,2048]{1,0:T(8,128)(2,1)} %w_ref.7), custom_call_target="tpu_custom_call" | custom-call | flops 4294967296 | bytes 16777216 | tf_op jit(solution)/shard_map/back_part/pallas_call | solution.py:127
  273.3 6.4 %collective-permute-done.55 = bf16[128,2048]{1,0:T(8,128)(2,1)} collective-permute-done((bf16[128,2048]{1,0:T(8,128)(2,1)}, bf16[128,2048]{1,0:T(8,128)(2,1)}, u32[]{:S(2)}, u32[]{:S(2)}) %collective-permute-start.55) | collective-permute-done | bytes 524320 | tf_op jit(solution)/shard_map/ppermute | solution.py:216
  280.3 2.3 maximum_bitcast_fusion
  283.1 1.5 collective-permute-start.66
  285.1 1.3 add_convert_fusion.8
  286.4 4.5 %collective-permute-start.62 = (bf16[128,2048]{1,0:T(8,128)(2,1)S(1)}, bf16[128,2048]{1,0:T(8,128)(2,1)S(1)}, u32[]{:S(2)}, u32[]{:S(2)}) collective-permute-start(bf16[128,2048]{1,0:T(8,128)(2,1)S(1)} %add_convert_fusion.8), channel_id=1, source_target_pairs={{0,4},{2,6},{12,8},{14,10},{1,5},{3,7},{13,9},{15,11},{16,20},{18,... | collective-permute-start | bytes 1572872 | tf_op jit(solution)/shard_map/ppermute | solution.py:216
  291.0 1.3 add_convert_fusion.4
  292.3 1.3 collective-permute-start.61
  294.5 1.5 add_convert_fusion.5
  296.1 7.2 %collective-permute-done.62 = bf16[128,2048]{1,0:T(8,128)(2,1)S(1)} collective-permute-done((bf16[128,2048]{1,0:T(8,128)(2,1)S(1)}, bf16[128,2048]{1,0:T(8,128)(2,1)S(1)}, u32[]{:S(2)}, u32[]{:S(2)}) %collective-permute-start.62) | collective-permute-done | bytes 524320 | tf_op jit(solution)/shard_map/ppermute | solution.py:216
  304.1 8.5 %collective-permute-done.61 = bf16[128,2048]{1,0:T(8,128)(2,1)S(1)} collective-permute-done((bf16[128,2048]{1,0:T(8,128)(2,1)S(1)}, bf16[128,2048]{1,0:T(8,128)(2,1)S(1)}, u32[]{:S(2)}, u32[]{:S(2)}) %collective-permute-start.61) | collective-permute-done | bytes 524320 | tf_op jit(solution)/shard_map/ppermute | solution.py:216
  312.6 2.5 collective-permute-start.59
  316.0 1.5 collective-permute-start.60
  317.5 1.4 collective-permute-start.65
  321.1 1.8 collective-permute-start.67
  322.9 5.1 %collective-permute-done.59 = bf16[128,2048]{1,0:T(8,128)(2,1)S(1)} collective-permute-done((bf16[128,2048]{1,0:T(8,128)(2,1)S(1)}, bf16[128,2048]{1,0:T(8,128)(2,1)S(1)}, u32[]{:S(2)}, u32[]{:S(2)}) %collective-permute-start.59) | collective-permute-done | bytes 524320 | tf_op jit(solution)/shard_map/ppermute | solution.py:216
  328.1 1.7 fusion.2
  331.9 4.9 %collective-permute-done.67 = bf16[128,2048]{1,0:T(8,128)(2,1)} collective-permute-done((bf16[128,2048]{1,0:T(8,128)(2,1)}, bf16[128,2048]{1,0:T(8,128)(2,1)}, u32[]{:S(2)}, u32[]{:S(2)}) %collective-permute-start.67) | collective-permute-done | bytes 524320 | tf_op jit(solution)/shard_map/ppermute | solution.py:216
  336.8 2.0 fusion.5
  (231 shorter events, 53.4 us)
Async XLA Ops:
  2.7 8.1 %collective-permute-start = (bf16[128,2048]{1,0:T(8,128)(2,1)S(1)}, bf16[128,2048]{1,0:T(8,128)(2,1)S(1)}, u32[]{:S(2)}, u32[]{:S(2)}) collective-permute-start(bf16[128,2048]{1,0:T(8,128)(2,1)S(1)} %bitcast.59), channel_id=1, source_target_pairs={{4,8},{6,10},{8,4},{10,6},{5,9},{7,11},{9,5},{11,7},{20,24},{22,26... | collective-permute-start | bytes 1572872 | tf_op jit(solution)/shard_map/ppermute | solution.py:216
  3.4 15.0 %collective-permute-start.1 = (bf16[128,2048]{1,0:T(8,128)(2,1)S(1)}, bf16[128,2048]{1,0:T(8,128)(2,1)S(1)}, u32[]{:S(2)}, u32[]{:S(2)}) collective-permute-start(bf16[128,2048]{1,0:T(8,128)(2,1)S(1)} %bitcast.60), channel_id=1, source_target_pairs={{0,2},{2,0},{4,6},{6,4},{8,10},{10,8},{12,14},{14,12},{1,3},{3,1},... | collective-permute-start | bytes 1572872 | tf_op jit(solution)/shard_map/ppermute | solution.py:216
  6.5 15.7 %collective-permute-start.2 = (bf16[128,2048]{1,0:T(8,128)(2,1)S(1)}, bf16[128,2048]{1,0:T(8,128)(2,1)S(1)}, u32[]{:S(2)}, u32[]{:S(2)}) collective-permute-start(bf16[128,2048]{1,0:T(8,128)(2,1)S(1)} %bitcast.61), channel_id=1, source_target_pairs={{0,4},{2,6},{4,0},{6,2},{8,12},{10,14},{12,8},{14,10},{1,5},{3,7},... | collective-permute-start | bytes 1572872 | tf_op jit(solution)/shard_map/ppermute | solution.py:216
  22.2 14.4 %collective-permute-start.3 = (bf16[128,2048]{1,0:T(8,128)(2,1)S(1)}, bf16[128,2048]{1,0:T(8,128)(2,1)S(1)}, u32[]{:S(2)}, u32[]{:S(2)}) collective-permute-start(bf16[128,2048]{1,0:T(8,128)(2,1)S(1)} %collective-permute-done), channel_id=1, source_target_pairs={{4,0},{6,2},{8,12},{10,14},{5,1},{7,3},{9,13},{11,15},{20,16},{22,... | collective-permute-start | bytes 1572872 | tf_op jit(solution)/shard_map/ppermute | solution.py:216
  23.5 13.1 %collective-permute-start.6 = (bf16[128,2048]{1,0:T(8,128)(2,1)S(1)}, bf16[128,2048]{1,0:T(8,128)(2,1)S(1)}, u32[]{:S(2)}, u32[]{:S(2)}) collective-permute-start(bf16[128,2048]{1,0:T(8,128)(2,1)S(1)} %collective-permute-done.2.refs_8_), channel_id=1, source_target_pairs={{0,2},{2,0},{4,6},{6,4},{8,10},{10,8},{12,14},{14,12},{1,3},{3,1},... | collective-permute-start | bytes 1572872 | tf_op jit(solution)/shard_map/ppermute | solution.py:216
  24.1 12.5 %collective-permute-start.7 = (bf16[128,2048]{1,0:T(8,128)(2,1)S(1)}, bf16[128,2048]{1,0:T(8,128)(2,1)}, u32[]{:S(2)}, u32[]{:S(2)}) collective-permute-start(bf16[128,2048]{1,0:T(8,128)(2,1)S(1)} %collective-permute-done.2.refs_8_), channel_id=1, source_target_pairs={{4,8},{6,10},{8,4},{10,6},{5,9},{7,11},{9,5},{11,7},{20,24},{22,26... | collective-permute-start | bytes 1572872 | tf_op jit(solution)/shard_map/ppermute | solution.py:216
  37.3 14.0 %collective-permute-start.11 = (bf16[128,2048]{1,0:T(8,128)(2,1)}, bf16[128,2048]{1,0:T(8,128)(2,1)S(1)}, u32[]{:S(2)}, u32[]{:S(2)}) collective-permute-start(bf16[128,2048]{1,0:T(8,128)(2,1)} %collective-permute-done.7), channel_id=1, source_target_pairs={{4,0},{6,2},{8,12},{10,14},{5,1},{7,3},{9,13},{11,15},{20,16},{22,... | collective-permute-start | bytes 1572872 | tf_op jit(solution)/shard_map/ppermute | solution.py:216
  39.8 12.2 %collective-permute-start.8 = (bf16[128,2048]{1,0:T(8,128)(2,1)S(1)}, bf16[128,2048]{1,0:T(8,128)(2,1)}, u32[]{:S(2)}, u32[]{:S(2)}) collective-permute-start(bf16[128,2048]{1,0:T(8,128)(2,1)S(1)} %broadcast_select_fusion.13.refs_1_), channel_id=1, source_target_pairs={{0,2},{2,0},{4,6},{6,4},{8,10},{10,8},{12,14},{14,12},{1,3},{3,1},... | collective-permute-start | bytes 1572872 | tf_op jit(solution)/shard_map/ppermute | solution.py:216
  40.3 15.4 %collective-permute-start.4 = (bf16[128,2048]{1,0:T(8,128)(2,1)S(1)}, bf16[128,2048]{1,0:T(8,128)(2,1)S(1)}, u32[]{:S(2)}, u32[]{:S(2)}) collective-permute-start(bf16[128,2048]{1,0:T(8,128)(2,1)S(1)} %bitcast.62), channel_id=1, source_target_pairs={{0,1},{1,0},{2,3},{3,2},{4,5},{5,4},{6,7},{7,6},{8,9},{9,8},{10,11... | collective-permute-start | bytes 1572872 | tf_op jit(solution)/shard_map/ppermute | solution.py:220
  40.3 16.1 %collective-permute-start.9 = (bf16[128,2048]{1,0:T(8,128)(2,1)S(1)}, bf16[128,2048]{1,0:T(8,128)(2,1)S(1)}, u32[]{:S(2)}, u32[]{:S(2)}) collective-permute-start(bf16[128,2048]{1,0:T(8,128)(2,1)S(1)} %collective-permute-done.1.refs_4_), channel_id=1, source_target_pairs={{0,1},{1,0},{2,3},{3,2},{4,5},{5,4},{6,7},{7,6},{8,9},{9,8},{10,11... | collective-permute-start | bytes 1572872 | tf_op jit(solution)/shard_map/ppermute | solution.py:220
  40.8 15.7 %collective-permute-start.12 = (bf16[128,2048]{1,0:T(8,128)(2,1)S(1)}, bf16[128,2048]{1,0:T(8,128)(2,1)S(1)}, u32[]{:S(2)}, u32[]{:S(2)}) collective-permute-start(bf16[128,2048]{1,0:T(8,128)(2,1)S(1)} %collective-permute-done.2.refs_8_), channel_id=1, source_target_pairs={{0,1},{1,0},{2,3},{3,2},{4,5},{5,4},{6,7},{7,6},{8,9},{9,8},{10,11... | collective-permute-start | bytes 1572872 | tf_op jit(solution)/shard_map/ppermute | solution.py:220
  51.9 10.8 %collective-permute-start.14 = (bf16[128,2048]{1,0:T(8,128)(2,1)S(1)}, bf16[128,2048]{1,0:T(8,128)(2,1)}, u32[]{:S(2)}, u32[]{:S(2)}) collective-permute-start(bf16[128,2048]{1,0:T(8,128)(2,1)S(1)} %broadcast_select_fusion.12.refs_9_), channel_id=1, source_target_pairs={{0,2},{2,0},{4,6},{6,4},{8,10},{10,8},{12,14},{14,12},{1,3},{3,1},... | collective-permute-start | bytes 1572872 | tf_op jit(solution)/shard_map/ppermute | solution.py:216
  53.0 10.5 %collective-permute-start.17 = (bf16[128,2048]{1,0:T(8,128)(2,1)}, bf16[128,2048]{1,0:T(8,128)(2,1)}, u32[]{:S(2)}, u32[]{:S(2)}) collective-permute-start(bf16[128,2048]{1,0:T(8,128)(2,1)} %bitcast.7.refs_0_), channel_id=1, source_target_pairs={{0,4},{2,6},{4,0},{6,2},{8,12},{10,14},{12,8},{14,10},{1,5},{3,7},... | collective-permute-start | bytes 1572872 | tf_op jit(solution)/shard_map/ppermute | solution.py:216
  55.7 7.8 %collective-permute-start.19 = (bf16[128,2048]{1,0:T(8,128)(2,1)}, bf16[128,2048]{1,0:T(8,128)(2,1)S(1)}, u32[]{:S(2)}, u32[]{:S(2)}) collective-permute-start(bf16[128,2048]{1,0:T(8,128)(2,1)} %bitcast.7.refs_0_), channel_id=1, source_target_pairs={{4,8},{6,10},{8,4},{10,6},{5,9},{7,11},{9,5},{11,7},{20,24},{22,26... | collective-permute-start | bytes 1572872 | tf_op jit(solution)/shard_map/ppermute | solution.py:216
  56.4 9.0 %collective-permute-start.5 = (bf16[128,2048]{1,0:T(8,128)(2,1)S(1)}, bf16[128,2048]{1,0:T(8,128)(2,1)}, u32[]{:S(2)}, u32[]{:S(2)}) collective-permute-start(bf16[128,2048]{1,0:T(8,128)(2,1)S(1)} %broadcast_select_fusion.13.refs_1_), channel_id=1, source_target_pairs={{0,1},{1,0},{2,3},{3,2},{4,5},{5,4},{6,7},{7,6},{8,9},{9,8},{10,11... | collective-permute-start | bytes 1572872 | tf_op jit(solution)/shard_map/ppermute | solution.py:220
  56.5 9.6 %collective-permute-start.15 = (bf16[128,2048]{1,0:T(8,128)(2,1)S(1)}, bf16[128,2048]{1,0:T(8,128)(2,1)}, u32[]{:S(2)}, u32[]{:S(2)}) collective-permute-start(bf16[128,2048]{1,0:T(8,128)(2,1)S(1)} %collective-permute-done.6.refs_12_), channel_id=1, source_target_pairs={{0,1},{1,0},{2,3},{3,2},{4,5},{5,4},{6,7},{7,6},{8,9},{9,8},{10,11... | collective-permute-start | bytes 1572872 | tf_op jit(solution)/shard_map/ppermute | solution.py:220
  63.5 5.4 %collective-permute-start.13 = (bf16[128,2048]{1,0:T(8,128)(2,1)S(1)}, bf16[128,2048]{1,0:T(8,128)(2,1)}, u32[]{:S(2)}, u32[]{:S(2)}) collective-permute-start(bf16[128,2048]{1,0:T(8,128)(2,1)S(1)} %broadcast_select_fusion.12.refs_9_), channel_id=1, source_target_pairs={{0,1},{1,0},{2,3},{3,2},{4,5},{5,4},{6,7},{7,6},{8,9},{9,8},{10,11... | collective-permute-start | bytes 1572872 | tf_op jit(solution)/shard_map/ppermute | solution.py:220
  64.3 5.9 %collective-permute-start.16 = (bf16[128,2048]{1,0:T(8,128)(2,1)}, bf16[128,2048]{1,0:T(8,128)(2,1)}, u32[]{:S(2)}, u32[]{:S(2)}) collective-permute-start(bf16[128,2048]{1,0:T(8,128)(2,1)} %collective-permute-done.14.refs_13_), channel_id=1, source_target_pairs={{0,1},{1,0},{2,3},{3,2},{4,5},{5,4},{6,7},{7,6},{8,9},{9,8},{10,11... | collective-permute-start | bytes 1572872 | tf_op jit(solution)/shard_map/ppermute | solution.py:220
  65.4 25.4 %collective-permute-start.20 = (bf16[128,2048]{1,0:T(8,128)(2,1)}, bf16[128,2048]{1,0:T(8,128)(2,1)}, u32[]{:S(2)}, u32[]{:S(2)}) collective-permute-start(bf16[128,2048]{1,0:T(8,128)(2,1)} %collective-permute-done.17.refs_8_), channel_id=1, source_target_pairs={{0,2},{2,0},{4,6},{6,4},{8,10},{10,8},{12,14},{14,12},{1,3},{3,1},... | collective-permute-start | bytes 1572872 | tf_op jit(solution)/shard_map/ppermute | solution.py:216
  66.1 24.7 %collective-permute-start.21 = (bf16[128,2048]{1,0:T(8,128)(2,1)}, bf16[128,2048]{1,0:T(8,128)(2,1)}, u32[]{:S(2)}, u32[]{:S(2)}) collective-permute-start(bf16[128,2048]{1,0:T(8,128)(2,1)} %collective-permute-done.17.refs_8_), channel_id=1, source_target_pairs={{4,8},{6,10},{8,4},{10,6},{5,9},{7,11},{9,5},{11,7},{20,24},{22,26... | collective-permute-start | bytes 1572872 | tf_op jit(solution)/shard_map/ppermute | solution.py:216
  67.6 23.2 %collective-permute-start.18 = (bf16[128,2048]{1,0:T(8,128)(2,1)}, bf16[128,2048]{1,0:T(8,128)(2,1)}, u32[]{:S(2)}, u32[]{:S(2)}) collective-permute-start(bf16[128,2048]{1,0:T(8,128)(2,1)} %bitcast.7.refs_0_), channel_id=1, source_target_pairs={{0,2},{2,0},{4,6},{6,4},{8,10},{10,8},{12,14},{14,12},{1,3},{3,1},... | collective-permute-start | bytes 1572872 | tf_op jit(solution)/shard_map/ppermute | solution.py:216
  69.0 21.9 %collective-permute-start.22 = (bf16[128,2048]{1,0:T(8,128)(2,1)}, bf16[128,2048]{1,0:T(8,128)(2,1)}, u32[]{:S(2)}, u32[]{:S(2)}) collective-permute-start(bf16[128,2048]{1,0:T(8,128)(2,1)} %copy-done.34), channel_id=1, source_target_pairs={{4,0},{6,2},{8,12},{10,14},{5,1},{7,3},{9,13},{11,15},{20,16},{22,... | collective-permute-start | bytes 1572872 | tf_op jit(solution)/shard_map/ppermute | solution.py:216
  90.9 21.2 %collective-permute-start.25 = (bf16[128,2048]{1,0:T(8,128)(2,1)}, bf16[128,2048]{1,0:T(8,128)(2,1)}, u32[]{:S(2)}, u32[]{:S(2)}) collective-permute-start(bf16[128,2048]{1,0:T(8,128)(2,1)} %collective-permute-done.21), channel_id=1, source_target_pairs={{4,0},{6,2},{8,12},{10,14},{5,1},{7,3},{9,13},{11,15},{20,16},{22,... | collective-permute-start | bytes 1572872 | tf_op jit(solution)/shard_map/ppermute | solution.py:216
  94.8 30.0 %all-to-all-start = ((bf16[8,16,16,128]{3,2,1,0:T(8,128)(2,1)}), bf16[8,16,16,128]{3,2,1,0:T(8,128)(2,1)}, u32[]{:S(2)}, u32[]{:S(2)}) async-start(bf16[8,16,16,128]{3,2,1,0:T(8,128)(2,1)} %bitcast.16), calls=%async_computation | async-start | bytes 1048576 | tf_op jit(solution)/shard_map/all_to_all | solution.py:265
  101.6 19.7 %collective-permute-start.24 = (bf16[128,2048]{1,0:T(8,128)(2,1)S(1)}, bf16[128,2048]{1,0:T(8,128)(2,1)S(1)}, u32[]{:S(2)}, u32[]{:S(2)}) collective-permute-start(bf16[128,2048]{1,0:T(8,128)(2,1)S(1)} %broadcast_select_fusion.11.refs_1_), channel_id=1, source_target_pairs={{0,2},{2,0},{4,6},{6,4},{8,10},{10,8},{12,14},{14,12},{1,3},{3,1},... | collective-permute-start | bytes 1572872 | tf_op jit(solution)/shard_map/ppermute | solution.py:216
  103.6 27.9 %collective-permute-start.30 = (bf16[128,2048]{1,0:T(8,128)(2,1)}, bf16[128,2048]{1,0:T(8,128)(2,1)}, u32[]{:S(2)}, u32[]{:S(2)}) collective-permute-start(bf16[128,2048]{1,0:T(8,128)(2,1)} %collective-permute-done.17.refs_8_), channel_id=1, source_target_pairs={{0,1},{1,0},{2,3},{3,2},{4,5},{5,4},{6,7},{7,6},{8,9},{9,8},{10,11... | collective-permute-start | bytes 1572872 | tf_op jit(solution)/shard_map/ppermute | solution.py:220
  103.6 28.0 %collective-permute-start.27 = (bf16[128,2048]{1,0:T(8,128)(2,1)S(1)}, bf16[128,2048]{1,0:T(8,128)(2,1)}, u32[]{:S(2)}, u32[]{:S(2)}) collective-permute-start(bf16[128,2048]{1,0:T(8,128)(2,1)S(1)} %broadcast_select_fusion.11.refs_1_), channel_id=1, source_target_pairs={{0,1},{1,0},{2,3},{3,2},{4,5},{5,4},{6,7},{7,6},{8,9},{9,8},{10,11... | collective-permute-start | bytes 1572872 | tf_op jit(solution)/shard_map/ppermute | solution.py:220
  121.3 13.2 %collective-permute-start.32 = (bf16[128,2048]{1,0:T(8,128)(2,1)S(1)}, bf16[128,2048]{1,0:T(8,128)(2,1)}, u32[]{:S(2)}, u32[]{:S(2)}) collective-permute-start(bf16[128,2048]{1,0:T(8,128)(2,1)S(1)} %broadcast_select_fusion.10.refs_9_), channel_id=1, source_target_pairs={{0,2},{2,0},{4,6},{6,4},{8,10},{10,8},{12,14},{14,12},{1,3},{3,1},... | collective-permute-start | bytes 1572872 | tf_op jit(solution)/shard_map/ppermute | solution.py:216
  122.1 12.4 %collective-permute-start.28 = (bf16[128,2048]{1,0:T(8,128)(2,1)}, bf16[128,2048]{1,0:T(8,128)(2,1)}, u32[]{:S(2)}, u32[]{:S(2)}) collective-permute-start(bf16[128,2048]{1,0:T(8,128)(2,1)} %collective-permute-done.18.refs_4_), channel_id=1, source_target_pairs={{0,1},{1,0},{2,3},{3,2},{4,5},{5,4},{6,7},{7,6},{8,9},{9,8},{10,11... | collective-permute-start | bytes 1572872 | tf_op jit(solution)/shard_map/ppermute | solution.py:220
  124.3 15.9 %collective-permute-start.33 = (bf16[128,2048]{1,0:T(8,128)(2,1)}, bf16[128,2048]{1,0:T(8,128)(2,1)}, u32[]{:S(2)}, u32[]{:S(2)}) collective-permute-start(bf16[128,2048]{1,0:T(8,128)(2,1)} %collective-permute-done.20.refs_12_), channel_id=1, source_target_pairs={{0,1},{1,0},{2,3},{3,2},{4,5},{5,4},{6,7},{7,6},{8,9},{9,8},{10,11... | collective-permute-start | bytes 1572872 | tf_op jit(solution)/shard_map/ppermute | solution.py:220
  131.6 8.6 %collective-permute-start.31 = (bf16[128,2048]{1,0:T(8,128)(2,1)S(1)}, bf16[128,2048]{1,0:T(8,128)(2,1)}, u32[]{:S(2)}, u32[]{:S(2)}) collective-permute-start(bf16[128,2048]{1,0:T(8,128)(2,1)S(1)} %broadcast_select_fusion.10.refs_9_), channel_id=1, source_target_pairs={{0,1},{1,0},{2,3},{3,2},{4,5},{5,4},{6,7},{7,6},{8,9},{9,8},{10,11... | collective-permute-start | bytes 1572872 | tf_op jit(solution)/shard_map/ppermute | solution.py:220
  131.7 8.5 %collective-permute-start.29 = (bf16[128,2048]{1,0:T(8,128)(2,1)}, bf16[128,2048]{1,0:T(8,128)(2,1)}, u32[]{:S(2)}, u32[]{:S(2)}) collective-permute-start(bf16[128,2048]{1,0:T(8,128)(2,1)} %copy-done.25), channel_id=1, source_target_pairs={{0,1},{1,0},{2,3},{3,2},{4,5},{5,4},{6,7},{7,6},{8,9},{9,8},{10,11... | collective-permute-start | bytes 1572872 | tf_op jit(solution)/shard_map/ppermute | solution.py:220
  134.5 5.7 %collective-permute-start.34 = (bf16[128,2048]{1,0:T(8,128)(2,1)}, bf16[128,2048]{1,0:T(8,128)(2,1)}, u32[]{:S(2)}, u32[]{:S(2)}) collective-permute-start(bf16[128,2048]{1,0:T(8,128)(2,1)} %collective-permute-done.32.refs_13_), channel_id=1, source_target_pairs={{0,1},{1,0},{2,3},{3,2},{4,5},{5,4},{6,7},{7,6},{8,9},{9,8},{10,11... | collective-permute-start | bytes 1572872 | tf_op jit(solution)/shard_map/ppermute | solution.py:220
  134.5 5.7 %collective-permute-start.26 = (bf16[128,2048]{1,0:T(8,128)(2,1)}, bf16[128,2048]{1,0:T(8,128)(2,1)}, u32[]{:S(2)}, u32[]{:S(2)}) collective-permute-start(bf16[128,2048]{1,0:T(8,128)(2,1)} %bitcast.7.refs_0_), channel_id=1, source_target_pairs={{0,1},{1,0},{2,3},{3,2},{4,5},{5,4},{6,7},{7,6},{8,9},{9,8},{10,11... | collective-permute-start | bytes 1572872 | tf_op jit(solution)/shard_map/ppermute | solution.py:220
  135.0 24.7 %all-to-all-start.1 = ((bf16[8,16,16,128]{3,2,1,0:T(8,128)(2,1)}), bf16[8,16,16,128]{3,2,1,0:T(8,128)(2,1)S(1)}, u32[]{:S(2)}, u32[]{:S(2)}) async-start(bf16[8,16,16,128]{3,2,1,0:T(8,128)(2,1)} %get-tuple-element.117), calls=%async_computation.1 | async-start | bytes 1048576 | tf_op jit(solution)/shard_map/all_to_all | solution.py:266
  160.0 12.0 %collective-permute-start.36 = (bf16[128,2048]{1,0:T(8,128)(2,1)S(1)}, bf16[128,2048]{1,0:T(8,128)(2,1)S(1)}, u32[]{:S(2)}, u32[]{:S(2)}) collective-permute-start(bf16[128,2048]{1,0:T(8,128)(2,1)S(1)} %fusion.own_ref), channel_id=1, source_target_pairs={{0,1},{1,0},{2,3},{3,2},{4,5},{5,4},{6,7},{7,6},{8,9},{9,8},{10,11... | collective-permute-start | bytes 1572872 | tf_op jit(solution)/shard_map/ppermute | solution.py:220
  165.3 20.9 %all-to-all-start.2 = ((bf16[8,16,16,128]{3,2,1,0:T(8,128)(2,1)}), bf16[8,16,16,128]{3,2,1,0:T(8,128)(2,1)}, u32[]{:S(2)}, u32[]{:S(2)}) async-start(bf16[8,16,16,128]{3,2,1,0:T(8,128)(2,1)} %bitcast.27), calls=%async_computation.2 | async-start | bytes 1048576 | tf_op jit(solution)/shard_map/all_to_all | solution.py:265
  186.2 5.5 %collective-permute-start.38 = (bf16[128,2048]{1,0:T(8,128)(2,1)}, bf16[128,2048]{1,0:T(8,128)(2,1)S(1)}, u32[]{:S(2)}, u32[]{:S(2)}) collective-permute-start(bf16[128,2048]{1,0:T(8,128)(2,1)} %get-tuple-element.131), channel_id=1, source_target_pairs={{0,1},{1,0},{2,3},{3,2},{4,5},{5,4},{6,7},{7,6},{8,9},{9,8},{10,11... | collective-permute-start | bytes 1572872 | tf_op jit(solution)/shard_map/ppermute | solution.py:220
  190.3 14.0 %collective-permute-start.39 = (bf16[128,2048]{1,0:T(8,128)(2,1)S(1)}, bf16[128,2048]{1,0:T(8,128)(2,1)S(1)}, u32[]{:S(2)}, u32[]{:S(2)}) collective-permute-start(bf16[128,2048]{1,0:T(8,128)(2,1)S(1)} %get-tuple-element.202), channel_id=1, source_target_pairs={{0,2},{2,0},{4,6},{6,4},{8,10},{10,8},{12,14},{14,12},{1,3},{3,1},... | collective-permute-start | bytes 1572872 | tf_op jit(solution)/shard_map/ppermute | solution.py:216
  205.1 21.0 %all-to-all-start.3 = ((bf16[8,16,16,128]{3,2,1,0:T(8,128)(2,1)}), bf16[8,16,16,128]{3,2,1,0:T(8,128)(2,1)S(1)}, u32[]{:S(2)}, u32[]{:S(2)}) async-start(bf16[8,16,16,128]{3,2,1,0:T(8,128)(2,1)} %get-tuple-element.140), calls=%async_computation.3 | async-start | bytes 1048576 | tf_op jit(solution)/shard_map/all_to_all | solution.py:266
  209.3 41.4 %collective-permute-start.43 = (bf16[128,2048]{1,0:T(8,128)(2,1)}, bf16[128,2048]{1,0:T(8,128)(2,1)}, u32[]{:S(2)}, u32[]{:S(2)}) collective-permute-start(bf16[128,2048]{1,0:T(8,128)(2,1)} %get-tuple-element.152), channel_id=1, source_target_pairs={{0,2},{2,0},{4,6},{6,4},{8,10},{10,8},{12,14},{14,12},{1,3},{3,1},... | collective-permute-start | bytes 1572872 | tf_op jit(solution)/shard_map/ppermute | solution.py:216
  212.5 11.5 %collective-permute-start.45 = (bf16[136,512]{1,0:T(8,128)(2,1)S(1)}, bf16[136,512]{1,0:T(8,128)(2,1)S(1)}, u32[]{:S(2)}, u32[]{:S(2)}) collective-permute-start(bf16[136,512]{1,0:T(8,128)(2,1)S(1)} %select_convert_fusion), channel_id=1, source_target_pairs={{0,1},{1,0},{2,3},{3,2},{4,5},{5,4},{6,7},{7,6},{8,9},{9,8},{10,11... | collective-permute-start | bytes 417800 | tf_op jit(solution)/shard_map/ppermute | solution.py:220
  223.9 25.0 %collective-permute-start.48 = (bf16[128,2048]{1,0:T(8,128)(2,1)}, bf16[128,2048]{1,0:T(8,128)(2,1)}, u32[]{:S(2)}, u32[]{:S(2)}) collective-permute-start(bf16[128,2048]{1,0:T(8,128)(2,1)} %get-tuple-element.165), channel_id=1, source_target_pairs={{0,2},{2,0},{4,6},{6,4},{8,10},{10,8},{12,14},{14,12},{1,3},{3,1},... | collective-permute-start | bytes 1572872 | tf_op jit(solution)/shard_map/ppermute | solution.py:216
  223.9 25.0 %collective-permute-start.40 = (bf16[128,2048]{1,0:T(8,128)(2,1)}, bf16[128,2048]{1,0:T(8,128)(2,1)}, u32[]{:S(2)}, u32[]{:S(2)}) collective-permute-start(bf16[128,2048]{1,0:T(8,128)(2,1)} %get-tuple-element.147), channel_id=1, source_target_pairs={{0,1},{1,0},{2,3},{3,2},{4,5},{5,4},{6,7},{7,6},{8,9},{9,8},{10,11... | collective-permute-start | bytes 1572872 | tf_op jit(solution)/shard_map/ppermute | solution.py:220
  224.1 6.3 %collective-permute-start.46 = (bf16[136,512]{1,0:T(8,128)(2,1)S(1)}, bf16[136,512]{1,0:T(8,128)(2,1)S(1)}, u32[]{:S(2)}, u32[]{:S(2)}) collective-permute-start(bf16[136,512]{1,0:T(8,128)(2,1)S(1)} %convert_add_fusion.1), channel_id=1, source_target_pairs={{0,4},{2,6},{4,0},{6,2},{8,12},{10,14},{12,8},{14,10},{1,5},{3,7},... | collective-permute-start | bytes 417800 | tf_op jit(solution)/shard_map/ppermute | solution.py:216
  227.3 9.2 %collective-permute-start.47 = (bf16[128,2048]{1,0:T(8,128)(2,1)S(1)}, bf16[128,2048]{1,0:T(8,128)(2,1)S(1)}, u32[]{:S(2)}, u32[]{:S(2)}) collective-permute-start(bf16[128,2048]{1,0:T(8,128)(2,1)S(1)} %fusion.3.own_ref), channel_id=1, source_target_pairs={{0,1},{1,0},{2,3},{3,2},{4,5},{5,4},{6,7},{7,6},{8,9},{9,8},{10,11... | collective-permute-start | bytes 1572872 | tf_op jit(solution)/shard_map/ppermute | solution.py:220
  231.1 17.8 %collective-permute-start.44 = (bf16[128,2048]{1,0:T(8,128)(2,1)}, bf16[128,2048]{1,0:T(8,128)(2,1)}, u32[]{:S(2)}, u32[]{:S(2)}) collective-permute-start(bf16[128,2048]{1,0:T(8,128)(2,1)} %add_convert_fusion.11), channel_id=1, source_target_pairs={{0,4},{2,6},{12,8},{14,10},{1,5},{3,7},{13,9},{15,11},{16,20},{18,... | collective-permute-start | bytes 1572872 | tf_op jit(solution)/shard_map/ppermute | solution.py:216
  236.5 36.8 %collective-permute-start.41 = (bf16[128,2048]{1,0:T(8,128)(2,1)}, bf16[128,2048]{1,0:T(8,128)(2,1)}, u32[]{:S(2)}, u32[]{:S(2)}) collective-permute-start(bf16[128,2048]{1,0:T(8,128)(2,1)} %get-tuple-element.148), channel_id=1, source_target_pairs={{0,2},{2,0},{4,6},{6,4},{8,10},{10,8},{12,14},{14,12},{1,3},{3,1},... | collective-permute-start | bytes 1572872 | tf_op jit(solution)/shard_map/ppermute | solution.py:216
  250.1 5.9 %collective-permute-start.50 = (bf16[128,2048]{1,0:T(8,128)(2,1)}, bf16[128,2048]{1,0:T(8,128)(2,1)S(1)}, u32[]{:S(2)}, u32[]{:S(2)}) collective-permute-start(bf16[128,2048]{1,0:T(8,128)(2,1)} %get-tuple-element.168), channel_id=1, source_target_pairs={{0,1},{1,0},{2,3},{3,2},{4,5},{5,4},{6,7},{7,6},{8,9},{9,8},{10,11... | collective-permute-start | bytes 1572872 | tf_op jit(solution)/shard_map/ppermute | solution.py:220
  251.8 21.5 %collective-permute-start.52 = (bf16[128,2048]{1,0:T(8,128)(2,1)S(1)}, bf16[128,2048]{1,0:T(8,128)(2,1)S(1)}, u32[]{:S(2)}, u32[]{:S(2)}) collective-permute-start(bf16[128,2048]{1,0:T(8,128)(2,1)S(1)} %add_convert_fusion.10), channel_id=1, source_target_pairs={{0,4},{2,6},{12,8},{14,10},{1,5},{3,7},{13,9},{15,11},{16,20},{18,... | collective-permute-start | bytes 1572872 | tf_op jit(solution)/shard_map/ppermute | solution.py:216
  254.6 18.7 %collective-permute-start.54 = (bf16[128,2048]{1,0:T(8,128)(2,1)}, bf16[128,2048]{1,0:T(8,128)(2,1)}, u32[]{:S(2)}, u32[]{:S(2)}) collective-permute-start(bf16[128,2048]{1,0:T(8,128)(2,1)} %get-tuple-element.177), channel_id=1, source_target_pairs={{0,2},{2,0},{4,6},{6,4},{8,10},{10,8},{12,14},{14,12},{1,3},{3,1},... | collective-permute-start | bytes 1572872 | tf_op jit(solution)/shard_map/ppermute | solution.py:216
  257.1 22.6 %collective-permute-start.55 = (bf16[128,2048]{1,0:T(8,128)(2,1)}, bf16[128,2048]{1,0:T(8,128)(2,1)}, u32[]{:S(2)}, u32[]{:S(2)}) collective-permute-start(bf16[128,2048]{1,0:T(8,128)(2,1)} %get-tuple-element.178), channel_id=1, source_target_pairs={{0,2},{2,0},{4,6},{6,4},{8,10},{10,8},{12,14},{14,12},{1,3},{3,1},... | collective-permute-start | bytes 1572872 | tf_op jit(solution)/shard_map/ppermute | solution.py:216
  259.8 20.0 %collective-permute-start.51 = (bf16[128,2048]{1,0:T(8,128)(2,1)}, bf16[128,2048]{1,0:T(8,128)(2,1)}, u32[]{:S(2)}, u32[]{:S(2)}) collective-permute-start(bf16[128,2048]{1,0:T(8,128)(2,1)} %add_convert_fusion.9), channel_id=1, source_target_pairs={{4,8},{6,10},{8,4},{10,6},{5,9},{7,11},{9,5},{11,7},{20,24},{22,26... | collective-permute-start | bytes 1572872 | tf_op jit(solution)/shard_map/ppermute | solution.py:216
  279.7 11.2 %collective-permute-start.58 = (bf16[128,2048]{1,0:T(8,128)(2,1)}, bf16[128,2048]{1,0:T(8,128)(2,1)S(1)}, u32[]{:S(2)}, u32[]{:S(2)}) collective-permute-start(bf16[128,2048]{1,0:T(8,128)(2,1)} %get-tuple-element.183), channel_id=1, source_target_pairs={{0,1},{1,0},{2,3},{3,2},{4,5},{5,4},{6,7},{7,6},{8,9},{9,8},{10,11... | collective-permute-start | bytes 1572872 | tf_op jit(solution)/shard_map/ppermute | solution.py:220
  282.6 11.1 %collective-permute-start.53 = (bf16[136,512]{1,0:T(8,128)(2,1)S(1)}, bf16[136,512]{1,0:T(8,128)(2,1)S(1)}, u32[]{:S(2)}, u32[]{:S(2)}) collective-permute-start(bf16[136,512]{1,0:T(8,128)(2,1)S(1)} %convert_add_fusion), channel_id=1, source_target_pairs={{0,8},{2,10},{4,12},{6,14},{8,0},{10,2},{12,4},{14,6},{1,9},{3,11}... | collective-permute-start | bytes 417800 | tf_op jit(solution)/shard_map/ppermute | solution.py:216
  283.1 32.9 %collective-permute-start.66 = (bf16[128,2048]{1,0:T(8,128)(2,1)S(1)}, bf16[128,2048]{1,0:T(8,128)(2,1)S(1)}, u32[]{:S(2)}, u32[]{:S(2)}) collective-permute-start(bf16[128,2048]{1,0:T(8,128)(2,1)S(1)} %copy-done.26), channel_id=1, source_target_pairs={{0,2},{2,0},{4,6},{6,4},{8,10},{10,8},{12,14},{14,12},{1,3},{3,1},... | collective-permute-start | bytes 1572872 | tf_op jit(solution)/shard_map/ppermute | solution.py:216
  284.6 47.3 %collective-permute-start.64 = (bf16[128,2048]{1,0:T(8,128)(2,1)}, bf16[128,2048]{1,0:T(8,128)(2,1)}, u32[]{:S(2)}, u32[]{:S(2)}) collective-permute-start(bf16[128,2048]{1,0:T(8,128)(2,1)} %get-tuple-element.190), channel_id=1, source_target_pairs={{0,2},{2,0},{4,6},{6,4},{8,10},{10,8},{12,14},{14,12},{1,3},{3,1},... | collective-permute-start | bytes 1572872 | tf_op jit(solution)/shard_map/ppermute | solution.py:216
  286.4 16.8 %collective-permute-start.62 = (bf16[128,2048]{1,0:T(8,128)(2,1)S(1)}, bf16[128,2048]{1,0:T(8,128)(2,1)S(1)}, u32[]{:S(2)}, u32[]{:S(2)}) collective-permute-start(bf16[128,2048]{1,0:T(8,128)(2,1)S(1)} %add_convert_fusion.8), channel_id=1, source_target_pairs={{0,4},{2,6},{12,8},{14,10},{1,5},{3,7},{13,9},{15,11},{16,20},{18,... | collective-permute-start | bytes 1572872 | tf_op jit(solution)/shard_map/ppermute | solution.py:216
  292.3 20.3 %collective-permute-start.61 = (bf16[128,2048]{1,0:T(8,128)(2,1)S(1)}, bf16[128,2048]{1,0:T(8,128)(2,1)S(1)}, u32[]{:S(2)}, u32[]{:S(2)}) collective-permute-start(bf16[128,2048]{1,0:T(8,128)(2,1)S(1)} %add_convert_fusion.4), channel_id=1, source_target_pairs={{0,4},{2,6},{12,8},{14,10},{1,5},{3,7},{13,9},{15,11},{16,20},{18,... | collective-permute-start | bytes 1572872 | tf_op jit(solution)/shard_map/ppermute | solution.py:216
  293.8 29.1 %collective-permute-start.57 = (bf16[128,2048]{1,0:T(8,128)(2,1)S(1)}, bf16[128,2048]{1,0:T(8,128)(2,1)S(1)}, u32[]{:S(2)}, u32[]{:S(2)}) collective-permute-start(bf16[128,2048]{1,0:T(8,128)(2,1)S(1)} %add_convert_fusion.7), channel_id=1, source_target_pairs={{4,8},{6,10},{8,4},{10,6},{5,9},{7,11},{9,5},{11,7},{20,24},{22,26... | collective-permute-start | bytes 1572872 | tf_op jit(solution)/shard_map/ppermute | solution.py:216
  303.4 14.1 %collective-permute-start.63 = (bf16[128,2048]{1,0:T(8,128)(2,1)S(1)}, bf16[128,2048]{1,0:T(8,128)(2,1)S(1)}, u32[]{:S(2)}, u32[]{:S(2)}) collective-permute-start(bf16[128,2048]{1,0:T(8,128)(2,1)S(1)} %add_convert_fusion.3), channel_id=1, source_target_pairs={{4,8},{6,10},{8,4},{10,6},{5,9},{7,11},{9,5},{11,7},{20,24},{22,26... | collective-permute-start | bytes 1572872 | tf_op jit(solution)/shard_map/ppermute | solution.py:216
  312.6 15.3 %collective-permute-start.59 = (bf16[128,2048]{1,0:T(8,128)(2,1)S(1)}, bf16[128,2048]{1,0:T(8,128)(2,1)S(1)}, u32[]{:S(2)}, u32[]{:S(2)}) collective-permute-start(bf16[128,2048]{1,0:T(8,128)(2,1)S(1)} %add_convert_fusion.5), channel_id=1, source_target_pairs={{0,4},{2,6},{4,0},{6,2},{8,12},{10,14},{12,8},{14,10},{1,5},{3,7},... | collective-permute-start | bytes 1572872 | tf_op jit(solution)/shard_map/ppermute | solution.py:216
  317.5 14.4 %collective-permute-start.65 = (bf16[128,2048]{1,0:T(8,128)(2,1)}, bf16[128,2048]{1,0:T(8,128)(2,1)}, u32[]{:S(2)}, u32[]{:S(2)}) collective-permute-start(bf16[128,2048]{1,0:T(8,128)(2,1)} %add_convert_fusion.2), channel_id=1, source_target_pairs={{4,8},{6,10},{8,4},{10,6},{5,9},{7,11},{9,5},{11,7},{20,24},{22,26... | collective-permute-start | bytes 1572872 | tf_op jit(solution)/shard_map/ppermute | solution.py:216
  321.1 15.7 %collective-permute-start.67 = (bf16[128,2048]{1,0:T(8,128)(2,1)}, bf16[128,2048]{1,0:T(8,128)(2,1)}, u32[]{:S(2)}, u32[]{:S(2)}) collective-permute-start(bf16[128,2048]{1,0:T(8,128)(2,1)} %add_convert_fusion), channel_id=1, source_target_pairs={{0,4},{2,6},{4,0},{6,2},{8,12},{10,14},{12,8},{14,10},{1,5},{3,7},... | collective-permute-start | bytes 1572872 | tf_op jit(solution)/shard_map/ppermute | solution.py:216
  (51 other events, 555.8 us)

commit v2 on v1

--- a/solution.py
+++ b/solution.py
@@ -348,7 +348,7 @@
     distant3, close3 = exchange(part, 3)
     distant1, close1 = exchange(part, 1)
     g3, g1 = step(distant3, ACROSS), step(after(distant1, distant3), ACROSS)
-    out_b, d_rows_b, *terms_b = hold(interact(after(owned_b, distant3, distant1), cotangent[1], *small), g3)
+    out_b, d_rows_b, *terms_b = interact(after(owned_b, distant3, distant1), cotangent[1], *small)
     back_b = exchange_rows(d_rows_b, 8)
     kept = grid_sum_start((terms_a, terms_b))
     second = back(after(d_linear, d_rows_b), other, (2, 0), g3, back_b)
@@ -370,7 +370,7 @@
     sent = kept.astype(BF16)
     got = step(sent, CROSS)
     sum_a = close0.astype(F32) + h1.astype(F32)
-    second = back(after(d_next, distant3, distant1), other, (2, 0), g3, g1, h1, r2, k2)
+    second = back(after(d_next, distant3, distant1), other, (2, 0), h1, r2, k2)
     h3, h1 = step(after(close3, g3), ACROSS), step(after(close1, g3), ACROSS)
     distant2, close2 = exchange(second, 2)
     close0, distant0 = roles(second, 0, near)

time: 342 us -> 336 us (0.982)
  waiting for transfers between devices: 99.7 us -> 89.6 us
  starting transfers between devices: 88.4 us -> 94.6 us
    ppermute x39, waiting for transfers between devices: 94.7 us -> 84.7 us  [step(): return lax.ppermute(value, 'tensor', pairs)]
    ppermute x39, starting transfers between devices: 59.9 us -> 66.2 us  [step(): return lax.ppermute(value, 'tensor', pairs)]
    unnamed x91 -> x93, local copies, waits for them, and re-layouts: 12.8 us -> 8.83 us
  transfers between devices with their start and end apart: 73 -> 73, of which waited for: 22 -> 20; matrix products, arithmetic and copies ran while one was open for 13% -> 13% of each run, Pallas kernels for 28% -> 27%
where the time goes in v2:
time: 336 us; the launch traced here: 334 us
  Pallas kernels  95.5 us (28%)
  starting transfers between devices  94.6 us (28%)
  waiting for transfers between devices  89.6 us (27%)
  other arithmetic  38.8 us (12%)
  local copies, waits for them, and re-layouts  13.9 us (4%)
    ppermute x39, waiting for transfers between devices, step(): return lax.ppermute(value, 'tensor', pairs)  84.7 us
    ppermute x39, starting transfers between devices, step(): return lax.ppermute(value, 'tensor', pairs)  66.2 us
    pallas_call x4, Pallas kernels, back_part(): pl.pallas_call(functools.partial(back_kernel, count), grid_spec=pltpu.Pre...  43.2 us
    pallas_call x2, Pallas kernels, forward_rows(): pl.pallas_call(functools.partial(forward_kernel, count), grid_spec=pltpu....  38.8 us
    all_to_all x4, starting transfers between devices, exchange_rows(): lax.all_to_all(value, 'tensor', split_axis=0, concat_axis=0, tiled=True)  21.7 us
    pallas_call x2, Pallas kernels, interact_rows(): pl.pallas_call(interact_kernel, grid=(count // group,), in_specs=[rows, r...  13.5 us
    convert_element_type x10, other arithmetic, add(): return (a.astype(F32) + b.astype(F32)).astype(BF16)  10.8 us
    unnamed x93, local copies, waits for them, and re-layouts  8.83 us
  transfers between devices with their start and end apart: 73, of which 20 were waited for; matrix products, arithmetic and copies ran while one was open for 13% of the time, Pallas kernels for 27%

profile of v2, /device:TPU:0, one launch (start us, length us, event | category | flops | bytes accessed | tf_op | source)
XLA Modules:
  0.0 334.0 jit_solution(3361346764323188874)
XLA Ops:
  0.6 2.1 fusion.11
  3.4 3.0 collective-permute-start.1
  6.5 4.4 %collective-permute-start.2 = (bf16[128,2048]{1,0:T(8,128)(2,1)S(1)}, bf16[128,2048]{1,0:T(8,128)(2,1)S(1)}, u32[]{:S(2)}, u32[]{:S(2)}) collective-permute-start(bf16[128,2048]{1,0:T(8,128)(2,1)S(1)} %bitcast.59), channel_id=1, source_target_pairs={{0,4},{2,6},{4,0},{6,2},{8,12},{10,14},{12,8},{14,10},{1,5},{3,7},... | collective-permute-start | bytes 1572872 | tf_op jit(solution)/shard_map/ppermute | solution.py:216
  10.8 7.6 %collective-permute-done.1.refs_4_ = bf16[128,2048]{1,0:T(8,128)(2,1)S(1)} collective-permute-done((bf16[128,2048]{1,0:T(8,128)(2,1)S(1)}, bf16[128,2048]{1,0:T(8,128)(2,1)S(1)}, u32[]{:S(2)}, u32[]{:S(2)}) %collective-permute-start.1) | collective-permute-done | bytes 524320 | tf_op jit(solution)/shard_map/ppermute | solution.py:216
  18.4 3.8 %collective-permute-done.2.refs_8_ = bf16[128,2048]{1,0:T(8,128)(2,1)S(1)} collective-permute-done((bf16[128,2048]{1,0:T(8,128)(2,1)S(1)}, bf16[128,2048]{1,0:T(8,128)(2,1)S(1)}, u32[]{:S(2)}, u32[]{:S(2)}) %collective-permute-start.2) | collective-permute-done | bytes 524320 | tf_op jit(solution)/shard_map/ppermute | solution.py:216
  22.2 1.3 collective-permute-start.3
  24.1 1.5 collective-permute-start.7
  25.5 11.0 %collective-permute-done.3 = bf16[128,2048]{1,0:T(8,128)(2,1)S(1)} collective-permute-done((bf16[128,2048]{1,0:T(8,128)(2,1)S(1)}, bf16[128,2048]{1,0:T(8,128)(2,1)S(1)}, u32[]{:S(2)}, u32[]{:S(2)}) %collective-permute-start.3) | collective-permute-done | bytes 524320 | tf_op jit(solution)/shard_map/ppermute | solution.py:216
  37.3 1.3 collective-permute-start.11
  40.8 10.5 %collective-permute-done.11 = bf16[128,2048]{1,0:T(8,128)(2,1)S(1)} collective-permute-done((bf16[128,2048]{1,0:T(8,128)(2,1)}, bf16[128,2048]{1,0:T(8,128)(2,1)S(1)}, u32[]{:S(2)}, u32[]{:S(2)}) %collective-permute-start.11) | collective-permute-done | bytes 524320 | tf_op jit(solution)/shard_map/ppermute | solution.py:216
  53.0 2.7 collective-permute-start.17
  57.0 5.7 %collective-permute-done.14.refs_13_ = bf16[128,2048]{1,0:T(8,128)(2,1)} collective-permute-done((bf16[128,2048]{1,0:T(8,128)(2,1)S(1)}, bf16[128,2048]{1,0:T(8,128)(2,1)}, u32[]{:S(2)}, u32[]{:S(2)}) %collective-permute-start.14) | collective-permute-done | bytes 524320 | tf_op jit(solution)/shard_map/ppermute | solution.py:216
  66.1 1.5 collective-permute-start.21
  67.6 1.3 collective-permute-start.18
  68.9 1.3 collective-permute-start.22
  70.3 19.4 %forward_rows.2 = (f32[128,2048]{1,0:T(8,128)}, bf16[128,2048]{1,0:T(8,128)(2,1)}) custom-call(s32[5]{0:T(128)} %stack.49.plan_ref, bf16[128,2048]{1,0:T(8,128)(2,1)} %bitcast.61, bf16[128,2048]{1,0:T(8,128)(2,1)} %copy-done.7, bf16[128,2048]{1,0:T(8,128)(2,1)} %copy-done.22, bf16[128,2048]{1,0:T(8,128)(2,1)} %collective-permute-done.5.refs_3_, ...), custom_call_target="tpu_custom_call" | custom-call | flops 8589934592 | bytes 33554432 | tf_op jit(solution)/shard_map/forward_rows/pallas_call | solution.py:73
  90.9 1.4 collective-permute-start.25
  94.8 6.8 %all-to-all-start = ((bf16[8,16,16,128]{3,2,1,0:T(8,128)(2,1)}), bf16[8,16,16,128]{3,2,1,0:T(8,128)(2,1)}, u32[]{:S(2)}, u32[]{:S(2)}) async-start(bf16[8,16,16,128]{3,2,1,0:T(8,128)(2,1)} %bitcast.16), calls=%async_computation | async-start | bytes 1048576 | tf_op jit(solution)/shard_map/all_to_all | solution.py:265
  101.6 2.0 collective-permute-start.24
  104.1 8.0 %collective-permute-done.25 = bf16[128,2048]{1,0:T(8,128)(2,1)} collective-permute-done((bf16[128,2048]{1,0:T(8,128)(2,1)}, bf16[128,2048]{1,0:T(8,128)(2,1)}, u32[]{:S(2)}, u32[]{:S(2)}) %collective-permute-start.25) | collective-permute-done | bytes 524320 | tf_op jit(solution)/shard_map/ppermute | solution.py:216
  113.2 8.1 %collective-permute-done.24.refs_5_ = bf16[128,2048]{1,0:T(8,128)(2,1)S(1)} collective-permute-done((bf16[128,2048]{1,0:T(8,128)(2,1)S(1)}, bf16[128,2048]{1,0:T(8,128)(2,1)S(1)}, u32[]{:S(2)}, u32[]{:S(2)}) %collective-permute-start.24) | collective-permute-done | bytes 524320 | tf_op jit(solution)/shard_map/ppermute | solution.py:216
  122.1 1.3 slice_bitcast_fusion
  124.8 6.7 %interact_rows.2 = (bf16[16,128,128]{2,1,0:T(8,128)(2,1)}, bf16[8,16,16,128]{3,2,1,0:T(8,128)(2,1)}, f32[128,512]{1,0:T(8,128)}, f32[8,512]{1,0:T(8,128)}, f32[512,128]{1,0:T(8,128)}) custom-call(bf16[8,16,16,128]{3,2,1,0:T(8,128)(2,1)} %all-to-all-done.x_ref, bf16[16,128,128]{2,1,0:T(8,128)(2,1)} %bitcast.71, bf16[128,512]{1,0:T(8,128)(2,1)} %mix_ref.3, ...), custom_call_target="tpu_custom_call" | custom-call | flops 1744830464 | bytes 2097152 | tf_op jit(solution)/shard_map/interact_rows/pallas_call | solution.py:194
  132.1 2.4 collective-permute-done.32.refs_13_
  135.0 5.2 %all-to-all-start.1 = ((bf16[8,16,16,128]{3,2,1,0:T(8,128)(2,1)}), bf16[8,16,16,128]{3,2,1,0:T(8,128)(2,1)S(1)}, u32[]{:S(2)}, u32[]{:S(2)}) async-start(bf16[8,16,16,128]{3,2,1,0:T(8,128)(2,1)} %get-tuple-element.112), calls=%async_computation.1 | async-start | bytes 1048576 | tf_op jit(solution)/shard_map/all_to_all | solution.py:266
  140.2 19.4 %forward_rows.3 = (f32[128,2048]{1,0:T(8,128)}, bf16[128,2048]{1,0:T(8,128)(2,1)}) custom-call(s32[5]{0:T(128)} %stack.49.plan_ref, bf16[128,2048]{1,0:T(8,128)(2,1)} %bitcast.7.refs_0_, bf16[128,2048]{1,0:T(8,128)(2,1)} %copy-done.9, bf16[128,2048]{1,0:T(8,128)(2,1)} %collective-permute-done.26.refs_2_, bf16[128,2048]{1,0:T(8,128)(2,1)} %collective-permute-done.27.refs_3_, ...), custom_call_target="tpu_custom_call" | custom-call | flops 8589934592 | bytes 33554432 | tf_op jit(solution)/shard_map/forward_rows/pallas_call | solution.py:73
  160.5 1.5 collective-permute-done.35
  161.9 2.5 fusion.8
  165.3 6.0 %all-to-all-start.2 = ((bf16[8,16,16,128]{3,2,1,0:T(8,128)(2,1)}), bf16[8,16,16,128]{3,2,1,0:T(8,128)(2,1)}, u32[]{:S(2)}, u32[]{:S(2)}) async-start(bf16[8,16,16,128]{3,2,1,0:T(8,128)(2,1)} %bitcast.27), calls=%async_computation.2 | async-start | bytes 1048576 | tf_op jit(solution)/shard_map/all_to_all | solution.py:265
  172.7 10.8 %back_part.4 = (bf16[128,2048]{1,0:T(8,128)(2,1)}, bf16[128,2048]{1,0:T(8,128)(2,1)}, bf16[128,2048]{1,0:T(8,128)(2,1)}, bf16[128,2048]{1,0:T(8,128)(2,1)}) custom-call(s32[2]{0:T(128)} %pad_add_fusion.plan_ref, bf16[128,2048]{1,0:T(8,128)(2,1)} %copy-done.2, bf16[128,2048]{1,0:T(8,128)(2,1)} %copy-done.5, bf16[8192,2048]{1,0:T(8,128)(2,1)} %w_ref.7), custom_call_target="tpu_custom_call" | custom-call | flops 4294967296 | bytes 16777216 | tf_op jit(solution)/shard_map/back_part/pallas_call | solution.py:127
  183.5 2.7 all-to-all-done.2.x_ref
  188.3 2.1 broadcast_select_fusion.5
  191.5 6.8 %interact_rows.3 = (bf16[16,128,128]{2,1,0:T(8,128)(2,1)}, bf16[8,16,16,128]{3,2,1,0:T(8,128)(2,1)}, f32[128,512]{1,0:T(8,128)}, f32[8,512]{1,0:T(8,128)}, f32[512,128]{1,0:T(8,128)}) custom-call(bf16[8,16,16,128]{3,2,1,0:T(8,128)(2,1)} %all-to-all-done.2.x_ref, bf16[16,128,128]{2,1,0:T(8,128)(2,1)} %bitcast.70, bf16[128,512]{1,0:T(8,128)(2,1)} %mix_ref.3, ...), custom_call_target="tpu_custom_call" | custom-call | flops 1744830464 | bytes 2097152 | tf_op jit(solution)/shard_map/interact_rows/pallas_call | solution.py:194
  198.3 3.8 %all-to-all-start.3 = ((bf16[8,16,16,128]{3,2,1,0:T(8,128)(2,1)}), bf16[8,16,16,128]{3,2,1,0:T(8,128)(2,1)S(1)}, u32[]{:S(2)}, u32[]{:S(2)}) async-start(bf16[8,16,16,128]{3,2,1,0:T(8,128)(2,1)} %get-tuple-element.130), calls=%async_computation.3 | async-start | bytes 1048576 | tf_op jit(solution)/shard_map/all_to_all | solution.py:266
  202.0 2.0 collective-permute-start.39
  207.1 10.8 %back_part.5 = (bf16[128,2048]{1,0:T(8,128)(2,1)}, bf16[128,2048]{1,0:T(8,128)(2,1)}, bf16[128,2048]{1,0:T(8,128)(2,1)}, bf16[128,2048]{1,0:T(8,128)(2,1)}) custom-call(s32[2]{0:T(128)} %pad_add_fusion.1.plan_ref, bf16[128,2048]{1,0:T(8,128)(2,1)} %copy-done.2, bf16[128,2048]{1,0:T(8,128)(2,1)} %copy-done.5, bf16[8192,2048]{1,0:T(8,128)(2,1)} %w_ref.7), custom_call_target="tpu_custom_call" | custom-call | flops 4294967296 | bytes 16777216 | tf_op jit(solution)/shard_map/back_part/pallas_call | solution.py:127
  217.9 4.8 %collective-permute-done.39 = bf16[128,2048]{1,0:T(8,128)(2,1)S(1)} collective-permute-done((bf16[128,2048]{1,0:T(8,128)(2,1)}, bf16[128,2048]{1,0:T(8,128)(2,1)S(1)}, u32[]{:S(2)}, u32[]{:S(2)}) %collective-permute-start.39) | collective-permute-done | bytes 524320 | tf_op jit(solution)/shard_map/ppermute | solution.py:216
  223.9 1.6 collective-permute-start.46
  225.5 1.2 fusion.3.own_ref
  227.4 2.2 add_convert_fusion.11
  230.5 4.2 %collective-permute-start.44 = (bf16[128,2048]{1,0:T(8,128)(2,1)}, bf16[128,2048]{1,0:T(8,128)(2,1)}, u32[]{:S(2)}, u32[]{:S(2)}) collective-permute-start(bf16[128,2048]{1,0:T(8,128)(2,1)} %add_convert_fusion.11), channel_id=1, source_target_pairs={{0,4},{2,6},{12,8},{14,10},{1,5},{3,7},{13,9},{15,11},{16,20},{18,... | collective-permute-start | bytes 1572872 | tf_op jit(solution)/shard_map/ppermute | solution.py:216
  235.7 1.7 collective-permute-start.41
  237.4 10.8 %back_part.6 = (bf16[128,2048]{1,0:T(8,128)(2,1)}, bf16[128,2048]{1,0:T(8,128)(2,1)}, bf16[128,2048]{1,0:T(8,128)(2,1)}, bf16[128,2048]{1,0:T(8,128)(2,1)}) custom-call(s32[2]{0:T(128)} %pad_add_fusion.plan_ref, bf16[128,2048]{1,0:T(8,128)(2,1)} %copy-done.3, bf16[128,2048]{1,0:T(8,128)(2,1)} %copy-done.6, bf16[8192,2048]{1,0:T(8,128)(2,1)} %w_ref.7), custom_call_target="tpu_custom_call" | custom-call | flops 4294967296 | bytes 16777216 | tf_op jit(solution)/shard_map/back_part/pallas_call | solution.py:127
  251.1 1.3 collective-permute-start.52
  254.7 2.1 add_convert_fusion.9
  256.8 1.4 collective-permute-start.51
  258.2 1.6 copy_bitcast_fusion.1
  259.8 1.4 collective-permute-start.55
  261.2 10.8 %back_part.7 = (bf16[128,2048]{1,0:T(8,128)(2,1)}, bf16[128,2048]{1,0:T(8,128)(2,1)}, bf16[128,2048]{1,0:T(8,128)(2,1)}, bf16[128,2048]{1,0:T(8,128)(2,1)}) custom-call(s32[2]{0:T(128)} %pad_add_fusion.1.plan_ref, bf16[128,2048]{1,0:T(8,128)(2,1)} %copy-done.3, bf16[128,2048]{1,0:T(8,128)(2,1)} %copy-done.6, bf16[8192,2048]{1,0:T(8,128)(2,1)} %w_ref.7), custom_call_target="tpu_custom_call" | custom-call | flops 4294967296 | bytes 16777216 | tf_op jit(solution)/shard_map/back_part/pallas_call | solution.py:127
  272.8 2.3 maximum_bitcast_fusion
  275.8 2.0 collective-permute-start.53
  279.9 1.3 add_convert_fusion.8
  281.2 2.9 collective-permute-start.62
  284.2 5.7 %collective-permute-done.58 = bf16[128,2048]{1,0:T(8,128)(2,1)S(1)} collective-permute-done((bf16[128,2048]{1,0:T(8,128)(2,1)S(1)}, bf16[128,2048]{1,0:T(8,128)(2,1)S(1)}, u32[]{:S(2)}, u32[]{:S(2)}) %collective-permute-start.58) | collective-permute-done | bytes 524320 | tf_op jit(solution)/shard_map/ppermute | solution.py:216
  290.1 4.0 %collective-permute-start.61 = (bf16[128,2048]{1,0:T(8,128)(2,1)S(1)}, bf16[128,2048]{1,0:T(8,128)(2,1)S(1)}, u32[]{:S(2)}, u32[]{:S(2)}) collective-permute-start(bf16[128,2048]{1,0:T(8,128)(2,1)S(1)} %add_convert_fusion.4), channel_id=1, source_target_pairs={{0,4},{2,6},{12,8},{14,10},{1,5},{3,7},{13,9},{15,11},{16,20},{18,... | collective-permute-start | bytes 1572872 | tf_op jit(solution)/shard_map/ppermute | solution.py:216
  294.9 1.5 add_convert_fusion.5
  297.4 8.3 %collective-permute-done.61 = bf16[128,2048]{1,0:T(8,128)(2,1)S(1)} collective-permute-done((bf16[128,2048]{1,0:T(8,128)(2,1)S(1)}, bf16[128,2048]{1,0:T(8,128)(2,1)S(1)}, u32[]{:S(2)}, u32[]{:S(2)}) %collective-permute-start.61) | collective-permute-done | bytes 524320 | tf_op jit(solution)/shard_map/ppermute | solution.py:216
  305.6 2.5 collective-permute-start.59
  309.1 1.7 collective-permute-start.60
  310.8 1.4 collective-permute-start.65
  314.3 7.5 %collective-permute-start.67 = (bf16[128,2048]{1,0:T(8,128)(2,1)}, bf16[128,2048]{1,0:T(8,128)(2,1)}, u32[]{:S(2)}, u32[]{:S(2)}) collective-permute-start(bf16[128,2048]{1,0:T(8,128)(2,1)} %add_convert_fusion), channel_id=1, source_target_pairs={{0,4},{2,6},{4,0},{6,2},{8,12},{10,14},{12,8},{14,10},{1,5},{3,7},... | collective-permute-start | bytes 1572872 | tf_op jit(solution)/shard_map/ppermute | solution.py:216
  321.9 1.7 fusion.2
  325.7 5.3 %collective-permute-done.67 = bf16[128,2048]{1,0:T(8,128)(2,1)} collective-permute-done((bf16[128,2048]{1,0:T(8,128)(2,1)}, bf16[128,2048]{1,0:T(8,128)(2,1)}, u32[]{:S(2)}, u32[]{:S(2)}) %collective-permute-start.67) | collective-permute-done | bytes 524320 | tf_op jit(solution)/shard_map/ppermute | solution.py:216
  331.0 2.0 fusion.5
  (234 shorter events, 48.8 us)
Async XLA Ops:
  2.7 8.1 %collective-permute-start = (bf16[128,2048]{1,0:T(8,128)(2,1)S(1)}, bf16[128,2048]{1,0:T(8,128)(2,1)S(1)}, u32[]{:S(2)}, u32[]{:S(2)}) collective-permute-start(bf16[128,2048]{1,0:T(8,128)(2,1)S(1)} %bitcast.57), channel_id=1, source_target_pairs={{4,8},{6,10},{8,4},{10,6},{5,9},{7,11},{9,5},{11,7},{20,24},{22,26... | collective-permute-start | bytes 1572872 | tf_op jit(solution)/shard_map/ppermute | solution.py:216
  3.4 15.0 %collective-permute-start.1 = (bf16[128,2048]{1,0:T(8,128)(2,1)S(1)}, bf16[128,2048]{1,0:T(8,128)(2,1)S(1)}, u32[]{:S(2)}, u32[]{:S(2)}) collective-permute-start(bf16[128,2048]{1,0:T(8,128)(2,1)S(1)} %bitcast.58), channel_id=1, source_target_pairs={{0,2},{2,0},{4,6},{6,4},{8,10},{10,8},{12,14},{14,12},{1,3},{3,1},... | collective-permute-start | bytes 1572872 | tf_op jit(solution)/shard_map/ppermute | solution.py:216
  6.5 15.7 %collective-permute-start.2 = (bf16[128,2048]{1,0:T(8,128)(2,1)S(1)}, bf16[128,2048]{1,0:T(8,128)(2,1)S(1)}, u32[]{:S(2)}, u32[]{:S(2)}) collective-permute-start(bf16[128,2048]{1,0:T(8,128)(2,1)S(1)} %bitcast.59), channel_id=1, source_target_pairs={{0,4},{2,6},{4,0},{6,2},{8,12},{10,14},{12,8},{14,10},{1,5},{3,7},... | collective-permute-start | bytes 1572872 | tf_op jit(solution)/shard_map/ppermute | solution.py:216
  22.2 14.4 %collective-permute-start.3 = (bf16[128,2048]{1,0:T(8,128)(2,1)S(1)}, bf16[128,2048]{1,0:T(8,128)(2,1)S(1)}, u32[]{:S(2)}, u32[]{:S(2)}) collective-permute-start(bf16[128,2048]{1,0:T(8,128)(2,1)S(1)} %collective-permute-done), channel_id=1, source_target_pairs={{4,0},{6,2},{8,12},{10,14},{5,1},{7,3},{9,13},{11,15},{20,16},{22,... | collective-permute-start | bytes 1572872 | tf_op jit(solution)/shard_map/ppermute | solution.py:216
  23.5 13.1 %collective-permute-start.6 = (bf16[128,2048]{1,0:T(8,128)(2,1)S(1)}, bf16[128,2048]{1,0:T(8,128)(2,1)S(1)}, u32[]{:S(2)}, u32[]{:S(2)}) collective-permute-start(bf16[128,2048]{1,0:T(8,128)(2,1)S(1)} %collective-permute-done.2.refs_8_), channel_id=1, source_target_pairs={{0,2},{2,0},{4,6},{6,4},{8,10},{10,8},{12,14},{14,12},{1,3},{3,1},... | collective-permute-start | bytes 1572872 | tf_op jit(solution)/shard_map/ppermute | solution.py:216
  24.1 12.5 %collective-permute-start.7 = (bf16[128,2048]{1,0:T(8,128)(2,1)S(1)}, bf16[128,2048]{1,0:T(8,128)(2,1)}, u32[]{:S(2)}, u32[]{:S(2)}) collective-permute-start(bf16[128,2048]{1,0:T(8,128)(2,1)S(1)} %collective-permute-done.2.refs_8_), channel_id=1, source_target_pairs={{4,8},{6,10},{8,4},{10,6},{5,9},{7,11},{9,5},{11,7},{20,24},{22,26... | collective-permute-start | bytes 1572872 | tf_op jit(solution)/shard_map/ppermute | solution.py:216
  37.3 14.0 %collective-permute-start.11 = (bf16[128,2048]{1,0:T(8,128)(2,1)}, bf16[128,2048]{1,0:T(8,128)(2,1)S(1)}, u32[]{:S(2)}, u32[]{:S(2)}) collective-permute-start(bf16[128,2048]{1,0:T(8,128)(2,1)} %collective-permute-done.7), channel_id=1, source_target_pairs={{4,0},{6,2},{8,12},{10,14},{5,1},{7,3},{9,13},{11,15},{20,16},{22,... | collective-permute-start | bytes 1572872 | tf_op jit(solution)/shard_map/ppermute | solution.py:216
  39.8 12.2 %collective-permute-start.8 = (bf16[128,2048]{1,0:T(8,128)(2,1)S(1)}, bf16[128,2048]{1,0:T(8,128)(2,1)}, u32[]{:S(2)}, u32[]{:S(2)}) collective-permute-start(bf16[128,2048]{1,0:T(8,128)(2,1)S(1)} %broadcast_select_fusion.13.refs_1_), channel_id=1, source_target_pairs={{0,2},{2,0},{4,6},{6,4},{8,10},{10,8},{12,14},{14,12},{1,3},{3,1},... | collective-permute-start | bytes 1572872 | tf_op jit(solution)/shard_map/ppermute | solution.py:216
  40.3 15.4 %collective-permute-start.4 = (bf16[128,2048]{1,0:T(8,128)(2,1)S(1)}, bf16[128,2048]{1,0:T(8,128)(2,1)S(1)}, u32[]{:S(2)}, u32[]{:S(2)}) collective-permute-start(bf16[128,2048]{1,0:T(8,128)(2,1)S(1)} %bitcast.60), channel_id=1, source_target_pairs={{0,1},{1,0},{2,3},{3,2},{4,5},{5,4},{6,7},{7,6},{8,9},{9,8},{10,11... | collective-permute-start | bytes 1572872 | tf_op jit(solution)/shard_map/ppermute | solution.py:220
  40.3 16.1 %collective-permute-start.9 = (bf16[128,2048]{1,0:T(8,128)(2,1)S(1)}, bf16[128,2048]{1,0:T(8,128)(2,1)S(1)}, u32[]{:S(2)}, u32[]{:S(2)}) collective-permute-start(bf16[128,2048]{1,0:T(8,128)(2,1)S(1)} %collective-permute-done.1.refs_4_), channel_id=1, source_target_pairs={{0,1},{1,0},{2,3},{3,2},{4,5},{5,4},{6,7},{7,6},{8,9},{9,8},{10,11... | collective-permute-start | bytes 1572872 | tf_op jit(solution)/shard_map/ppermute | solution.py:220
  40.8 15.7 %collective-permute-start.12 = (bf16[128,2048]{1,0:T(8,128)(2,1)S(1)}, bf16[128,2048]{1,0:T(8,128)(2,1)S(1)}, u32[]{:S(2)}, u32[]{:S(2)}) collective-permute-start(bf16[128,2048]{1,0:T(8,128)(2,1)S(1)} %collective-permute-done.2.refs_8_), channel_id=1, source_target_pairs={{0,1},{1,0},{2,3},{3,2},{4,5},{5,4},{6,7},{7,6},{8,9},{9,8},{10,11... | collective-permute-start | bytes 1572872 | tf_op jit(solution)/shard_map/ppermute | solution.py:220
  51.9 10.8 %collective-permute-start.14 = (bf16[128,2048]{1,0:T(8,128)(2,1)S(1)}, bf16[128,2048]{1,0:T(8,128)(2,1)}, u32[]{:S(2)}, u32[]{:S(2)}) collective-permute-start(bf16[128,2048]{1,0:T(8,128)(2,1)S(1)} %broadcast_select_fusion.12.refs_9_), channel_id=1, source_target_pairs={{0,2},{2,0},{4,6},{6,4},{8,10},{10,8},{12,14},{14,12},{1,3},{3,1},... | collective-permute-start | bytes 1572872 | tf_op jit(solution)/shard_map/ppermute | solution.py:216
  53.0 10.5 %collective-permute-start.17 = (bf16[128,2048]{1,0:T(8,128)(2,1)}, bf16[128,2048]{1,0:T(8,128)(2,1)}, u32[]{:S(2)}, u32[]{:S(2)}) collective-permute-start(bf16[128,2048]{1,0:T(8,128)(2,1)} %bitcast.7.refs_0_), channel_id=1, source_target_pairs={{0,4},{2,6},{4,0},{6,2},{8,12},{10,14},{12,8},{14,10},{1,5},{3,7},... | collective-permute-start | bytes 1572872 | tf_op jit(solution)/shard_map/ppermute | solution.py:216
  55.7 7.8 %collective-permute-start.19 = (bf16[128,2048]{1,0:T(8,128)(2,1)}, bf16[128,2048]{1,0:T(8,128)(2,1)S(1)}, u32[]{:S(2)}, u32[]{:S(2)}) collective-permute-start(bf16[128,2048]{1,0:T(8,128)(2,1)} %bitcast.7.refs_0_), channel_id=1, source_target_pairs={{4,8},{6,10},{8,4},{10,6},{5,9},{7,11},{9,5},{11,7},{20,24},{22,26... | collective-permute-start | bytes 1572872 | tf_op jit(solution)/shard_map/ppermute | solution.py:216
  56.4 9.0 %collective-permute-start.5 = (bf16[128,2048]{1,0:T(8,128)(2,1)S(1)}, bf16[128,2048]{1,0:T(8,128)(2,1)}, u32[]{:S(2)}, u32[]{:S(2)}) collective-permute-start(bf16[128,2048]{1,0:T(8,128)(2,1)S(1)} %broadcast_select_fusion.13.refs_1_), channel_id=1, source_target_pairs={{0,1},{1,0},{2,3},{3,2},{4,5},{5,4},{6,7},{7,6},{8,9},{9,8},{10,11... | collective-permute-start | bytes 1572872 | tf_op jit(solution)/shard_map/ppermute | solution.py:220
  56.5 9.6 %collective-permute-start.15 = (bf16[128,2048]{1,0:T(8,128)(2,1)S(1)}, bf16[128,2048]{1,0:T(8,128)(2,1)}, u32[]{:S(2)}, u32[]{:S(2)}) collective-permute-start(bf16[128,2048]{1,0:T(8,128)(2,1)S(1)} %collective-permute-done.6.refs_12_), channel_id=1, source_target_pairs={{0,1},{1,0},{2,3},{3,2},{4,5},{5,4},{6,7},{7,6},{8,9},{9,8},{10,11... | collective-permute-start | bytes 1572872 | tf_op jit(solution)/shard_map/ppermute | solution.py:220
  63.5 5.4 %collective-permute-start.13 = (bf16[128,2048]{1,0:T(8,128)(2,1)S(1)}, bf16[128,2048]{1,0:T(8,128)(2,1)}, u32[]{:S(2)}, u32[]{:S(2)}) collective-permute-start(bf16[128,2048]{1,0:T(8,128)(2,1)S(1)} %broadcast_select_fusion.12.refs_9_), channel_id=1, source_target_pairs={{0,1},{1,0},{2,3},{3,2},{4,5},{5,4},{6,7},{7,6},{8,9},{9,8},{10,11... | collective-permute-start | bytes 1572872 | tf_op jit(solution)/shard_map/ppermute | solution.py:220
  64.3 5.9 %collective-permute-start.16 = (bf16[128,2048]{1,0:T(8,128)(2,1)}, bf16[128,2048]{1,0:T(8,128)(2,1)}, u32[]{:S(2)}, u32[]{:S(2)}) collective-permute-start(bf16[128,2048]{1,0:T(8,128)(2,1)} %collective-permute-done.14.refs_13_), channel_id=1, source_target_pairs={{0,1},{1,0},{2,3},{3,2},{4,5},{5,4},{6,7},{7,6},{8,9},{9,8},{10,11... | collective-permute-start | bytes 1572872 | tf_op jit(solution)/shard_map/ppermute | solution.py:220
  65.4 25.4 %collective-permute-start.20 = (bf16[128,2048]{1,0:T(8,128)(2,1)}, bf16[128,2048]{1,0:T(8,128)(2,1)}, u32[]{:S(2)}, u32[]{:S(2)}) collective-permute-start(bf16[128,2048]{1,0:T(8,128)(2,1)} %collective-permute-done.17.refs_8_), channel_id=1, source_target_pairs={{0,2},{2,0},{4,6},{6,4},{8,10},{10,8},{12,14},{14,12},{1,3},{3,1},... | collective-permute-start | bytes 1572872 | tf_op jit(solution)/shard_map/ppermute | solution.py:216
  66.1 24.7 %collective-permute-start.21 = (bf16[128,2048]{1,0:T(8,128)(2,1)}, bf16[128,2048]{1,0:T(8,128)(2,1)}, u32[]{:S(2)}, u32[]{:S(2)}) collective-permute-start(bf16[128,2048]{1,0:T(8,128)(2,1)} %collective-permute-done.17.refs_8_), channel_id=1, source_target_pairs={{4,8},{6,10},{8,4},{10,6},{5,9},{7,11},{9,5},{11,7},{20,24},{22,26... | collective-permute-start | bytes 1572872 | tf_op jit(solution)/shard_map/ppermute | solution.py:216
  67.6 23.2 %collective-permute-start.18 = (bf16[128,2048]{1,0:T(8,128)(2,1)}, bf16[128,2048]{1,0:T(8,128)(2,1)}, u32[]{:S(2)}, u32[]{:S(2)}) collective-permute-start(bf16[128,2048]{1,0:T(8,128)(2,1)} %bitcast.7.refs_0_), channel_id=1, source_target_pairs={{0,2},{2,0},{4,6},{6,4},{8,10},{10,8},{12,14},{14,12},{1,3},{3,1},... | collective-permute-start | bytes 1572872 | tf_op jit(solution)/shard_map/ppermute | solution.py:216
  68.9 21.9 %collective-permute-start.22 = (bf16[128,2048]{1,0:T(8,128)(2,1)}, bf16[128,2048]{1,0:T(8,128)(2,1)}, u32[]{:S(2)}, u32[]{:S(2)}) collective-permute-start(bf16[128,2048]{1,0:T(8,128)(2,1)} %copy-done.34), channel_id=1, source_target_pairs={{4,0},{6,2},{8,12},{10,14},{5,1},{7,3},{9,13},{11,15},{20,16},{22,... | collective-permute-start | bytes 1572872 | tf_op jit(solution)/shard_map/ppermute | solution.py:216
  90.9 21.2 %collective-permute-start.25 = (bf16[128,2048]{1,0:T(8,128)(2,1)}, bf16[128,2048]{1,0:T(8,128)(2,1)}, u32[]{:S(2)}, u32[]{:S(2)}) collective-permute-start(bf16[128,2048]{1,0:T(8,128)(2,1)} %collective-permute-done.21), channel_id=1, source_target_pairs={{4,0},{6,2},{8,12},{10,14},{5,1},{7,3},{9,13},{11,15},{20,16},{22,... | collective-permute-start | bytes 1572872 | tf_op jit(solution)/shard_map/ppermute | solution.py:216
  94.8 30.0 %all-to-all-start = ((bf16[8,16,16,128]{3,2,1,0:T(8,128)(2,1)}), bf16[8,16,16,128]{3,2,1,0:T(8,128)(2,1)}, u32[]{:S(2)}, u32[]{:S(2)}) async-start(bf16[8,16,16,128]{3,2,1,0:T(8,128)(2,1)} %bitcast.16), calls=%async_computation | async-start | bytes 1048576 | tf_op jit(solution)/shard_map/all_to_all | solution.py:265
  101.6 19.7 %collective-permute-start.24 = (bf16[128,2048]{1,0:T(8,128)(2,1)S(1)}, bf16[128,2048]{1,0:T(8,128)(2,1)S(1)}, u32[]{:S(2)}, u32[]{:S(2)}) collective-permute-start(bf16[128,2048]{1,0:T(8,128)(2,1)S(1)} %broadcast_select_fusion.11.refs_1_), channel_id=1, source_target_pairs={{0,2},{2,0},{4,6},{6,4},{8,10},{10,8},{12,14},{14,12},{1,3},{3,1},... | collective-permute-start | bytes 1572872 | tf_op jit(solution)/shard_map/ppermute | solution.py:216
  103.6 27.9 %collective-permute-start.30 = (bf16[128,2048]{1,0:T(8,128)(2,1)}, bf16[128,2048]{1,0:T(8,128)(2,1)}, u32[]{:S(2)}, u32[]{:S(2)}) collective-permute-start(bf16[128,2048]{1,0:T(8,128)(2,1)} %collective-permute-done.17.refs_8_), channel_id=1, source_target_pairs={{0,1},{1,0},{2,3},{3,2},{4,5},{5,4},{6,7},{7,6},{8,9},{9,8},{10,11... | collective-permute-start | bytes 1572872 | tf_op jit(solution)/shard_map/ppermute | solution.py:220
  103.6 28.0 %collective-permute-start.27 = (bf16[128,2048]{1,0:T(8,128)(2,1)S(1)}, bf16[128,2048]{1,0:T(8,128)(2,1)}, u32[]{:S(2)}, u32[]{:S(2)}) collective-permute-start(bf16[128,2048]{1,0:T(8,128)(2,1)S(1)} %broadcast_select_fusion.11.refs_1_), channel_id=1, source_target_pairs={{0,1},{1,0},{2,3},{3,2},{4,5},{5,4},{6,7},{7,6},{8,9},{9,8},{10,11... | collective-permute-start | bytes 1572872 | tf_op jit(solution)/shard_map/ppermute | solution.py:220
  121.3 13.2 %collective-permute-start.32 = (bf16[128,2048]{1,0:T(8,128)(2,1)S(1)}, bf16[128,2048]{1,0:T(8,128)(2,1)}, u32[]{:S(2)}, u32[]{:S(2)}) collective-permute-start(bf16[128,2048]{1,0:T(8,128)(2,1)S(1)} %broadcast_select_fusion.10.refs_9_), channel_id=1, source_target_pairs={{0,2},{2,0},{4,6},{6,4},{8,10},{10,8},{12,14},{14,12},{1,3},{3,1},... | collective-permute-start | bytes 1572872 | tf_op jit(solution)/shard_map/ppermute | solution.py:216
  122.1 12.4 %collective-permute-start.28 = (bf16[128,2048]{1,0:T(8,128)(2,1)}, bf16[128,2048]{1,0:T(8,128)(2,1)}, u32[]{:S(2)}, u32[]{:S(2)}) collective-permute-start(bf16[128,2048]{1,0:T(8,128)(2,1)} %collective-permute-done.18.refs_4_), channel_id=1, source_target_pairs={{0,1},{1,0},{2,3},{3,2},{4,5},{5,4},{6,7},{7,6},{8,9},{9,8},{10,11... | collective-permute-start | bytes 1572872 | tf_op jit(solution)/shard_map/ppermute | solution.py:220
  124.3 15.9 %collective-permute-start.33 = (bf16[128,2048]{1,0:T(8,128)(2,1)}, bf16[128,2048]{1,0:T(8,128)(2,1)}, u32[]{:S(2)}, u32[]{:S(2)}) collective-permute-start(bf16[128,2048]{1,0:T(8,128)(2,1)} %collective-permute-done.20.refs_12_), channel_id=1, source_target_pairs={{0,1},{1,0},{2,3},{3,2},{4,5},{5,4},{6,7},{7,6},{8,9},{9,8},{10,11... | collective-permute-start | bytes 1572872 | tf_op jit(solution)/shard_map/ppermute | solution.py:220
  131.5 8.6 %collective-permute-start.31 = (bf16[128,2048]{1,0:T(8,128)(2,1)S(1)}, bf16[128,2048]{1,0:T(8,128)(2,1)}, u32[]{:S(2)}, u32[]{:S(2)}) collective-permute-start(bf16[128,2048]{1,0:T(8,128)(2,1)S(1)} %broadcast_select_fusion.10.refs_9_), channel_id=1, source_target_pairs={{0,1},{1,0},{2,3},{3,2},{4,5},{5,4},{6,7},{7,6},{8,9},{9,8},{10,11... | collective-permute-start | bytes 1572872 | tf_op jit(solution)/shard_map/ppermute | solution.py:220
  131.6 8.5 %collective-permute-start.29 = (bf16[128,2048]{1,0:T(8,128)(2,1)}, bf16[128,2048]{1,0:T(8,128)(2,1)}, u32[]{:S(2)}, u32[]{:S(2)}) collective-permute-start(bf16[128,2048]{1,0:T(8,128)(2,1)} %copy-done.25), channel_id=1, source_target_pairs={{0,1},{1,0},{2,3},{3,2},{4,5},{5,4},{6,7},{7,6},{8,9},{9,8},{10,11... | collective-permute-start | bytes 1572872 | tf_op jit(solution)/shard_map/ppermute | solution.py:220
  134.5 5.7 %collective-permute-start.34 = (bf16[128,2048]{1,0:T(8,128)(2,1)}, bf16[128,2048]{1,0:T(8,128)(2,1)}, u32[]{:S(2)}, u32[]{:S(2)}) collective-permute-start(bf16[128,2048]{1,0:T(8,128)(2,1)} %collective-permute-done.32.refs_13_), channel_id=1, source_target_pairs={{0,1},{1,0},{2,3},{3,2},{4,5},{5,4},{6,7},{7,6},{8,9},{9,8},{10,11... | collective-permute-start | bytes 1572872 | tf_op jit(solution)/shard_map/ppermute | solution.py:220
  134.5 5.7 %collective-permute-start.26 = (bf16[128,2048]{1,0:T(8,128)(2,1)}, bf16[128,2048]{1,0:T(8,128)(2,1)}, u32[]{:S(2)}, u32[]{:S(2)}) collective-permute-start(bf16[128,2048]{1,0:T(8,128)(2,1)} %bitcast.7.refs_0_), channel_id=1, source_target_pairs={{0,1},{1,0},{2,3},{3,2},{4,5},{5,4},{6,7},{7,6},{8,9},{9,8},{10,11... | collective-permute-start | bytes 1572872 | tf_op jit(solution)/shard_map/ppermute | solution.py:220
  135.0 24.7 %all-to-all-start.1 = ((bf16[8,16,16,128]{3,2,1,0:T(8,128)(2,1)}), bf16[8,16,16,128]{3,2,1,0:T(8,128)(2,1)S(1)}, u32[]{:S(2)}, u32[]{:S(2)}) async-start(bf16[8,16,16,128]{3,2,1,0:T(8,128)(2,1)} %get-tuple-element.112), calls=%async_computation.1 | async-start | bytes 1048576 | tf_op jit(solution)/shard_map/all_to_all | solution.py:266
  159.9 12.0 %collective-permute-start.36 = (bf16[128,2048]{1,0:T(8,128)(2,1)S(1)}, bf16[128,2048]{1,0:T(8,128)(2,1)S(1)}, u32[]{:S(2)}, u32[]{:S(2)}) collective-permute-start(bf16[128,2048]{1,0:T(8,128)(2,1)S(1)} %fusion.own_ref), channel_id=1, source_target_pairs={{0,1},{1,0},{2,3},{3,2},{4,5},{5,4},{6,7},{7,6},{8,9},{9,8},{10,11... | collective-permute-start | bytes 1572872 | tf_op jit(solution)/shard_map/ppermute | solution.py:220
  165.3 20.9 %all-to-all-start.2 = ((bf16[8,16,16,128]{3,2,1,0:T(8,128)(2,1)}), bf16[8,16,16,128]{3,2,1,0:T(8,128)(2,1)}, u32[]{:S(2)}, u32[]{:S(2)}) async-start(bf16[8,16,16,128]{3,2,1,0:T(8,128)(2,1)} %bitcast.27), calls=%async_computation.2 | async-start | bytes 1048576 | tf_op jit(solution)/shard_map/all_to_all | solution.py:265
  198.3 27.3 %all-to-all-start.3 = ((bf16[8,16,16,128]{3,2,1,0:T(8,128)(2,1)}), bf16[8,16,16,128]{3,2,1,0:T(8,128)(2,1)S(1)}, u32[]{:S(2)}, u32[]{:S(2)}) async-start(bf16[8,16,16,128]{3,2,1,0:T(8,128)(2,1)} %get-tuple-element.130), calls=%async_computation.3 | async-start | bytes 1048576 | tf_op jit(solution)/shard_map/all_to_all | solution.py:266
  202.0 20.6 %collective-permute-start.39 = (bf16[128,2048]{1,0:T(8,128)(2,1)}, bf16[128,2048]{1,0:T(8,128)(2,1)S(1)}, u32[]{:S(2)}, u32[]{:S(2)}) collective-permute-start(bf16[128,2048]{1,0:T(8,128)(2,1)} %get-tuple-element.192), channel_id=1, source_target_pairs={{0,2},{2,0},{4,6},{6,4},{8,10},{10,8},{12,14},{14,12},{1,3},{3,1},... | collective-permute-start | bytes 1572872 | tf_op jit(solution)/shard_map/ppermute | solution.py:216
  206.9 15.8 %collective-permute-start.45 = (bf16[136,512]{1,0:T(8,128)(2,1)S(1)}, bf16[136,512]{1,0:T(8,128)(2,1)}, u32[]{:S(2)}, u32[]{:S(2)}) collective-permute-start(bf16[136,512]{1,0:T(8,128)(2,1)S(1)} %select_convert_fusion), channel_id=1, source_target_pairs={{0,1},{1,0},{2,3},{3,2},{4,5},{5,4},{6,7},{7,6},{8,9},{9,8},{10,11... | collective-permute-start | bytes 417800 | tf_op jit(solution)/shard_map/ppermute | solution.py:220
  207.0 43.0 %collective-permute-start.43 = (bf16[128,2048]{1,0:T(8,128)(2,1)}, bf16[128,2048]{1,0:T(8,128)(2,1)}, u32[]{:S(2)}, u32[]{:S(2)}) collective-permute-start(bf16[128,2048]{1,0:T(8,128)(2,1)} %get-tuple-element.142), channel_id=1, source_target_pairs={{0,2},{2,0},{4,6},{6,4},{8,10},{10,8},{12,14},{14,12},{1,3},{3,1},... | collective-permute-start | bytes 1572872 | tf_op jit(solution)/shard_map/ppermute | solution.py:216
  223.8 24.4 %collective-permute-start.48 = (bf16[128,2048]{1,0:T(8,128)(2,1)}, bf16[128,2048]{1,0:T(8,128)(2,1)}, u32[]{:S(2)}, u32[]{:S(2)}) collective-permute-start(bf16[128,2048]{1,0:T(8,128)(2,1)} %get-tuple-element.155), channel_id=1, source_target_pairs={{0,2},{2,0},{4,6},{6,4},{8,10},{10,8},{12,14},{14,12},{1,3},{3,1},... | collective-permute-start | bytes 1572872 | tf_op jit(solution)/shard_map/ppermute | solution.py:216
  223.9 6.0 %collective-permute-start.46 = (bf16[136,512]{1,0:T(8,128)(2,1)S(1)}, bf16[136,512]{1,0:T(8,128)(2,1)S(1)}, u32[]{:S(2)}, u32[]{:S(2)}) collective-permute-start(bf16[136,512]{1,0:T(8,128)(2,1)S(1)} %convert_add_fusion.1), channel_id=1, source_target_pairs={{0,4},{2,6},{4,0},{6,2},{8,12},{10,14},{12,8},{14,10},{1,5},{3,7},... | collective-permute-start | bytes 417800 | tf_op jit(solution)/shard_map/ppermute | solution.py:216
  225.5 22.8 %collective-permute-start.40 = (bf16[128,2048]{1,0:T(8,128)(2,1)}, bf16[128,2048]{1,0:T(8,128)(2,1)}, u32[]{:S(2)}, u32[]{:S(2)}) collective-permute-start(bf16[128,2048]{1,0:T(8,128)(2,1)} %get-tuple-element.137), channel_id=1, source_target_pairs={{0,1},{1,0},{2,3},{3,2},{4,5},{5,4},{6,7},{7,6},{8,9},{9,8},{10,11... | collective-permute-start | bytes 1572872 | tf_op jit(solution)/shard_map/ppermute | solution.py:220
  226.8 8.9 %collective-permute-start.47 = (bf16[128,2048]{1,0:T(8,128)(2,1)S(1)}, bf16[128,2048]{1,0:T(8,128)(2,1)S(1)}, u32[]{:S(2)}, u32[]{:S(2)}) collective-permute-start(bf16[128,2048]{1,0:T(8,128)(2,1)S(1)} %fusion.3.own_ref), channel_id=1, source_target_pairs={{0,1},{1,0},{2,3},{3,2},{4,5},{5,4},{6,7},{7,6},{8,9},{9,8},{10,11... | collective-permute-start | bytes 1572872 | tf_op jit(solution)/shard_map/ppermute | solution.py:220
  230.5 17.7 %collective-permute-start.44 = (bf16[128,2048]{1,0:T(8,128)(2,1)}, bf16[128,2048]{1,0:T(8,128)(2,1)}, u32[]{:S(2)}, u32[]{:S(2)}) collective-permute-start(bf16[128,2048]{1,0:T(8,128)(2,1)} %add_convert_fusion.11), channel_id=1, source_target_pairs={{0,4},{2,6},{12,8},{14,10},{1,5},{3,7},{13,9},{15,11},{16,20},{18,... | collective-permute-start | bytes 1572872 | tf_op jit(solution)/shard_map/ppermute | solution.py:216
  235.7 36.3 %collective-permute-start.41 = (bf16[128,2048]{1,0:T(8,128)(2,1)}, bf16[128,2048]{1,0:T(8,128)(2,1)}, u32[]{:S(2)}, u32[]{:S(2)}) collective-permute-start(bf16[128,2048]{1,0:T(8,128)(2,1)} %get-tuple-element.138), channel_id=1, source_target_pairs={{0,2},{2,0},{4,6},{6,4},{8,10},{10,8},{12,14},{14,12},{1,3},{3,1},... | collective-permute-start | bytes 1572872 | tf_op jit(solution)/shard_map/ppermute | solution.py:216
  251.1 20.9 %collective-permute-start.52 = (bf16[128,2048]{1,0:T(8,128)(2,1)S(1)}, bf16[128,2048]{1,0:T(8,128)(2,1)S(1)}, u32[]{:S(2)}, u32[]{:S(2)}) collective-permute-start(bf16[128,2048]{1,0:T(8,128)(2,1)S(1)} %add_convert_fusion.10), channel_id=1, source_target_pairs={{0,4},{2,6},{12,8},{14,10},{1,5},{3,7},{13,9},{15,11},{16,20},{18,... | collective-permute-start | bytes 1572872 | tf_op jit(solution)/shard_map/ppermute | solution.py:216
  256.8 15.2 %collective-permute-start.51 = (bf16[128,2048]{1,0:T(8,128)(2,1)}, bf16[128,2048]{1,0:T(8,128)(2,1)}, u32[]{:S(2)}, u32[]{:S(2)}) collective-permute-start(bf16[128,2048]{1,0:T(8,128)(2,1)} %add_convert_fusion.9), channel_id=1, source_target_pairs={{4,8},{6,10},{8,4},{10,6},{5,9},{7,11},{9,5},{11,7},{20,24},{22,26... | collective-permute-start | bytes 1572872 | tf_op jit(solution)/shard_map/ppermute | solution.py:216
  259.8 18.0 %collective-permute-start.55 = (bf16[128,2048]{1,0:T(8,128)(2,1)}, bf16[128,2048]{1,0:T(8,128)(2,1)}, u32[]{:S(2)}, u32[]{:S(2)}) collective-permute-start(bf16[128,2048]{1,0:T(8,128)(2,1)} %get-tuple-element.169), channel_id=1, source_target_pairs={{0,2},{2,0},{4,6},{6,4},{8,10},{10,8},{12,14},{14,12},{1,3},{3,1},... | collective-permute-start | bytes 1572872 | tf_op jit(solution)/shard_map/ppermute | solution.py:216
  272.0 6.7 %collective-permute-start.54 = (bf16[128,2048]{1,0:T(8,128)(2,1)}, bf16[128,2048]{1,0:T(8,128)(2,1)S(1)}, u32[]{:S(2)}, u32[]{:S(2)}) collective-permute-start(bf16[128,2048]{1,0:T(8,128)(2,1)} %get-tuple-element.167), channel_id=1, source_target_pairs={{0,1},{1,0},{2,3},{3,2},{4,5},{5,4},{6,7},{7,6},{8,9},{9,8},{10,11... | collective-permute-start | bytes 1572872 | tf_op jit(solution)/shard_map/ppermute | solution.py:220
  272.1 9.1 %collective-permute-start.57 = (bf16[128,2048]{1,0:T(8,128)(2,1)}, bf16[128,2048]{1,0:T(8,128)(2,1)S(1)}, u32[]{:S(2)}, u32[]{:S(2)}) collective-permute-start(bf16[128,2048]{1,0:T(8,128)(2,1)} %get-tuple-element.172), channel_id=1, source_target_pairs={{0,1},{1,0},{2,3},{3,2},{4,5},{5,4},{6,7},{7,6},{8,9},{9,8},{10,11... | collective-permute-start | bytes 1572872 | tf_op jit(solution)/shard_map/ppermute | solution.py:220
  275.1 14.8 %collective-permute-start.58 = (bf16[128,2048]{1,0:T(8,128)(2,1)S(1)}, bf16[128,2048]{1,0:T(8,128)(2,1)S(1)}, u32[]{:S(2)}, u32[]{:S(2)}) collective-permute-start(bf16[128,2048]{1,0:T(8,128)(2,1)S(1)} %copy-done.29), channel_id=1, source_target_pairs={{0,2},{2,0},{4,6},{6,4},{8,10},{10,8},{12,14},{14,12},{1,3},{3,1},... | collective-permute-start | bytes 1572872 | tf_op jit(solution)/shard_map/ppermute | solution.py:216
  275.8 18.3 %collective-permute-start.53 = (bf16[136,512]{1,0:T(8,128)(2,1)S(1)}, bf16[136,512]{1,0:T(8,128)(2,1)S(1)}, u32[]{:S(2)}, u32[]{:S(2)}) collective-permute-start(bf16[136,512]{1,0:T(8,128)(2,1)S(1)} %convert_add_fusion), channel_id=1, source_target_pairs={{0,8},{2,10},{4,12},{6,14},{8,0},{10,2},{12,4},{14,6},{1,9},{3,11}... | collective-permute-start | bytes 417800 | tf_op jit(solution)/shard_map/ppermute | solution.py:216
  277.8 31.3 %collective-permute-start.66 = (bf16[128,2048]{1,0:T(8,128)(2,1)S(1)}, bf16[128,2048]{1,0:T(8,128)(2,1)S(1)}, u32[]{:S(2)}, u32[]{:S(2)}) collective-permute-start(bf16[128,2048]{1,0:T(8,128)(2,1)S(1)} %copy-done.26), channel_id=1, source_target_pairs={{0,2},{2,0},{4,6},{6,4},{8,10},{10,8},{12,14},{14,12},{1,3},{3,1},... | collective-permute-start | bytes 1572872 | tf_op jit(solution)/shard_map/ppermute | solution.py:216
  278.7 47.0 %collective-permute-start.64 = (bf16[128,2048]{1,0:T(8,128)(2,1)}, bf16[128,2048]{1,0:T(8,128)(2,1)}, u32[]{:S(2)}, u32[]{:S(2)}) collective-permute-start(bf16[128,2048]{1,0:T(8,128)(2,1)} %get-tuple-element.180), channel_id=1, source_target_pairs={{0,2},{2,0},{4,6},{6,4},{8,10},{10,8},{12,14},{14,12},{1,3},{3,1},... | collective-permute-start | bytes 1572872 | tf_op jit(solution)/shard_map/ppermute | solution.py:216
  281.2 15.3 %collective-permute-start.62 = (bf16[128,2048]{1,0:T(8,128)(2,1)S(1)}, bf16[128,2048]{1,0:T(8,128)(2,1)S(1)}, u32[]{:S(2)}, u32[]{:S(2)}) collective-permute-start(bf16[128,2048]{1,0:T(8,128)(2,1)S(1)} %add_convert_fusion.8), channel_id=1, source_target_pairs={{0,4},{2,6},{12,8},{14,10},{1,5},{3,7},{13,9},{15,11},{16,20},{18,... | collective-permute-start | bytes 1572872 | tf_op jit(solution)/shard_map/ppermute | solution.py:216
  290.1 15.6 %collective-permute-start.61 = (bf16[128,2048]{1,0:T(8,128)(2,1)S(1)}, bf16[128,2048]{1,0:T(8,128)(2,1)S(1)}, u32[]{:S(2)}, u32[]{:S(2)}) collective-permute-start(bf16[128,2048]{1,0:T(8,128)(2,1)S(1)} %add_convert_fusion.4), channel_id=1, source_target_pairs={{0,4},{2,6},{12,8},{14,10},{1,5},{3,7},{13,9},{15,11},{16,20},{18,... | collective-permute-start | bytes 1572872 | tf_op jit(solution)/shard_map/ppermute | solution.py:216
  294.2 27.5 %collective-permute-start.56 = (bf16[128,2048]{1,0:T(8,128)(2,1)S(1)}, bf16[128,2048]{1,0:T(8,128)(2,1)S(1)}, u32[]{:S(2)}, u32[]{:S(2)}) collective-permute-start(bf16[128,2048]{1,0:T(8,128)(2,1)S(1)} %add_convert_fusion.7), channel_id=1, source_target_pairs={{4,8},{6,10},{8,4},{10,6},{5,9},{7,11},{9,5},{11,7},{20,24},{22,26... | collective-permute-start | bytes 1572872 | tf_op jit(solution)/shard_map/ppermute | solution.py:216
  296.6 14.1 %collective-permute-start.63 = (bf16[128,2048]{1,0:T(8,128)(2,1)S(1)}, bf16[128,2048]{1,0:T(8,128)(2,1)S(1)}, u32[]{:S(2)}, u32[]{:S(2)}) collective-permute-start(bf16[128,2048]{1,0:T(8,128)(2,1)S(1)} %add_convert_fusion.3), channel_id=1, source_target_pairs={{4,8},{6,10},{8,4},{10,6},{5,9},{7,11},{9,5},{11,7},{20,24},{22,26... | collective-permute-start | bytes 1572872 | tf_op jit(solution)/shard_map/ppermute | solution.py:216
  305.6 16.1 %collective-permute-start.59 = (bf16[128,2048]{1,0:T(8,128)(2,1)S(1)}, bf16[128,2048]{1,0:T(8,128)(2,1)S(1)}, u32[]{:S(2)}, u32[]{:S(2)}) collective-permute-start(bf16[128,2048]{1,0:T(8,128)(2,1)S(1)} %add_convert_fusion.5), channel_id=1, source_target_pairs={{0,4},{2,6},{4,0},{6,2},{8,12},{10,14},{12,8},{14,10},{1,5},{3,7},... | collective-permute-start | bytes 1572872 | tf_op jit(solution)/shard_map/ppermute | solution.py:216
  309.1 5.2 %collective-permute-start.60 = (bf16[136,512]{1,0:T(8,128)(2,1)S(1)}, bf16[136,512]{1,0:T(8,128)(2,1)S(1)}, u32[]{:S(2)}, u32[]{:S(2)}) collective-permute-start(bf16[136,512]{1,0:T(8,128)(2,1)S(1)} %add_convert_fusion.13), channel_id=1, source_target_pairs={{0,2},{2,0},{4,6},{6,4},{8,10},{10,8},{12,14},{14,12},{1,3},{3,1},... | collective-permute-start | bytes 417800 | tf_op jit(solution)/shard_map/ppermute | solution.py:216
  310.8 14.9 %collective-permute-start.65 = (bf16[128,2048]{1,0:T(8,128)(2,1)}, bf16[128,2048]{1,0:T(8,128)(2,1)}, u32[]{:S(2)}, u32[]{:S(2)}) collective-permute-start(bf16[128,2048]{1,0:T(8,128)(2,1)} %add_convert_fusion.2), channel_id=1, source_target_pairs={{4,8},{6,10},{8,4},{10,6},{5,9},{7,11},{9,5},{11,7},{20,24},{22,26... | collective-permute-start | bytes 1572872 | tf_op jit(solution)/shard_map/ppermute | solution.py:216
  314.3 16.8 %collective-permute-start.67 = (bf16[128,2048]{1,0:T(8,128)(2,1)}, bf16[128,2048]{1,0:T(8,128)(2,1)}, u32[]{:S(2)}, u32[]{:S(2)}) collective-permute-start(bf16[128,2048]{1,0:T(8,128)(2,1)} %add_convert_fusion), channel_id=1, source_target_pairs={{0,4},{2,6},{4,0},{6,2},{8,12},{10,14},{12,8},{14,10},{1,5},{3,7},... | collective-permute-start | bytes 1572872 | tf_op jit(solution)/shard_map/ppermute | solution.py:216
  (53 other events, 567.7 us)
